TPU v7x, 256 devices: a whole 4x4x8 slice. The times are simulated.
256 devices in a mesh: seq: 32 (over x, y, core), head: 8 (over z).
Axes of the slice: x: 4, y: 4, z: 8, core: 2. Of those that a mesh axis runs over, the one named last changes fastest.
Arguments:
- queries: bfloat16 [32, 8192, 128], P('head', 'seq'), may hold values from -0.5390625 to 0.5390625
- keys: bfloat16 [32, 8192, 128], P('head', 'seq'), may hold values from -0.5390625 to 0.5390625
- values: bfloat16 [32, 8192, 128], P('head', 'seq'), may hold values from -15 to 15
- log_decay: float32 [32, 8192], P('head', 'seq'), may hold values from -1 to 0, as said below
- level_weight: float32 [32, 21, 8192], P('head', None, 'seq'), may hold values from 0.2 to 2
- gate_input: bfloat16 [32, 8192, 128], P('head', 'seq'), may hold values from -6 to 6
- norm_gain: float32 [32, 128], P('head'), may hold values from 0.5 to 1.5
- out_grad: bfloat16 [32, 8192, 128], P('head', 'seq'), may hold values from -15 to 15
Outputs:
- layer_out: bfloat16 [32, 8192, 128], P('head', 'seq')
- grad_queries: bfloat16 [32, 8192, 128], P('head', 'seq')
- grad_keys: bfloat16 [32, 8192, 128], P('head', 'seq')
- grad_values: bfloat16 [32, 8192, 128], P('head', 'seq')
- grad_levels: float32 [32, 21, 8192], P('head', None, 'seq')
- grad_gate: bfloat16 [32, 8192, 128], P('head', 'seq')
- grad_gain: float32 [32, 128], P('head')
Inputs may be any that keep to these rules, and one draw needn't show every extreme that they name: `log_decay`: negative logarithms of decays.
All inputs are finite; a program needn't handle non-finite values.
Results may differ from a plain program's by a relative error of at most 0.0051.
Values sent between devices are 32-bit elements; how exact they have to be, the bound alone decides.
No kernel may reach another device: no remote copies, remote signals or barrier semaphores. Data moves between devices by JAX's collectives and lax.ppermute only.
A program may use at most 64 MiB of HBM per device.

v0:
```python
import jax
import jax.numpy as jnp
from jax import lax
from jax.experimental import pallas as pl
from jax.experimental.pallas import tpu as pltpu
from jax.sharding import PartitionSpec as P


HEADS = 32
HEAD_DIM = 128
TOTAL = HEADS * HEAD_DIM
EPSILON = 1e-05
HIGH = lax.Precision.HIGHEST
F32 = jnp.float32
BF16 = jnp.bfloat16

LOCAL = 4
WIDTH = 256
DEPTH = 8
INTER = 5
LEVELS = 21
ROWS = HEAD_DIM + 8


def place():
    me = lax.axis_index("seq")
    return me // 8, lax.rem(me // 2, 4), lax.rem(me, 2)


def ring(function):
    pairs = []
    for x in range(4):
        for y in range(4):
            for core in range(2):
                to = function(x, y, core)
                if to is not None:
                    pairs.append(((x * 4 + y) * 2 + core, (to[0] * 4 + to[1]) * 2 + to[2]))
    return pairs


SWAP = ring(lambda x, y, core: (x, y, 1 - core))
UP = ring(lambda x, y, core: (x, y, 1) if core == 0 else None)
DOWN = ring(lambda x, y, core: (x, y, 0) if core == 1 else None)


def along_y(step):
    return ring(lambda x, y, core: (x, (y + step) % 4, core))


def along_x(step):
    return ring(lambda x, y, core: ((x + step) % 4, y, core))


def send(array, pairs):
    return lax.ppermute(array, "seq", pairs)


def split(array):
    high = array.astype(BF16)
    return high, (array - high.astype(F32)).astype(BF16)


def flag(condition):
    return condition.astype(F32)


def dot(a, b, dims, precision=None):
    return lax.dot_general(a, b, (dims, ((), ())), precision=precision, preferred_element_type=F32)


NN = ((1,), (0,))
NT = ((1,), (1,))
TN = ((0,), (0,))


def iotas(shape):
    return lax.broadcasted_iota(jnp.int32, shape, 0), lax.broadcasted_iota(jnp.int32, shape, 1)


def state_kernel(decay_ref, k_hbm, v_hbm, keep_ref, send_ref, run_ref, k_ref, v_ref, rows_ref, sems):
    copies = [
        pltpu.make_async_copy(source, to, sems.at[i])
        for i, (source, to) in enumerate(((v_hbm, v_ref), (k_hbm, k_ref)))
    ]
    for copy in copies:
        copy.start()
    core = place()[2]
    early, late = iotas((WIDTH, WIDTH))
    upper = (early <= late).astype(F32).astype(BF16)
    decay = decay_ref[...]
    first = decay.astype(BF16).astype(F32)
    second = (decay - first).astype(BF16).astype(F32)
    rows_ref[0:4, :] = first
    rows_ref[4:8, :] = second
    rows_ref[8:12, :] = decay - first - second
    rows_ref[12:16, :] = jnp.zeros((4, WIDTH), F32)
    parts = dot(rows_ref[...].astype(BF16), upper, NN)
    running = parts[0:4, :] + parts[4:8, :] + parts[8:12, :]
    run_ref[...] = running
    rows_ref[0:4, :] = jnp.exp(running[:, WIDTH - 1 :] - running)
    tails = jnp.transpose(rows_ref[...])
    for copy in copies:
        copy.wait()
    for head in range(LOCAL):
        weighted = v_ref[head].astype(F32) * tails[:, head : head + 1]
        both = dot(k_ref[head], jnp.concatenate(split(weighted), axis=1), TN)
        state = both[:, 0:HEAD_DIM] + both[:, HEAD_DIM:]
        total = jnp.broadcast_to(running[head : head + 1, WIDTH - 1 :], (4, HEAD_DIM))
        totals = jnp.broadcast_to(running[:, WIDTH - 1 :], (4, HEAD_DIM))

        def put(ref):
            ref[head % 2, 0:HEAD_DIM, :] = state
            ref[head % 2, HEAD_DIM : HEAD_DIM + 4, :] = total
            ref[head % 2, HEAD_DIM + 4 :, :] = totals

        pl.when(core == head // 2)(lambda: put(keep_ref))
        pl.when(core != head // 2)(lambda: put(send_ref))


def pair_kernel(keep_ref, first_ref, chip_ref):
    late = place()[2] == 1
    before = jnp.where(late, first_ref[...], keep_ref[...])
    after = jnp.where(late, keep_ref[...], first_ref[...])
    carry = jnp.exp(after[:, HEAD_DIM : HEAD_DIM + 1, :])
    chip_ref[:, 0:HEAD_DIM, :] = carry * before[:, 0:HEAD_DIM, :] + after[:, 0:HEAD_DIM, :]
    chip_ref[:, HEAD_DIM:, :] = before[:, HEAD_DIM:, :] + after[:, HEAD_DIM:, :]


def intra_kernel(
    q_ref, k_ref, v_ref, level_ref, run_ref, inner_ref, mix_ref, weight_ref, scored_ref, cols_ref, rows_ref
):
    running = run_ref[...]
    grown = jnp.exp(running)
    rows_ref[...] = jnp.zeros_like(rows_ref)
    for level in range(INTER):
        rows_ref[4 * level : 4 * level + 4, :] = level_ref[DEPTH + 1 + level] * grown
    rows_ref[20:24, :] = running
    rows_ref[24:28, :] = jnp.exp(running[:, WIDTH - 1 :] - running)
    cols_ref[...] = jnp.transpose(rows_ref[...])
    early, late = iotas((WIDTH, WIDTH))
    crossed = jnp.bitwise_xor(early, late)
    causal = early <= late
    for head in range(LOCAL):
        spread = run_ref[head : head + 1, :] - cols_ref[:, 20 + head : 21 + head]
        decay = jnp.where(causal, jnp.exp(jnp.where(causal, spread, 0.0)), 0.0)
        chosen = jnp.broadcast_to(level_ref[0, head : head + 1, :], (WIDTH, WIDTH))
        for level in range(1, DEPTH + 1):
            chosen = jnp.where(crossed >= 2 ** (level - 1), level_ref[level, head : head + 1, :], chosen)
        scored = dot(k_ref[head], q_ref[head], NT)
        weight = decay * chosen
        mixing = (scored * weight).astype(BF16)
        weight_ref[head] = weight
        scored_ref[head] = scored * decay
        mix_ref[head] = mixing
        inner_ref[head] = dot(mixing, v_ref[head], TN)


def order(position, step):
    return lax.rem(position + 4 - step, 4)


def y_kernel(own_ref, one_ref, two_ref, three_ref, next_ref, bucket_ref, info_ref):
    y = place()[1]
    refs = (own_ref, one_ref, two_ref, three_ref)
    where = [order(y, step) for step in range(4)]
    totals = [ref[:, HEAD_DIM : HEAD_DIM + 1, :] for ref in refs]
    by_y = [sum(flag(where[i] == j) * totals[i] for i in range(4)) for j in range(4)]
    carry = jnp.exp(by_y[1])
    whole = jnp.zeros((2, HEAD_DIM, HEAD_DIM), F32)
    pair = jnp.zeros((2, HEAD_DIM, HEAD_DIM), F32)
    for i in range(4):
        state = refs[i][:, 0:HEAD_DIM, :]
        later = sum(flag(j > where[i]) * by_y[j] for j in range(1, 4))
        whole = whole + jnp.exp(later) * state
        if i:
            part = flag(y >= 2) * (flag(where[i] == 1) + flag(where[i] == 0) * carry)
            pair = pair + part * state
    below = sum(flag(j < y) * by_y[j] for j in range(3))
    next_ref[:, 0:HEAD_DIM, :] = whole
    next_ref[:, HEAD_DIM:, :] = jnp.broadcast_to(by_y[0] + by_y[1] + by_y[2] + by_y[3], (2, 8, HEAD_DIM))
    bucket_ref[0, :, 0:HEAD_DIM, :] = flag(lax.rem(y, 2) == 1) * one_ref[:, 0:HEAD_DIM, :]
    bucket_ref[0, :, HEAD_DIM:, :] = jnp.zeros((2, 8, HEAD_DIM), F32)
    bucket_ref[1, :, 0:HEAD_DIM, :] = pair
    bucket_ref[1, :, HEAD_DIM:, :] = jnp.broadcast_to(flag(y == 3) * by_y[2], (2, 8, HEAD_DIM))
    for j in range(4):
        info_ref[:, j : j + 1, :] = by_y[j]
    info_ref[:, 4:8, :] = jnp.broadcast_to(below, (2, 4, HEAD_DIM))


def x_kernel(own_ref, one_ref, two_ref, three_ref, info_ref, bucket_ref, wide_ref):
    x = place()[0]
    refs = (own_ref, one_ref, two_ref, three_ref)
    where = [order(x, step) for step in range(4)]
    totals = [ref[:, HEAD_DIM : HEAD_DIM + 1, :] for ref in refs]
    by_x = [sum(flag(where[i] == j) * totals[i] for i in range(4)) for j in range(4)]
    carry = jnp.exp(by_x[1])
    pair = jnp.zeros((2, HEAD_DIM, HEAD_DIM), F32)
    for i in range(1, 4):
        part = flag(x >= 2) * (flag(where[i] == 1) + flag(where[i] == 0) * carry)
        pair = pair + part * refs[i][:, 0:HEAD_DIM, :]
    below = info_ref[:, 4:5, :]
    bucket_ref[0, :, 0:HEAD_DIM, :] = flag(lax.rem(x, 2) == 1) * one_ref[:, 0:HEAD_DIM, :]
    bucket_ref[0, :, HEAD_DIM:, :] = jnp.broadcast_to(below, (2, 8, HEAD_DIM))
    bucket_ref[1, :, 0:HEAD_DIM, :] = pair
    bucket_ref[1, :, HEAD_DIM:, :] = jnp.broadcast_to(below + flag(x == 3) * by_x[2], (2, 8, HEAD_DIM))
    for j in range(4):
        wide_ref[:, j : j + 1, :] = by_x[j]
        wide_ref[:, 4 + j : 5 + j, :] = by_x[j]


def mixed_kernel(
    q_ref, inner_ref, gate_ref, grad_ref, gain_ref, cols_ref, near_ref, near_other_ref, far_ref, far_other_ref,
    first_ref, rest_ref, mixed_ref, pay_ref, bucket_ref, finer_ref, shift_ref,
):
    core = place()[2]
    odd = flag(core == 1)
    ones = jnp.ones((8, HEAD_DIM), BF16)
    squares = jnp.zeros((8, WIDTH), F32)
    crosses = jnp.zeros((8, WIDTH), F32)
    for head in range(LOCAL):
        slot, mine = head % 2, core == head // 2
        zeroth = rest_ref[slot, 0:HEAD_DIM, :] if head < 2 else first_ref[slot, 0:HEAD_DIM, :]
        earlier = odd * first_ref[0, HEAD_DIM + 4 + head : HEAD_DIM + 5 + head, :]
        parts = [split(odd * zeroth)]
        shift_ref[head] = jnp.ones((8, HEAD_DIM), F32)
        for level in range(1, INTER):
            own, other = (near_ref, near_other_ref) if level < 3 else (far_ref, far_other_ref)
            at = (level - 1) % 2
            chosen = jnp.where(mine, own[at, slot], other[at, slot])
            shift = jnp.exp(earlier + chosen[HEAD_DIM : HEAD_DIM + 1, :])
            shift_ref[head, level : level + 1, :] = shift
            parts.append(split(chosen[0:HEAD_DIM, :] * shift))
        bucket, finer = (jnp.concatenate([part[i] for part in parts], axis=1) for i in range(2))
        bucket_ref[head] = bucket
        finer_ref[head] = finer
        through = dot(q_ref[head], bucket, NN) + dot(q_ref[head], finer, NN)
        mixed = inner_ref[head]
        for level in range(INTER):
            at = 4 * level + head
            mixed = mixed + cols_ref[:, at : at + 1] * through[:, HEAD_DIM * level : HEAD_DIM * (level + 1)]
        mixed_ref[head] = mixed
        gate = gate_ref[head].astype(F32)
        gated = mixed * (gate * jax.nn.sigmoid(gate))
        scaled = grad_ref[head].astype(F32) * gain_ref[head : head + 1, :]
        squares = squares + dot(ones, (gated * gated).astype(BF16), NT)
        crosses = crosses + dot(ones, (gated * scaled).astype(BF16), NT)
    for peer in range(8):
        for half in range(2):
            piece = slice(HEAD_DIM * half, HEAD_DIM * (half + 1))
            pay_ref[peer, half : half + 1, :] = squares[0:1, piece]
            pay_ref[peer, 2 + half : 3 + half, :] = crosses[0:1, piece]


def gate_kernel(
    q_ref, mixed_ref, gate_ref, grad_ref, gain_ref, cols_ref, shift_ref, sums_ref,
    g_ref, scale_ref, keep_ref, send_ref,
):
    x, _, core = place()
    ones = jnp.ones((8, HEAD_DIM), F32)
    wide = [dot(sums_ref[:, i, :], ones, TN, HIGH) for i in range(4)]
    squares = jnp.concatenate(wide[0:2], axis=0)
    crosses = jnp.concatenate(wide[2:4], axis=0)
    inverse = lax.rsqrt(squares * (1.0 / TOTAL) + EPSILON)
    pull = inverse * inverse * inverse * crosses * (1.0 / TOTAL)
    scale_ref[0] = inverse
    scale_ref[1] = pull
    gains = []
    for ref in (keep_ref, send_ref):
        ref[:, :, HEAD_DIM:, :] = jnp.zeros((2, 2, 8, HEAD_DIM), F32)
    for head in range(LOCAL):
        gate = gate_ref[head].astype(F32)
        act = gate * jax.nn.sigmoid(gate)
        gated = mixed_ref[head] * act
        grad = grad_ref[head].astype(F32)
        gains.append(jnp.sum(grad * (gated * inverse), axis=0, keepdims=True))
        grad_gated = inverse * (grad * gain_ref[head : head + 1, :]) - gated * pull
        g = (grad_gated * act).astype(BF16)
        g_ref[head] = g
        far = reached(q_ref[head], g.astype(F32), cols_ref, shift_ref, head, (3, 4))
        near = jnp.where(lax.rem(x, 2) == 1, far[0], far[1])

        def put(ref):
            ref[0, head % 2, 0:HEAD_DIM, :] = near
            ref[1, head % 2, 0:HEAD_DIM, :] = far[1]

        pl.when(core == head // 2)(lambda: put(keep_ref))
        pl.when(core != head // 2)(lambda: put(send_ref))
    for head in range(LOCAL):
        for ref in (keep_ref, send_ref):
            ref[0, 0, HEAD_DIM + head : HEAD_DIM + head + 1, :] = gains[head]
            ref[1, 0, HEAD_DIM + head : HEAD_DIM + head + 1, :] = gains[head]


def reached(q, g, cols_ref, shift_ref, head, levels):
    parts = [split(cols_ref[:, 4 * level + head : 4 * level + head + 1] * g) for level in levels]
    both = dot(q, jnp.concatenate([part for pair in parts for part in pair], axis=1), TN)
    found = []
    for i, level in enumerate(levels):
        at = 2 * HEAD_DIM * i
        grad = both[:, at : at + HEAD_DIM] + both[:, at + HEAD_DIM : at + 2 * HEAD_DIM]
        found.append(grad * shift_ref[head, level : level + 1, :])
    return found


def meet_kernel(keep_ref, other_ref, near_ref, far_ref):
    near_ref[...] = keep_ref[0] + other_ref[0]
    far_ref[...] = keep_ref[1] + other_ref[1]


def close_kernel(
    q_ref, g_ref, mixed_ref, gate_ref, grad_ref, gain_ref, cols_ref, shift_ref, scale_ref,
    out_ref, grad_gate_ref, keep_ref, send_ref, zeroth_ref,
):
    core = place()[2]
    inverse, pull = scale_ref[0], scale_ref[1]
    for ref in (keep_ref, send_ref):
        ref[:, :, HEAD_DIM:, :] = jnp.zeros((2, 2, 8, HEAD_DIM), F32)
    for head in range(LOCAL):
        near = reached(q_ref[head], g_ref[head].astype(F32), cols_ref, shift_ref, head, (0, 1, 2))
        zeroth_ref[head] = near[0]

        def put(ref):
            ref[0, head % 2, 0:HEAD_DIM, :] = near[1]
            ref[1, head % 2, 0:HEAD_DIM, :] = near[2]

        pl.when(core == head // 2)(lambda: put(keep_ref))
        pl.when(core != head // 2)(lambda: put(send_ref))
    for head in range(LOCAL):
        gain = gain_ref[head : head + 1, :]
        gate = gate_ref[head].astype(F32)
        sigmoid = jax.nn.sigmoid(gate)
        mixed = mixed_ref[head]
        gated = mixed * (gate * sigmoid)
        out_ref[head] = (gain * (gated * inverse)).astype(BF16)
        grad_gated = inverse * (grad_ref[head].astype(F32) * gain) - gated * pull
        grad_gate_ref[head] = (grad_gated * mixed * sigmoid * (1.0 + gate * (1.0 - sigmoid))).astype(BF16)


def down_kernel(
    own_ref, one_ref, two_ref, three_ref, near_ref, near_other_ref, info_ref, wide_ref,
    m0_ref, m1_ref, m2_ref, m3_ref,
):
    x, y, _ = place()
    refs = (own_ref, one_ref, two_ref, three_ref)
    carry_x = jnp.exp(wide_ref[:, 1:2, :])
    first = x == 0
    c1 = flag(x <= 2)
    c2 = flag(first) * carry_x + flag(x == 1)
    c3 = flag(first) * carry_x
    body = slice(0, HEAD_DIM)
    state = c1 * one_ref[:, body, :] + c2 * two_ref[:, body, :] + c3 * three_ref[:, body, :]
    tails = [ref[:, HEAD_DIM:, :] for ref in refs]
    where = [lax.rem(x + step, 4) for step in range(4)]
    by_x = [sum(flag(where[i] == j) * tails[i] for i in range(4)) for j in range(4)]
    gains = ((by_x[0] + by_x[1]) + by_x[2]) + by_x[3]
    low = near_ref[0, :, body, :] + near_other_ref[0, :, body, :]
    high = near_ref[1, :, body, :] + near_other_ref[1, :, body, :]
    totals = [info_ref[:, j : j + 1, :] for j in range(4)]
    after = [totals[1] + totals[2] + totals[3], totals[2] + totals[3], totals[3], jnp.zeros_like(totals[3])]
    after = [jnp.exp(part) for part in after]
    carry_y = jnp.exp(totals[1])
    for step, ref in enumerate((m0_ref, m1_ref, m2_ref, m3_ref)):
        to = order(y, step)
        message = sum(flag(to == j) * after[j] for j in range(4)) * state
        if step == 1:
            message = message + flag(lax.rem(y, 2) == 1) * low
        if step:
            message = message + flag(y >= 2) * (flag(to == 1) + flag(to == 0) * carry_y) * high
        ref[:, body, :] = message
        ref[:, HEAD_DIM:, :] = gains


def backward_kernel(
    q_ref, k_ref, v_ref, g_ref, mix_ref, weight_ref, scored_ref, bucket_ref, finer_ref, cols_ref, run_ref,
    grad_q_ref, grad_k_ref, grad_v_ref, levels_ref,
):
    early, late = iotas((WIDTH, WIDTH))
    crossed = jnp.bitwise_xor(early, late)
    ones = jnp.ones((8, HEAD_DIM), BF16)
    for level in range(DEPTH + 1 + INTER, LEVELS):
        levels_ref[level] = jnp.zeros((LOCAL, WIDTH), F32)
    for head in range(LOCAL):
        q, k, v, g = q_ref[head], k_ref[head], v_ref[head], g_ref[head]
        grad_mixing = dot(v, g, NT)
        grad_scores = (grad_mixing * weight_ref[head]).astype(BF16)
        grad_k_ref[head] = dot(grad_scores, q, NN)
        grad_v_ref[head] = dot(mix_ref[head], g, NN)
        grad_q = dot(grad_scores, k, TN)
        moved = grad_mixing * scored_ref[head]
        for level in range(DEPTH + 1):
            inside = crossed == 0
            if level:
                inside = (crossed >= 2 ** (level - 1)) & (crossed < 2**level)
            levels_ref[level, head : head + 1, :] = jnp.sum(jnp.where(inside, moved, 0.0), axis=0, keepdims=True)
        wide_q = q.astype(F32)
        grown = jnp.exp(run_ref[head : head + 1, :])
        for level in range(INTER):
            piece = slice(HEAD_DIM * level, HEAD_DIM * (level + 1))
            pulled = dot(g, bucket_ref[head, :, piece], NT) + dot(g, finer_ref[head, :, piece], NT)
            at = 4 * level + head
            grad_q = grad_q + cols_ref[:, at : at + 1] * pulled
            high, low = split(wide_q * pulled)
            sums = dot(ones, high, NT) + dot(ones, low, NT)
            levels_ref[DEPTH + 1 + level, head : head + 1, :] = grown * sums[0:1, :]
        grad_q_ref[head] = grad_q.astype(BF16)


def join_kernel(own_ref, one_ref, two_ref, three_ref, half_ref, gain_ref):
    y = place()[1]
    refs = (own_ref, one_ref, two_ref, three_ref)
    where = [lax.rem(y + step, 4) for step in range(4)]
    tails = [ref[0, HEAD_DIM : HEAD_DIM + LOCAL, :] for ref in refs]
    by_y = [sum(flag(where[i] == j) * tails[i] for i in range(4)) for j in range(4)]
    gain_ref[...] = ((by_y[0] + by_y[1]) + by_y[2]) + by_y[3]
    half_ref[...] = sum(ref[:, 0:HEAD_DIM, :] for ref in refs)


def final_kernel(
    k_ref, v_ref, cols_ref, half_ref, other_ref, zeroth_ref, first_ref, grad_k_ref, grad_v_ref, out_k_ref, out_v_ref
):
    core = place()[2]
    even = core == 0
    for head in range(LOCAL):
        slot = head % 2
        half = jnp.where(core == head // 2, half_ref[slot], other_ref[slot])
        carry = jnp.exp(first_ref[0, HEAD_DIM + 4 + head : HEAD_DIM + 5 + head, :])
        high, low = split(jnp.where(even, carry * half + zeroth_ref[head], half))
        tail = cols_ref[:, 24 + head : 25 + head]
        k, v = k_ref[head], v_ref[head]
        out_k_ref[head] = (grad_k_ref[head] + tail * (dot(v, high, NT) + dot(v, low, NT))).astype(BF16)
        out_v_ref[head] = (grad_v_ref[head] + tail * (dot(k, high, NN) + dot(k, low, NN))).astype(BF16)


def call(kernel, outs, *args, scratch=(), flops=0, hbm=(), limit=12):
    size = sum(a.size * a.dtype.itemsize for a in args)
    shapes = [jax.ShapeDtypeStruct(shape, kind) for shape, kind in outs]
    size += sum(s.size * s.dtype.itemsize for s in shapes)
    spaces = [pltpu.HBM if i in hbm else pltpu.VMEM for i in range(len(args))]
    return pl.pallas_call(
        kernel,
        out_shape=shapes,
        in_specs=[pl.BlockSpec(memory_space=space) for space in spaces],
        scratch_shapes=list(scratch),
        cost_estimate=pl.CostEstimate(flops=flops, bytes_accessed=size, transcendentals=0),
        compiler_params=pltpu.CompilerParams(vmem_limit_bytes=limit * 2**20),
    )(*args)


def layer(queries, keys, values, log_decay, level_weight, gate_input, norm_gain, out_grad):
    level_rows = jnp.transpose(level_weight, (1, 0, 2))
    message = ((2, ROWS, HEAD_DIM), F32)
    double = ((2, 2, ROWS, HEAD_DIM), F32)
    tokens = (LOCAL, WIDTH, HEAD_DIM)
    square = (LOCAL, WIDTH, WIDTH)
    info = ((2, 8, HEAD_DIM), F32)
    columns = ((WIDTH, HEAD_DIM), F32)

    keep, away, running = call(
        state_kernel,
        [message, message, ((LOCAL, WIDTH), F32)],
        log_decay, keys, values,
        scratch=[pltpu.VMEM(tokens, BF16), pltpu.VMEM(tokens, BF16), pltpu.VMEM((16, WIDTH), F32), pltpu.SemaphoreType.DMA((2,))],
        hbm=(1, 2),
    )
    first = send(away, SWAP)
    (chip,) = call(pair_kernel, [message], keep, first)
    from_y = [send(chip, along_y(step)) for step in (1, 2, 3)]
    rest = send(keep, UP)
    inner, mixing, weight, scored, cols = call(
        intra_kernel,
        [(tokens, F32), (square, BF16), (square, F32), (square, F32), columns],
        queries, keys, values, level_rows, running,
        scratch=[pltpu.VMEM((HEAD_DIM, WIDTH), F32)],
        flops=10**9,
    )
    row, near, totals_y = call(y_kernel, [message, double, info], chip, *from_y)
    from_x = [send(row, along_x(step)) for step in (1, 2, 3)]
    near_other = send(near, SWAP)
    far, totals_x = call(x_kernel, [double, info], row, *from_x, totals_y)
    far_other = send(far, SWAP)
    bucket_kind = ((LOCAL, HEAD_DIM, INTER * HEAD_DIM), BF16)
    mixed, pay, bucket, finer, shift = call(
        mixed_kernel,
        [(tokens, F32), ((8, 4, HEAD_DIM), F32), bucket_kind, bucket_kind, ((LOCAL, 8, HEAD_DIM), F32)],
        queries, inner, gate_input, out_grad, norm_gain, cols, near, near_other, far, far_other, first, rest,
    )
    sums = lax.all_to_all(pay, "head", 0, 0, tiled=True)
    grad_mixed, scale, far_keep, far_away = call(
        gate_kernel,
        [(tokens, BF16), ((2, WIDTH, HEAD_DIM), F32), double, double],
        queries, mixed, gate_input, out_grad, norm_gain, cols, shift, sums,
    )
    to_one, to_far = call(meet_kernel, [message] * 2, far_keep, send(far_away, SWAP))
    back_x = [send(to_one, along_x(-1)), send(to_far, along_x(-2)), send(to_far, along_x(-3))]
    layer_out, grad_gate, near_keep, near_away, zeroth = call(
        close_kernel,
        [(tokens, BF16)] * 2 + [double] * 2 + [((LOCAL, HEAD_DIM, HEAD_DIM), F32)],
        queries, grad_mixed, mixed, gate_input, out_grad, norm_gain, cols, shift, scale,
        flops=10**9,
    )
    near_back = send(near_away, SWAP)
    messages = call(down_kernel, [message] * 4, to_far, *back_x, near_keep, near_back, totals_y, totals_x)
    back_y = [messages[0]] + [send(messages[step], along_y(-step)) for step in (1, 2, 3)]
    zeroth_back = send(zeroth, DOWN)
    grad_queries, grad_k, grad_v, levels = call(
        backward_kernel,
        [(tokens, BF16), (tokens, F32), (tokens, F32), ((LEVELS, LOCAL, WIDTH), F32)],
        queries, keys, values, grad_mixed, mixing, weight, scored, bucket, finer, cols, running,
        flops=10**9,
    )
    half, grad_gain = call(join_kernel, [((2, HEAD_DIM, HEAD_DIM), F32), ((LOCAL, HEAD_DIM), F32)], *back_y)
    half_other = send(half, SWAP)
    grad_keys, grad_values = call(
        final_kernel,
        [(tokens, BF16)] * 2,
        keys, values, cols, half, half_other, zeroth_back, first, grad_k, grad_v,
    )
    grad_levels = jnp.transpose(levels, (1, 0, 2))
    return (layer_out, grad_queries, grad_keys, grad_values, grad_levels, grad_gate, grad_gain)


def solution(mesh):
    rows = P("head", "seq", None)
    in_specs = (rows, rows, rows, P("head", "seq"), P("head", None, "seq"), rows, P("head", None), rows)
    out_specs = (rows, rows, rows, rows, P("head", None, "seq"), rows, P("head", None))
    return jax.shard_map(layer, mesh=mesh, in_specs=in_specs, out_specs=out_specs, check_vma=False)
```

profile of v0, /device:TPU:1, one launch (start us, length us, event | category | flops | bytes accessed | tf_op | source)
XLA Modules:
  0.0 87.4 jit_solution(361499477031836718)
XLA Ops:
  0.6 0.9 %copy-done = bf16[4,256,128]{2,1,0:T(8,128)(2,1)S(1)} copy-done((bf16[4,256,128]{2,1,0:T(8,128)(2,1)S(1)}, bf16[4,256,128]{2,1,0:T(8,128)(2,1)}, u32[]{:S(2)}) %copy-start) | copy-done | bytes 262168
  1.6 0.9 %copy-done.2 = bf16[4,256,128]{2,1,0:T(8,128)(2,1)S(1)} copy-done((bf16[4,256,128]{2,1,0:T(8,128)(2,1)S(1)}, bf16[4,256,128]{2,1,0:T(8,128)(2,1)}, u32[]{:S(2)}) %copy-start.2) | copy-done | bytes 262168
  3.2 1.7 %shard_map.135 = (f32[2,136,128]{2,1,0:T(8,128)S(1)}, f32[2,136,128]{2,1,0:T(8,128)S(1)}, f32[4,256]{1,0:T(4,128)S(1)}) custom-call(f32[4,256]{1,0:T(4,128)S(1)} %copy-done.8, bf16[4,256,128]{2,1,0:T(8,128)(2,1)S(1)} %copy-done, bf16[4,256,128]{2,1,0:T(8,128)(2,1)S(1)} %copy-done.2), custom_call_target="tpu_custom_call" | custom-call | bytes 811008 | tf_op jit(solution)/shard_map/pallas_call | solution.py:439
  4.9 3.3 %collective-permute-start = (f32[2,136,128]{2,1,0:T(8,128)S(1)}, f32[2,136,128]{2,1,0:T(8,128)S(1)}, u32[]{:S(2)}, u32[]{:S(2)}) collective-permute-start(f32[2,136,128]{2,1,0:T(8,128)S(1)} %get-tuple-element.52), channel_id=1, source_target_pairs={{0,8},{8,0},{16,24},{24,16},{32,40},{40,32},{48,56},{56,48},{64,72... | collective-permute-start | bytes 417800 | tf_op jit(solution)/shard_map/ppermute | solution.py:55
  8.2 1.0 %collective-permute-done.first_ref = f32[2,136,128]{2,1,0:T(8,128)S(1)} collective-permute-done((f32[2,136,128]{2,1,0:T(8,128)S(1)}, f32[2,136,128]{2,1,0:T(8,128)S(1)}, u32[]{:S(2)}, u32[]{:S(2)}) %collective-permute-start) | collective-permute-done | bytes 139296 | tf_op jit(solution)/shard_map/ppermute | solution.py:55
  9.4 2.2 %collective-permute-start.2 = (f32[2,136,128]{2,1,0:T(8,128)S(1)}, f32[2,136,128]{2,1,0:T(8,128)S(1)}, u32[]{:S(2)}, u32[]{:S(2)}) collective-permute-start(f32[2,136,128]{2,1,0:T(8,128)S(1)} %shard_map.137.own_ref), channel_id=1, source_target_pairs={{0,32},{8,40},{16,48},{24,56},{32,0},{40,8},{48,16},{56,24},{64,96... | collective-permute-start | bytes 417800 | tf_op jit(solution)/shard_map/ppermute | solution.py:55
  11.6 1.1 %collective-permute-start.3 = (f32[2,136,128]{2,1,0:T(8,128)S(1)}, f32[2,136,128]{2,1,0:T(8,128)S(1)}, u32[]{:S(2)}, u32[]{:S(2)}) collective-permute-start(f32[2,136,128]{2,1,0:T(8,128)S(1)} %shard_map.137.own_ref), channel_id=1, source_target_pairs={{0,48},{8,56},{16,0},{24,8},{32,16},{40,24},{48,32},{56,40},{64,11... | collective-permute-start | bytes 417800 | tf_op jit(solution)/shard_map/ppermute | solution.py:55
  12.6 3.3 %collective-permute-done.1.one_ref = f32[2,136,128]{2,1,0:T(8,128)S(1)} collective-permute-done((f32[2,136,128]{2,1,0:T(8,128)S(1)}, f32[2,136,128]{2,1,0:T(8,128)S(1)}, u32[]{:S(2)}, u32[]{:S(2)}) %collective-permute-start.1) | collective-permute-done | bytes 139296 | tf_op jit(solution)/shard_map/ppermute | solution.py:55
  15.9 2.1 %collective-permute-done.2.two_ref = f32[2,136,128]{2,1,0:T(8,128)S(1)} collective-permute-done((f32[2,136,128]{2,1,0:T(8,128)S(1)}, f32[2,136,128]{2,1,0:T(8,128)S(1)}, u32[]{:S(2)}, u32[]{:S(2)}) %collective-permute-start.2) | collective-permute-done | bytes 139296 | tf_op jit(solution)/shard_map/ppermute | solution.py:55
  19.4 2.5 %collective-permute-start.6 = (f32[2,136,128]{2,1,0:T(8,128)S(1)}, f32[2,136,128]{2,1,0:T(8,128)S(1)}, u32[]{:S(2)}, u32[]{:S(2)}) collective-permute-start(f32[2,136,128]{2,1,0:T(8,128)S(1)} %get-tuple-element.54.own_ref), channel_id=1, source_target_pairs={{0,128},{8,136},{16,144},{24,152},{32,160},{40,168},{48,176},{56,1... | collective-permute-start | bytes 417800 | tf_op jit(solution)/shard_map/ppermute | solution.py:55
  21.8 1.1 %collective-permute-start.7 = (f32[2,136,128]{2,1,0:T(8,128)S(1)}, f32[2,136,128]{2,1,0:T(8,128)S(1)}, u32[]{:S(2)}, u32[]{:S(2)}) collective-permute-start(f32[2,136,128]{2,1,0:T(8,128)S(1)} %get-tuple-element.54.own_ref), channel_id=1, source_target_pairs={{0,192},{8,200},{16,208},{24,216},{32,224},{40,232},{48,240},{56,2... | collective-permute-start | bytes 417800 | tf_op jit(solution)/shard_map/ppermute | solution.py:55
  23.0 2.1 %collective-permute-start.4 = (f32[2,2,136,128]{3,2,1,0:T(8,128)S(1)}, f32[2,2,136,128]{3,2,1,0:T(8,128)S(1)}, u32[]{:S(2)}, u32[]{:S(2)}) collective-permute-start(f32[2,2,136,128]{3,2,1,0:T(8,128)S(1)} %get-tuple-element.53.near_ref), channel_id=1, source_target_pairs={{0,8},{8,0},{16,24},{24,16},{32,40},{40,32},{48,56},{56,48},{64,72... | collective-permute-start | bytes 835592 | tf_op jit(solution)/shard_map/ppermute | solution.py:55
  25.0 2.0 %collective-permute-done.6.two_ref = f32[2,136,128]{2,1,0:T(8,128)S(1)} collective-permute-done((f32[2,136,128]{2,1,0:T(8,128)S(1)}, f32[2,136,128]{2,1,0:T(8,128)S(1)}, u32[]{:S(2)}, u32[]{:S(2)}) %collective-permute-start.6) | collective-permute-done | bytes 139296 | tf_op jit(solution)/shard_map/ppermute | solution.py:55
  27.2 2.7 %collective-permute-start.8 = (f32[2,2,136,128]{3,2,1,0:T(8,128)S(1)}, f32[2,2,136,128]{3,2,1,0:T(8,128)S(1)}, u32[]{:S(2)}, u32[]{:S(2)}) collective-permute-start(f32[2,2,136,128]{3,2,1,0:T(8,128)S(1)} %get-tuple-element.56.far_ref), channel_id=1, source_target_pairs={{0,8},{8,0},{16,24},{24,16},{32,40},{40,32},{48,56},{56,48},{64,72... | collective-permute-start | bytes 835592 | tf_op jit(solution)/shard_map/ppermute | solution.py:55
  29.9 1.3 %collective-permute-start.9 = (f32[2,136,128]{2,1,0:T(8,128)S(1)}, f32[2,136,128]{2,1,0:T(8,128)S(1)}, u32[]{:S(2)}, u32[]{:S(2)}) collective-permute-start(f32[2,136,128]{2,1,0:T(8,128)S(1)} %get-tuple-element.51.keep_ref), channel_id=1, source_target_pairs={{0,8},{16,24},{32,40},{48,56},{64,72},{80,88},{96,104},{112,120},{... | collective-permute-start | bytes 417800 | tf_op jit(solution)/shard_map/ppermute | solution.py:55
  31.3 1.1 %shard_map.136 = (f32[4,256,128]{2,1,0:T(8,128)S(1)}, bf16[4,256,256]{2,1,0:T(8,128)(2,1)S(1)}, f32[4,256,256]{2,1,0:T(8,128)S(1)}, f32[4,256,256]{2,1,0:T(8,128)S(1)}, f32[256,128]{1,0:T(8,128)S(1)}) custom-call(bf16[4,256,128]{2,1,0:T(8,128)(2,1)S(1)} %copy-done.4, bf16[4,256,128]{2,1,0:T(8,128)(2,1)S(1)} %copy-done.1, bf16[4,256,128]{2,1,0:T(8,128)(2,1)S(1)} %copy-done.3, ...), custom_call_target="tpu_custom_call" | custom-call | flops 1000000000 | bytes 4153344 | tf_op jit(solution)/shard_map/pallas_call | solution.py:439
  32.4 0.8 collective-permute-done.9.rest_ref
  33.2 1.7 %shard_map.140 = (f32[4,256,128]{2,1,0:T(8,128)S(1)}, f32[8,4,128]{2,1,0:T(4,128)S(1)}, bf16[4,128,640]{2,1,0:T(8,128)(2,1)S(1)}, bf16[4,128,640]{2,1,0:T(8,128)(2,1)S(1)}, f32[4,8,128]{2,1,0:T(8,128)S(1)}) custom-call(bf16[4,256,128]{2,1,0:T(8,128)(2,1)S(1)} %copy-done.4, f32[4,256,128]{2,1,0:T(8,128)S(1)} %get-tuple-element.49.inner_ref, ...), custom_call_target="tpu_custom_call" | custom-call | bytes 4704256 | tf_op jit(solution)/shard_map/pallas_call | solution.py:439
  34.9 14.3 %all_to_all.5.sums_ref = f32[8,4,128]{2,1,0:T(4,128)S(1)} all-to-all(f32[8,4,128]{2,1,0:T(4,128)S(1)} %get-tuple-element.59), channel_id=1, replica_groups=mesh['seq'=32,'head'=8] {'head'}, dimensions={0} | all-to-all | bytes 32768 | tf_op jit(solution)/shard_map/all_to_all | solution.py:487
  49.2 1.7 %shard_map.141 = (bf16[4,256,128]{2,1,0:T(8,128)(2,1)S(1)}, f32[2,256,128]{2,1,0:T(8,128)S(1)}, f32[2,2,136,128]{3,2,1,0:T(8,128)S(1)}, f32[2,2,136,128]{3,2,1,0:T(8,128)S(1)}) custom-call(bf16[4,256,128]{2,1,0:T(8,128)(2,1)S(1)} %copy-done.4, f32[4,256,128]{2,1,0:T(8,128)S(1)} %get-tuple-element.57.mixed_ref, bf16[4,256,128]{2,1,0:T(8,128)(2,1)S(1)} %copy-done.5, ...), custom_call_target="tpu_custom_call" | custom-call | bytes 2557952 | tf_op jit(solution)/shard_map/pallas_call | solution.py:439
  50.9 2.5 %collective-permute-start.10 = (f32[2,2,136,128]{3,2,1,0:T(8,128)S(1)}, f32[2,2,136,128]{3,2,1,0:T(8,128)S(1)}, u32[]{:S(2)}, u32[]{:S(2)}) collective-permute-start(f32[2,2,136,128]{3,2,1,0:T(8,128)S(1)} %get-tuple-element.70), channel_id=1, source_target_pairs={{0,8},{8,0},{16,24},{24,16},{32,40},{40,32},{48,56},{56,48},{64,72... | collective-permute-start | bytes 835592 | tf_op jit(solution)/shard_map/ppermute | solution.py:55
  53.3 2.9 %shard_map.142 = (bf16[4,256,128]{2,1,0:T(8,128)(2,1)}, bf16[4,256,128]{2,1,0:T(8,128)(2,1)}, f32[2,2,136,128]{3,2,1,0:T(8,128)S(1)}, f32[2,2,136,128]{3,2,1,0:T(8,128)S(1)}, f32[4,128,128]{2,1,0:T(8,128)S(1)}) custom-call(bf16[4,256,128]{2,1,0:T(8,128)(2,1)S(1)} %copy-done.4, bf16[4,256,128]{2,1,0:T(8,128)(2,1)S(1)} %get-tuple-element.60.g_ref, ...), custom_call_target="tpu_custom_call" | custom-call | flops 1000000000 | bytes 3328000 | tf_op jit(solution)/shard_map/pallas_call | solution.py:439
  56.2 2.4 %collective-permute-start.11 = (f32[2,136,128]{2,1,0:T(8,128)S(1)}, f32[2,136,128]{2,1,0:T(8,128)S(1)}, u32[]{:S(2)}, u32[]{:S(2)}) collective-permute-start(f32[2,136,128]{2,1,0:T(8,128)S(1)} %get-tuple-element.72), channel_id=1, source_target_pairs={{0,192},{8,200},{16,208},{24,216},{32,224},{40,232},{48,240},{56,2... | collective-permute-start | bytes 417800 | tf_op jit(solution)/shard_map/ppermute | solution.py:55
  59.6 2.4 %collective-permute-done.11.one_ref = f32[2,136,128]{2,1,0:T(8,128)S(1)} collective-permute-done((f32[2,136,128]{2,1,0:T(8,128)S(1)}, f32[2,136,128]{2,1,0:T(8,128)S(1)}, u32[]{:S(2)}, u32[]{:S(2)}) %collective-permute-start.11) | collective-permute-done | bytes 139296 | tf_op jit(solution)/shard_map/ppermute | solution.py:55
  61.9 2.7 %collective-permute-done.12.two_ref = f32[2,136,128]{2,1,0:T(8,128)S(1)} collective-permute-done((f32[2,136,128]{2,1,0:T(8,128)S(1)}, f32[2,136,128]{2,1,0:T(8,128)S(1)}, u32[]{:S(2)}, u32[]{:S(2)}) %collective-permute-start.12) | collective-permute-done | bytes 139296 | tf_op jit(solution)/shard_map/ppermute | solution.py:55
  64.6 4.1 %collective-permute-done.13.three_ref = f32[2,136,128]{2,1,0:T(8,128)S(1)} collective-permute-done((f32[2,136,128]{2,1,0:T(8,128)S(1)}, f32[2,136,128]{2,1,0:T(8,128)S(1)}, u32[]{:S(2)}, u32[]{:S(2)}) %collective-permute-start.13) | collective-permute-done | bytes 139296 | tf_op jit(solution)/shard_map/ppermute | solution.py:55
  68.9 2.1 %collective-permute-start.15 = (f32[2,136,128]{2,1,0:T(8,128)S(1)}, f32[2,136,128]{2,1,0:T(8,128)S(1)}, u32[]{:S(2)}, u32[]{:S(2)}) collective-permute-start(f32[2,136,128]{2,1,0:T(8,128)S(1)} %get-tuple-element.77), channel_id=1, source_target_pairs={{0,48},{8,56},{16,0},{24,8},{32,16},{40,24},{48,32},{56,40},{64,11... | collective-permute-start | bytes 417800 | tf_op jit(solution)/shard_map/ppermute | solution.py:55
  71.9 3.2 %collective-permute-start.19 = (f32[4,128,128]{2,1,0:T(8,128)S(1)}, f32[4,128,128]{2,1,0:T(8,128)S(1)}, u32[]{:S(2)}, u32[]{:S(2)}) collective-permute-start(f32[4,128,128]{2,1,0:T(8,128)S(1)} %get-tuple-element.81), channel_id=1, source_target_pairs={{8,0},{24,16},{40,32},{56,48},{72,64},{88,80},{104,96},{120,112},{... | collective-permute-start | bytes 786440 | tf_op jit(solution)/shard_map/ppermute | solution.py:55
  75.1 1.8 %collective-permute-done.16.two_ref = f32[2,136,128]{2,1,0:T(8,128)S(1)} collective-permute-done((f32[2,136,128]{2,1,0:T(8,128)S(1)}, f32[2,136,128]{2,1,0:T(8,128)S(1)}, u32[]{:S(2)}, u32[]{:S(2)}) %collective-permute-start.16) | collective-permute-done | bytes 139296 | tf_op jit(solution)/shard_map/ppermute | solution.py:55
  76.9 4.1 %collective-permute-done.17.three_ref = f32[2,136,128]{2,1,0:T(8,128)S(1)} collective-permute-done((f32[2,136,128]{2,1,0:T(8,128)S(1)}, f32[2,136,128]{2,1,0:T(8,128)S(1)}, u32[]{:S(2)}, u32[]{:S(2)}) %collective-permute-start.17) | collective-permute-done | bytes 139296 | tf_op jit(solution)/shard_map/ppermute | solution.py:55
  82.1 4.0 %shard_map.143 = (bf16[4,256,128]{2,1,0:T(8,128)(2,1)}, f32[4,256,128]{2,1,0:T(8,128)S(1)}, f32[4,256,128]{2,1,0:T(8,128)S(1)}, f32[21,4,256]{2,1,0:T(4,128)}) custom-call(bf16[4,256,128]{2,1,0:T(8,128)(2,1)S(1)} %copy-done.4, bf16[4,256,128]{2,1,0:T(8,128)(2,1)S(1)} %copy-done.1, bf16[4,256,128]{2,1,0:T(8,128)(2,1)S(1)} %copy-done.3, ...), custom_call_target="tpu_custom_call" | custom-call | flops 1000000000 | bytes 6512640 | tf_op jit(solution)/shard_map/pallas_call | solution.py:439
  86.2 1.3 %shard_map.147 = (bf16[4,256,128]{2,1,0:T(8,128)(2,1)}, bf16[4,256,128]{2,1,0:T(8,128)(2,1)}) custom-call(bf16[4,256,128]{2,1,0:T(8,128)(2,1)S(1)} %copy-done.1, bf16[4,256,128]{2,1,0:T(8,128)(2,1)S(1)} %copy-done.3, f32[256,128]{1,0:T(8,128)S(1)} %get-tuple-element.50.cols_ref, f32[2,128,128]{2,1,0:T(8,128)S(1)} %get-tuple-element.80.half_ref, ...), custom_call_target="tpu_custom_call" | custom-call | bytes 2891776 | tf_op jit(solution)/shard_map/pallas_call | solution.py:439
  (42 shorter events, 5.6 us)
Async XLA Ops:
  0.6 1.0 %copy-start = (bf16[4,256,128]{2,1,0:T(8,128)(2,1)S(1)}, bf16[4,256,128]{2,1,0:T(8,128)(2,1)}, u32[]{:S(2)}) copy-start(bf16[4,256,128]{2,1,0:T(8,128)(2,1)} %k_ref.5) | copy-start | bytes 786436
  1.6 0.9 %copy-start.2 = (bf16[4,256,128]{2,1,0:T(8,128)(2,1)S(1)}, bf16[4,256,128]{2,1,0:T(8,128)(2,1)}, u32[]{:S(2)}) copy-start(bf16[4,256,128]{2,1,0:T(8,128)(2,1)} %v_ref.5) | copy-start | bytes 786436
  2.5 0.7 copy-start.8
  4.9 4.3 %collective-permute-start = (f32[2,136,128]{2,1,0:T(8,128)S(1)}, f32[2,136,128]{2,1,0:T(8,128)S(1)}, u32[]{:S(2)}, u32[]{:S(2)}) collective-permute-start(f32[2,136,128]{2,1,0:T(8,128)S(1)} %get-tuple-element.52), channel_id=1, source_target_pairs={{0,8},{8,0},{16,24},{24,16},{32,40},{40,32},{48,56},{56,48},{64,72... | collective-permute-start | bytes 417800 | tf_op jit(solution)/shard_map/ppermute | solution.py:55
  9.3 6.6 %collective-permute-start.1 = (f32[2,136,128]{2,1,0:T(8,128)S(1)}, f32[2,136,128]{2,1,0:T(8,128)S(1)}, u32[]{:S(2)}, u32[]{:S(2)}) collective-permute-start(f32[2,136,128]{2,1,0:T(8,128)S(1)} %shard_map.137.own_ref), channel_id=1, source_target_pairs={{0,16},{8,24},{16,32},{24,40},{32,48},{40,56},{48,0},{56,8},{64,80... | collective-permute-start | bytes 417800 | tf_op jit(solution)/shard_map/ppermute | solution.py:55
  9.4 8.6 %collective-permute-start.2 = (f32[2,136,128]{2,1,0:T(8,128)S(1)}, f32[2,136,128]{2,1,0:T(8,128)S(1)}, u32[]{:S(2)}, u32[]{:S(2)}) collective-permute-start(f32[2,136,128]{2,1,0:T(8,128)S(1)} %shard_map.137.own_ref), channel_id=1, source_target_pairs={{0,32},{8,40},{16,48},{24,56},{32,0},{40,8},{48,16},{56,24},{64,96... | collective-permute-start | bytes 417800 | tf_op jit(solution)/shard_map/ppermute | solution.py:55
  11.6 7.2 %collective-permute-start.3 = (f32[2,136,128]{2,1,0:T(8,128)S(1)}, f32[2,136,128]{2,1,0:T(8,128)S(1)}, u32[]{:S(2)}, u32[]{:S(2)}) collective-permute-start(f32[2,136,128]{2,1,0:T(8,128)S(1)} %shard_map.137.own_ref), channel_id=1, source_target_pairs={{0,48},{8,56},{16,0},{24,8},{32,16},{40,24},{48,32},{56,40},{64,11... | collective-permute-start | bytes 417800 | tf_op jit(solution)/shard_map/ppermute | solution.py:55
  18.7 12.5 %copy-start.4 = (bf16[4,256,128]{2,1,0:T(8,128)(2,1)S(1)}, bf16[4,256,128]{2,1,0:T(8,128)(2,1)}, u32[]{:S(2)}) copy-start(bf16[4,256,128]{2,1,0:T(8,128)(2,1)} %q_ref.9) | copy-start | bytes 786436
  18.7 12.5 %copy-start.9 = (f32[4,21,256]{2,0,1:T(4,128)S(1)}, f32[4,21,256]{2,0,1:T(4,128)}, u32[]{:S(2)}) copy-start(f32[4,21,256]{2,0,1:T(4,128)} %param.12) | copy-start | bytes 258052
  18.8 6.2 %collective-permute-start.5 = (f32[2,136,128]{2,1,0:T(8,128)S(1)}, f32[2,136,128]{2,1,0:T(8,128)S(1)}, u32[]{:S(2)}, u32[]{:S(2)}) collective-permute-start(f32[2,136,128]{2,1,0:T(8,128)S(1)} %get-tuple-element.54.own_ref), channel_id=1, source_target_pairs={{0,64},{8,72},{16,80},{24,88},{32,96},{40,104},{48,112},{56,120},{... | collective-permute-start | bytes 417800 | tf_op jit(solution)/shard_map/ppermute | solution.py:55
  19.4 7.7 %collective-permute-start.6 = (f32[2,136,128]{2,1,0:T(8,128)S(1)}, f32[2,136,128]{2,1,0:T(8,128)S(1)}, u32[]{:S(2)}, u32[]{:S(2)}) collective-permute-start(f32[2,136,128]{2,1,0:T(8,128)S(1)} %get-tuple-element.54.own_ref), channel_id=1, source_target_pairs={{0,128},{8,136},{16,144},{24,152},{32,160},{40,168},{48,176},{56,1... | collective-permute-start | bytes 417800 | tf_op jit(solution)/shard_map/ppermute | solution.py:55
  21.8 5.3 %collective-permute-start.7 = (f32[2,136,128]{2,1,0:T(8,128)S(1)}, f32[2,136,128]{2,1,0:T(8,128)S(1)}, u32[]{:S(2)}, u32[]{:S(2)}) collective-permute-start(f32[2,136,128]{2,1,0:T(8,128)S(1)} %get-tuple-element.54.own_ref), channel_id=1, source_target_pairs={{0,192},{8,200},{16,208},{24,216},{32,224},{40,232},{48,240},{56,2... | collective-permute-start | bytes 417800 | tf_op jit(solution)/shard_map/ppermute | solution.py:55
  23.0 10.2 %collective-permute-start.4 = (f32[2,2,136,128]{3,2,1,0:T(8,128)S(1)}, f32[2,2,136,128]{3,2,1,0:T(8,128)S(1)}, u32[]{:S(2)}, u32[]{:S(2)}) collective-permute-start(f32[2,2,136,128]{3,2,1,0:T(8,128)S(1)} %get-tuple-element.53.near_ref), channel_id=1, source_target_pairs={{0,8},{8,0},{16,24},{24,16},{32,40},{40,32},{48,56},{56,48},{64,72... | collective-permute-start | bytes 835592 | tf_op jit(solution)/shard_map/ppermute | solution.py:55
  27.1 4.1 %copy-start.1 = (bf16[4,256,128]{2,1,0:T(8,128)(2,1)S(1)}, bf16[4,256,128]{2,1,0:T(8,128)(2,1)}, u32[]{:S(2)}) copy-start(bf16[4,256,128]{2,1,0:T(8,128)(2,1)} %k_ref.5) | copy-start | bytes 786436
  27.1 4.1 %copy-start.3 = (bf16[4,256,128]{2,1,0:T(8,128)(2,1)S(1)}, bf16[4,256,128]{2,1,0:T(8,128)(2,1)}, u32[]{:S(2)}) copy-start(bf16[4,256,128]{2,1,0:T(8,128)(2,1)} %v_ref.5) | copy-start | bytes 786436
  27.2 6.0 %collective-permute-start.8 = (f32[2,2,136,128]{3,2,1,0:T(8,128)S(1)}, f32[2,2,136,128]{3,2,1,0:T(8,128)S(1)}, u32[]{:S(2)}, u32[]{:S(2)}) collective-permute-start(f32[2,2,136,128]{3,2,1,0:T(8,128)S(1)} %get-tuple-element.56.far_ref), channel_id=1, source_target_pairs={{0,8},{8,0},{16,24},{24,16},{32,40},{40,32},{48,56},{56,48},{64,72... | collective-permute-start | bytes 835592 | tf_op jit(solution)/shard_map/ppermute | solution.py:55
  29.9 3.2 %collective-permute-start.9 = (f32[2,136,128]{2,1,0:T(8,128)S(1)}, f32[2,136,128]{2,1,0:T(8,128)S(1)}, u32[]{:S(2)}, u32[]{:S(2)}) collective-permute-start(f32[2,136,128]{2,1,0:T(8,128)S(1)} %get-tuple-element.51.keep_ref), channel_id=1, source_target_pairs={{0,8},{16,24},{32,40},{48,56},{64,72},{80,88},{96,104},{112,120},{... | collective-permute-start | bytes 417800 | tf_op jit(solution)/shard_map/ppermute | solution.py:55
  31.3 1.9 %copy-start.5 = (bf16[4,256,128]{2,1,0:T(8,128)(2,1)S(1)}, bf16[4,256,128]{2,1,0:T(8,128)(2,1)}, u32[]{:S(2)}) copy-start(bf16[4,256,128]{2,1,0:T(8,128)(2,1)} %gate_ref.5) | copy-start | bytes 786436
  31.3 1.9 %copy-start.6 = (bf16[4,256,128]{2,1,0:T(8,128)(2,1)S(1)}, bf16[4,256,128]{2,1,0:T(8,128)(2,1)}, u32[]{:S(2)}) copy-start(bf16[4,256,128]{2,1,0:T(8,128)(2,1)} %grad_ref.5) | copy-start | bytes 786436
  32.4 0.9 copy-start.7
  50.9 5.3 %collective-permute-start.10 = (f32[2,2,136,128]{3,2,1,0:T(8,128)S(1)}, f32[2,2,136,128]{3,2,1,0:T(8,128)S(1)}, u32[]{:S(2)}, u32[]{:S(2)}) collective-permute-start(f32[2,2,136,128]{3,2,1,0:T(8,128)S(1)} %get-tuple-element.70), channel_id=1, source_target_pairs={{0,8},{8,0},{16,24},{24,16},{32,40},{40,32},{48,56},{56,48},{64,72... | collective-permute-start | bytes 835592 | tf_op jit(solution)/shard_map/ppermute | solution.py:55
  56.2 3.4 %collective-permute-start.14 = (f32[2,2,136,128]{3,2,1,0:T(8,128)S(1)}, f32[2,2,136,128]{3,2,1,0:T(8,128)S(1)}, u32[]{:S(2)}, u32[]{:S(2)}) collective-permute-start(f32[2,2,136,128]{3,2,1,0:T(8,128)S(1)} %get-tuple-element.74), channel_id=1, source_target_pairs={{0,8},{8,0},{16,24},{24,16},{32,40},{40,32},{48,56},{56,48},{64,72... | collective-permute-start | bytes 835592 | tf_op jit(solution)/shard_map/ppermute | solution.py:55
  56.2 5.7 %collective-permute-start.11 = (f32[2,136,128]{2,1,0:T(8,128)S(1)}, f32[2,136,128]{2,1,0:T(8,128)S(1)}, u32[]{:S(2)}, u32[]{:S(2)}) collective-permute-start(f32[2,136,128]{2,1,0:T(8,128)S(1)} %get-tuple-element.72), channel_id=1, source_target_pairs={{0,192},{8,200},{16,208},{24,216},{32,224},{40,232},{48,240},{56,2... | collective-permute-start | bytes 417800 | tf_op jit(solution)/shard_map/ppermute | solution.py:55
  58.7 6.0 %collective-permute-start.12 = (f32[2,136,128]{2,1,0:T(8,128)S(1)}, f32[2,136,128]{2,1,0:T(8,128)S(1)}, u32[]{:S(2)}, u32[]{:S(2)}) collective-permute-start(f32[2,136,128]{2,1,0:T(8,128)S(1)} %get-tuple-element.71.own_ref), channel_id=1, source_target_pairs={{0,128},{8,136},{16,144},{24,152},{32,160},{40,168},{48,176},{56,1... | collective-permute-start | bytes 417800 | tf_op jit(solution)/shard_map/ppermute | solution.py:55
  59.2 9.6 %collective-permute-start.13 = (f32[2,136,128]{2,1,0:T(8,128)S(1)}, f32[2,136,128]{2,1,0:T(8,128)S(1)}, u32[]{:S(2)}, u32[]{:S(2)}) collective-permute-start(f32[2,136,128]{2,1,0:T(8,128)S(1)} %get-tuple-element.71.own_ref), channel_id=1, source_target_pairs={{0,64},{8,72},{16,80},{24,88},{32,96},{40,104},{48,112},{56,120},{... | collective-permute-start | bytes 417800 | tf_op jit(solution)/shard_map/ppermute | solution.py:55
  68.9 6.2 %collective-permute-start.15 = (f32[2,136,128]{2,1,0:T(8,128)S(1)}, f32[2,136,128]{2,1,0:T(8,128)S(1)}, u32[]{:S(2)}, u32[]{:S(2)}) collective-permute-start(f32[2,136,128]{2,1,0:T(8,128)S(1)} %get-tuple-element.77), channel_id=1, source_target_pairs={{0,48},{8,56},{16,0},{24,8},{32,16},{40,24},{48,32},{56,40},{64,11... | collective-permute-start | bytes 417800 | tf_op jit(solution)/shard_map/ppermute | solution.py:55
  70.9 6.0 %collective-permute-start.16 = (f32[2,136,128]{2,1,0:T(8,128)S(1)}, f32[2,136,128]{2,1,0:T(8,128)S(1)}, u32[]{:S(2)}, u32[]{:S(2)}) collective-permute-start(f32[2,136,128]{2,1,0:T(8,128)S(1)} %get-tuple-element.78), channel_id=1, source_target_pairs={{0,32},{8,40},{16,48},{24,56},{32,0},{40,8},{48,16},{56,24},{64,96... | collective-permute-start | bytes 417800 | tf_op jit(solution)/shard_map/ppermute | solution.py:55
  71.7 9.3 %collective-permute-start.17 = (f32[2,136,128]{2,1,0:T(8,128)S(1)}, f32[2,136,128]{2,1,0:T(8,128)S(1)}, u32[]{:S(2)}, u32[]{:S(2)}) collective-permute-start(f32[2,136,128]{2,1,0:T(8,128)S(1)} %get-tuple-element.79), channel_id=1, source_target_pairs={{0,16},{8,24},{16,32},{24,40},{32,48},{40,56},{48,0},{56,8},{64,80... | collective-permute-start | bytes 417800 | tf_op jit(solution)/shard_map/ppermute | solution.py:55
  71.9 14.3 %collective-permute-start.19 = (f32[4,128,128]{2,1,0:T(8,128)S(1)}, f32[4,128,128]{2,1,0:T(8,128)S(1)}, u32[]{:S(2)}, u32[]{:S(2)}) collective-permute-start(f32[4,128,128]{2,1,0:T(8,128)S(1)} %get-tuple-element.81), channel_id=1, source_target_pairs={{8,0},{24,16},{40,32},{56,48},{72,64},{88,80},{104,96},{120,112},{... | collective-permute-start | bytes 786440 | tf_op jit(solution)/shard_map/ppermute | solution.py:55
  81.6 4.5 %collective-permute-start.18 = (f32[2,128,128]{2,1,0:T(8,128)S(1)}, f32[2,128,128]{2,1,0:T(8,128)S(1)}, u32[]{:S(2)}, u32[]{:S(2)}) collective-permute-start(f32[2,128,128]{2,1,0:T(8,128)S(1)} %get-tuple-element.80.half_ref), channel_id=1, source_target_pairs={{0,8},{8,0},{16,24},{24,16},{32,40},{40,32},{48,56},{56,48},{64,72... | collective-permute-start | bytes 393224 | tf_op jit(solution)/shard_map/ppermute | solution.py:55
where the time goes:
time: 87.7 us; the launch traced here: 87.4 us
  starting transfers between devices  29.4 us (34%)
  waiting for transfers between devices  25.1 us (29%)
  Pallas kernels  15.3 us (17%)
  blocking collectives  14.3 us (16%)
  local copies, waits for them, and re-layouts  2.61 us (3%)
    ppermute x20, starting transfers between devices, send(): return lax.ppermute(array, 'seq', pairs)  29.4 us
    ppermute x20, waiting for transfers between devices, send(): return lax.ppermute(array, 'seq', pairs)  25.1 us
    pallas_call x13, Pallas kernels, call(): pl.pallas_call(kernel, out_shape=shapes, in_specs=[pl.BlockSpec(memory_sp...  15.3 us
    all_to_all x1, blocking collectives, layer(): sums = lax.all_to_all(pay, 'head', 0, 0, tiled=True)  14.3 us
    unnamed x20, local copies, waits for them, and re-layouts  2.61 us
  transfers between devices with their start and end apart: 20, of which 12 were waited for; matrix products, arithmetic and copies ran while one was open for 0% of the time, Pallas kernels for 10%

commit v1 on v0

--- a/solution.py
+++ b/solution.py
@@ -43,6 +43,14 @@
 DOWN = ring(lambda x, y, core: (x, y, 0) if core == 1 else None)
 
 
+Z_STEPS = (((0, 1), (2, 3), (4, 5), (6, 7)), ((1, 2), (3, 4), (5, 6), (7, 0)), ((0, 3), (1, 6), (2, 5), (4, 7)))
+
+
+def along_z(array, step):
+    pairs = [pair for a, b in Z_STEPS[step] for pair in ((a, b), (b, a))]
+    return lax.ppermute(array, "head", pairs)
+
+
 def along_y(step):
     return ring(lambda x, y, core: (x, (y + step) % 4, core))
 
@@ -77,16 +85,19 @@
     return lax.broadcasted_iota(jnp.int32, shape, 0), lax.broadcasted_iota(jnp.int32, shape, 1)
 
 
-def state_kernel(decay_ref, k_hbm, v_hbm, keep_ref, send_ref, run_ref, k_ref, v_ref, rows_ref, sems):
+def state_kernel(
+    decay_hbm, k_hbm, v_hbm, keep_ref, send_ref, run_ref, decay_ref, k_ref, v_ref, rows_ref, sems
+):
     copies = [
         pltpu.make_async_copy(source, to, sems.at[i])
-        for i, (source, to) in enumerate(((v_hbm, v_ref), (k_hbm, k_ref)))
+        for i, (source, to) in enumerate(((decay_hbm, decay_ref), (v_hbm, v_ref), (k_hbm, k_ref)))
     ]
     for copy in copies:
         copy.start()
     core = place()[2]
     early, late = iotas((WIDTH, WIDTH))
     upper = (early <= late).astype(F32).astype(BF16)
+    copies[0].wait()
     decay = decay_ref[...]
     first = decay.astype(BF16).astype(F32)
     second = (decay - first).astype(BF16).astype(F32)
@@ -99,7 +110,7 @@
     run_ref[...] = running
     rows_ref[0:4, :] = jnp.exp(running[:, WIDTH - 1 :] - running)
     tails = jnp.transpose(rows_ref[...])
-    for copy in copies:
+    for copy in copies[1:]:
         copy.wait()
     for head in range(LOCAL):
         weighted = v_ref[head].astype(F32) * tails[:, head : head + 1]
@@ -244,20 +255,26 @@
         scaled = grad_ref[head].astype(F32) * gain_ref[head : head + 1, :]
         squares = squares + dot(ones, (gated * gated).astype(BF16), NT)
         crosses = crosses + dot(ones, (gated * scaled).astype(BF16), NT)
-    for peer in range(8):
-        for half in range(2):
-            piece = slice(HEAD_DIM * half, HEAD_DIM * (half + 1))
-            pay_ref[peer, half : half + 1, :] = squares[0:1, piece]
-            pay_ref[peer, 2 + half : 3 + half, :] = crosses[0:1, piece]
+    for half in range(2):
+        piece = slice(HEAD_DIM * half, HEAD_DIM * (half + 1))
+        pay_ref[half : half + 1, :] = squares[0:1, piece]
+        pay_ref[2 + half : 3 + half, :] = crosses[0:1, piece]
+    pay_ref[4:8, :] = jnp.zeros((4, HEAD_DIM), F32)
+
+
+def add_kernel(a_ref, b_ref, out_ref):
+    out_ref[...] = a_ref[...] + b_ref[...]
 
 
 def gate_kernel(
-    q_ref, mixed_ref, gate_ref, grad_ref, gain_ref, cols_ref, shift_ref, sums_ref,
+    q_ref, mixed_ref, gate_ref, grad_ref, gain_ref, cols_ref, shift_ref, sums_ref, other_ref,
     g_ref, scale_ref, keep_ref, send_ref,
 ):
     x, _, core = place()
     ones = jnp.ones((8, HEAD_DIM), F32)
-    wide = [dot(sums_ref[:, i, :], ones, TN, HIGH) for i in range(4)]
+    sums = sums_ref[...] + other_ref[...]
+    row = iotas((8, HEAD_DIM))[0]
+    wide = [dot(jnp.where(row == i, sums, 0.0), ones, TN, HIGH) for i in range(4)]
     squares = jnp.concatenate(wide[0:2], axis=0)
     crosses = jnp.concatenate(wide[2:4], axis=0)
     inverse = lax.rsqrt(squares * (1.0 / TOTAL) + EPSILON)
@@ -405,19 +422,21 @@
         grad_q_ref[head] = grad_q.astype(BF16)
 
 
-def join_kernel(own_ref, one_ref, two_ref, three_ref, half_ref, gain_ref):
+def join_kernel(own_ref, one_ref, two_ref, three_ref, half_ref, sum_ref):
     y = place()[1]
     refs = (own_ref, one_ref, two_ref, three_ref)
     where = [lax.rem(y + step, 4) for step in range(4)]
     tails = [ref[0, HEAD_DIM : HEAD_DIM + LOCAL, :] for ref in refs]
     by_y = [sum(flag(where[i] == j) * tails[i] for i in range(4)) for j in range(4)]
-    gain_ref[...] = ((by_y[0] + by_y[1]) + by_y[2]) + by_y[3]
+    sum_ref[...] = ((by_y[0] + by_y[1]) + by_y[2]) + by_y[3]
     half_ref[...] = sum(ref[:, 0:HEAD_DIM, :] for ref in refs)
 
 
 def final_kernel(
-    k_ref, v_ref, cols_ref, half_ref, other_ref, zeroth_ref, first_ref, grad_k_ref, grad_v_ref, out_k_ref, out_v_ref
-):
+    k_ref, v_ref, cols_ref, half_ref, other_ref, zeroth_ref, first_ref, grad_k_ref, grad_v_ref, sum_ref,
+    out_k_ref, out_v_ref, gain_ref,
+):
+    gain_ref[...] = sum_ref[...]
     core = place()[2]
     even = core == 0
     for head in range(LOCAL):
@@ -458,9 +477,12 @@
     keep, away, running = call(
         state_kernel,
         [message, message, ((LOCAL, WIDTH), F32)],
-        log_decay, keys, values,
-        scratch=[pltpu.VMEM(tokens, BF16), pltpu.VMEM(tokens, BF16), pltpu.VMEM((16, WIDTH), F32), pltpu.SemaphoreType.DMA((2,))],
-        hbm=(1, 2),
+        *(pltpu.with_memory_space_constraint(a, pltpu.HBM) for a in (log_decay, keys, values)),
+        scratch=[
+            pltpu.VMEM((LOCAL, WIDTH), F32), pltpu.VMEM(tokens, BF16), pltpu.VMEM(tokens, BF16),
+            pltpu.VMEM((16, WIDTH), F32), pltpu.SemaphoreType.DMA((3,)),
+        ],
+        hbm=(0, 1, 2),
     )
     first = send(away, SWAP)
     (chip,) = call(pair_kernel, [message], keep, first)
@@ -481,14 +503,15 @@
     bucket_kind = ((LOCAL, HEAD_DIM, INTER * HEAD_DIM), BF16)
     mixed, pay, bucket, finer, shift = call(
         mixed_kernel,
-        [(tokens, F32), ((8, 4, HEAD_DIM), F32), bucket_kind, bucket_kind, ((LOCAL, 8, HEAD_DIM), F32)],
+        [(tokens, F32), ((8, HEAD_DIM), F32), bucket_kind, bucket_kind, ((LOCAL, 8, HEAD_DIM), F32)],
         queries, inner, gate_input, out_grad, norm_gain, cols, near, near_other, far, far_other, first, rest,
     )
-    sums = lax.all_to_all(pay, "head", 0, 0, tiled=True)
+    for step in range(2):
+        (pay,) = call(add_kernel, [((8, HEAD_DIM), F32)], pay, along_z(pay, step))
     grad_mixed, scale, far_keep, far_away = call(
         gate_kernel,
         [(tokens, BF16), ((2, WIDTH, HEAD_DIM), F32), double, double],
-        queries, mixed, gate_input, out_grad, norm_gain, cols, shift, sums,
+        queries, mixed, gate_input, out_grad, norm_gain, cols, shift, pay, along_z(pay, 2),
     )
     to_one, to_far = call(meet_kernel, [message] * 2, far_keep, send(far_away, SWAP))
     back_x = [send(to_one, along_x(-1)), send(to_far, along_x(-2)), send(to_far, along_x(-3))]
@@ -508,12 +531,12 @@
         queries, keys, values, grad_mixed, mixing, weight, scored, bucket, finer, cols, running,
         flops=10**9,
     )
-    half, grad_gain = call(join_kernel, [((2, HEAD_DIM, HEAD_DIM), F32), ((LOCAL, HEAD_DIM), F32)], *back_y)
+    half, gain_sum = call(join_kernel, [((2, HEAD_DIM, HEAD_DIM), F32), ((LOCAL, HEAD_DIM), F32)], *back_y)
     half_other = send(half, SWAP)
-    grad_keys, grad_values = call(
+    grad_keys, grad_values, grad_gain = call(
         final_kernel,
-        [(tokens, BF16)] * 2,
-        keys, values, cols, half, half_other, zeroth_back, first, grad_k, grad_v,
+        [(tokens, BF16)] * 2 + [((LOCAL, HEAD_DIM), F32)],
+        keys, values, cols, half, half_other, zeroth_back, first, grad_k, grad_v, gain_sum,
     )
     grad_levels = jnp.transpose(levels, (1, 0, 2))
     return (layer_out, grad_queries, grad_keys, grad_values, grad_levels, grad_gate, grad_gain)

time: 87.7 us -> 85.6 us (0.976)
  blocking collectives: 14.3 us -> 0 us
  starting transfers between devices: 29.4 us -> 39.5 us
  waiting for transfers between devices: 25.1 us -> 29.9 us
  local copies, waits for them, and re-layouts: 2.61 us -> 0.03 us
    all_to_all x1 -> x0, blocking collectives: 14.3 us -> none  [layer(): sums = lax.all_to_all(pay, 'head', 0, 0, tiled=True)]
    ppermute x0 -> x3, starting transfers between devices: none -> 8.15 us  [along_z(): return lax.ppermute(array, 'head', pairs)]
    ppermute x0 -> x3, waiting for transfers between devices: none -> 4.84 us  [along_z(): return lax.ppermute(array, 'head', pairs)]
    unnamed x20 -> x14, local copies, waits for them, and re-layouts: 2.61 us -> 0.03 us
    ppermute x20, starting transfers between devices: 29.4 us -> 31.3 us  [send(): return lax.ppermute(array, 'seq', pairs)]
    pallas_call x13 -> x15, Pallas kernels: 15.3 us -> 15.2 us  [call(): pl.pallas_call(kernel, out_shape=shapes, in_specs=[pl.BlockSpec(memory_sp...]
  transfers between devices with their start and end apart: 20 -> 23, of which waited for: 12 -> 15; matrix products, arithmetic and copies ran while one was open for 0% -> 0% of each run, Pallas kernels for 10% -> 9%
where the time goes in v1:
time: 85.6 us; the launch traced here: 85.4 us
  starting transfers between devices  39.5 us (46%)
  waiting for transfers between devices  29.9 us (35%)
  Pallas kernels  15.2 us (18%)
    ppermute x20, starting transfers between devices, send(): return lax.ppermute(array, 'seq', pairs)  31.3 us
    ppermute x20, waiting for transfers between devices, send(): return lax.ppermute(array, 'seq', pairs)  25.1 us
    pallas_call x15, Pallas kernels, call(): pl.pallas_call(kernel, out_shape=shapes, in_specs=[pl.BlockSpec(memory_sp...  15.2 us
    ppermute x3, starting transfers between devices, along_z(): return lax.ppermute(array, 'head', pairs)  8.15 us
    ppermute x3, waiting for transfers between devices, along_z(): return lax.ppermute(array, 'head', pairs)  4.84 us
  transfers between devices with their start and end apart: 23, of which 15 were waited for; matrix products, arithmetic and copies ran while one was open for 0% of the time, Pallas kernels for 9%

profile of v1, /device:TPU:1, one launch (start us, length us, event | category | flops | bytes accessed | tf_op | source)
XLA Modules:
  0.0 85.4 jit_solution(10090813943673148825)
XLA Ops:
  0.6 2.4 %shard_map.135 = (f32[2,136,128]{2,1,0:T(8,128)S(1)}, f32[2,136,128]{2,1,0:T(8,128)S(1)}, f32[4,256]{1,0:T(4,128)S(1)}) custom-call(f32[4,256]{1,0:T(4,128)} %decay_hbm.1, bf16[4,256,128]{2,1,0:T(8,128)(2,1)} %k_ref.5, bf16[4,256,128]{2,1,0:T(8,128)(2,1)} %v_ref.5), custom_call_target="tpu_custom_call" | custom-call | bytes 811008 | tf_op jit(solution)/shard_map/pallas_call | solution.py:458
  3.0 3.3 %collective-permute-start = (f32[2,136,128]{2,1,0:T(8,128)S(1)}, f32[2,136,128]{2,1,0:T(8,128)S(1)}, u32[]{:S(2)}, u32[]{:S(2)}) collective-permute-start(f32[2,136,128]{2,1,0:T(8,128)S(1)} %get-tuple-element.53), channel_id=1, source_target_pairs={{0,8},{8,0},{16,24},{24,16},{32,40},{40,32},{48,56},{56,48},{64,72... | collective-permute-start | bytes 417800 | tf_op jit(solution)/shard_map/ppermute | solution.py:63
  7.5 2.2 %collective-permute-start.2 = (f32[2,136,128]{2,1,0:T(8,128)S(1)}, f32[2,136,128]{2,1,0:T(8,128)S(1)}, u32[]{:S(2)}, u32[]{:S(2)}) collective-permute-start(f32[2,136,128]{2,1,0:T(8,128)S(1)} %shard_map.137.own_ref), channel_id=1, source_target_pairs={{0,32},{8,40},{16,48},{24,56},{32,0},{40,8},{48,16},{56,24},{64,96... | collective-permute-start | bytes 417800 | tf_op jit(solution)/shard_map/ppermute | solution.py:63
  9.7 1.1 %collective-permute-start.3 = (f32[2,136,128]{2,1,0:T(8,128)S(1)}, f32[2,136,128]{2,1,0:T(8,128)S(1)}, u32[]{:S(2)}, u32[]{:S(2)}) collective-permute-start(f32[2,136,128]{2,1,0:T(8,128)S(1)} %shard_map.137.own_ref), channel_id=1, source_target_pairs={{0,48},{8,56},{16,0},{24,8},{32,16},{40,24},{48,32},{56,40},{64,11... | collective-permute-start | bytes 417800 | tf_op jit(solution)/shard_map/ppermute | solution.py:63
  10.7 3.3 %collective-permute-done.1.one_ref = f32[2,136,128]{2,1,0:T(8,128)S(1)} collective-permute-done((f32[2,136,128]{2,1,0:T(8,128)S(1)}, f32[2,136,128]{2,1,0:T(8,128)S(1)}, u32[]{:S(2)}, u32[]{:S(2)}) %collective-permute-start.1) | collective-permute-done | bytes 139296 | tf_op jit(solution)/shard_map/ppermute | solution.py:63
  14.0 2.1 %collective-permute-done.2.two_ref = f32[2,136,128]{2,1,0:T(8,128)S(1)} collective-permute-done((f32[2,136,128]{2,1,0:T(8,128)S(1)}, f32[2,136,128]{2,1,0:T(8,128)S(1)}, u32[]{:S(2)}, u32[]{:S(2)}) %collective-permute-start.2) | collective-permute-done | bytes 139296 | tf_op jit(solution)/shard_map/ppermute | solution.py:63
  17.5 2.4 %collective-permute-start.6 = (f32[2,136,128]{2,1,0:T(8,128)S(1)}, f32[2,136,128]{2,1,0:T(8,128)S(1)}, u32[]{:S(2)}, u32[]{:S(2)}) collective-permute-start(f32[2,136,128]{2,1,0:T(8,128)S(1)} %get-tuple-element.55.own_ref), channel_id=1, source_target_pairs={{0,128},{8,136},{16,144},{24,152},{32,160},{40,168},{48,176},{56,1... | collective-permute-start | bytes 417800 | tf_op jit(solution)/shard_map/ppermute | solution.py:63
  19.9 1.2 %collective-permute-start.7 = (f32[2,136,128]{2,1,0:T(8,128)S(1)}, f32[2,136,128]{2,1,0:T(8,128)S(1)}, u32[]{:S(2)}, u32[]{:S(2)}) collective-permute-start(f32[2,136,128]{2,1,0:T(8,128)S(1)} %get-tuple-element.55.own_ref), channel_id=1, source_target_pairs={{0,192},{8,200},{16,208},{24,216},{32,224},{40,232},{48,240},{56,2... | collective-permute-start | bytes 417800 | tf_op jit(solution)/shard_map/ppermute | solution.py:63
  21.1 2.1 %collective-permute-start.4 = (f32[2,2,136,128]{3,2,1,0:T(8,128)S(1)}, f32[2,2,136,128]{3,2,1,0:T(8,128)S(1)}, u32[]{:S(2)}, u32[]{:S(2)}) collective-permute-start(f32[2,2,136,128]{3,2,1,0:T(8,128)S(1)} %get-tuple-element.54.near_ref), channel_id=1, source_target_pairs={{0,8},{8,0},{16,24},{24,16},{32,40},{40,32},{48,56},{56,48},{64,72... | collective-permute-start | bytes 835592 | tf_op jit(solution)/shard_map/ppermute | solution.py:63
  23.1 2.0 %collective-permute-done.6.two_ref = f32[2,136,128]{2,1,0:T(8,128)S(1)} collective-permute-done((f32[2,136,128]{2,1,0:T(8,128)S(1)}, f32[2,136,128]{2,1,0:T(8,128)S(1)}, u32[]{:S(2)}, u32[]{:S(2)}) %collective-permute-start.6) | collective-permute-done | bytes 139296 | tf_op jit(solution)/shard_map/ppermute | solution.py:63
  25.3 2.7 %collective-permute-start.8 = (f32[2,2,136,128]{3,2,1,0:T(8,128)S(1)}, f32[2,2,136,128]{3,2,1,0:T(8,128)S(1)}, u32[]{:S(2)}, u32[]{:S(2)}) collective-permute-start(f32[2,2,136,128]{3,2,1,0:T(8,128)S(1)} %get-tuple-element.57.far_ref), channel_id=1, source_target_pairs={{0,8},{8,0},{16,24},{24,16},{32,40},{40,32},{48,56},{56,48},{64,72... | collective-permute-start | bytes 835592 | tf_op jit(solution)/shard_map/ppermute | solution.py:63
  28.0 1.3 %collective-permute-start.9 = (f32[2,136,128]{2,1,0:T(8,128)S(1)}, f32[2,136,128]{2,1,0:T(8,128)S(1)}, u32[]{:S(2)}, u32[]{:S(2)}) collective-permute-start(f32[2,136,128]{2,1,0:T(8,128)S(1)} %get-tuple-element.52.keep_ref), channel_id=1, source_target_pairs={{0,8},{16,24},{32,40},{48,56},{64,72},{80,88},{96,104},{112,120},{... | collective-permute-start | bytes 417800 | tf_op jit(solution)/shard_map/ppermute | solution.py:63
  29.4 1.1 %shard_map.136 = (f32[4,256,128]{2,1,0:T(8,128)S(1)}, bf16[4,256,256]{2,1,0:T(8,128)(2,1)S(1)}, f32[4,256,256]{2,1,0:T(8,128)S(1)}, f32[4,256,256]{2,1,0:T(8,128)S(1)}, f32[256,128]{1,0:T(8,128)S(1)}) custom-call(bf16[4,256,128]{2,1,0:T(8,128)(2,1)S(1)} %copy-done, bf16[4,256,128]{2,1,0:T(8,128)(2,1)S(1)} %copy-done.1, bf16[4,256,128]{2,1,0:T(8,128)(2,1)S(1)} %copy-done.2, ...), custom_call_target="tpu_custom_call" | custom-call | flops 1000000000 | bytes 4153344 | tf_op jit(solution)/shard_map/pallas_call | solution.py:458
  31.3 1.6 %shard_map.140 = (f32[4,256,128]{2,1,0:T(8,128)S(1)}, f32[8,128]{1,0:T(8,128)S(1)}, bf16[4,128,640]{2,1,0:T(8,128)(2,1)S(1)}, bf16[4,128,640]{2,1,0:T(8,128)(2,1)S(1)}, f32[4,8,128]{2,1,0:T(8,128)S(1)}) custom-call(bf16[4,256,128]{2,1,0:T(8,128)(2,1)S(1)} %copy-done, f32[4,256,128]{2,1,0:T(8,128)S(1)} %get-tuple-element.50.inner_ref, ...), custom_call_target="tpu_custom_call" | custom-call | bytes 4691968 | tf_op jit(solution)/shard_map/pallas_call | solution.py:458
  33.0 1.3 %collective-permute-start.10 = (f32[8,128]{1,0:T(8,128)S(1)}, f32[8,128]{1,0:T(8,128)S(1)}, u32[]{:S(2)}, u32[]{:S(2)}) collective-permute-start(f32[8,128]{1,0:T(8,128)S(1)} %get-tuple-element.60.a_ref), channel_id=1, source_target_pairs={{0,1},{1,0},{2,3},{3,2},{4,5},{5,4},{6,7},{7,6},{8,9},{9,8},{10,11... | collective-permute-start | bytes 12296 | tf_op jit(solution)/shard_map/ppermute | solution.py:51
  34.3 1.2 %collective-permute-done.10.b_ref = f32[8,128]{1,0:T(8,128)S(1)} collective-permute-done((f32[8,128]{1,0:T(8,128)S(1)}, f32[8,128]{1,0:T(8,128)S(1)}, u32[]{:S(2)}, u32[]{:S(2)}) %collective-permute-start.10) | collective-permute-done | bytes 4128 | tf_op jit(solution)/shard_map/ppermute | solution.py:51
  35.4 5.2 %collective-permute-start.11 = (f32[8,128]{1,0:T(8,128)S(1)}, f32[8,128]{1,0:T(8,128)S(1)}, u32[]{:S(2)}, u32[]{:S(2)}) collective-permute-start(f32[8,128]{1,0:T(8,128)S(1)} %shard_map.141.a_ref), channel_id=1, source_target_pairs={{1,2},{2,1},{3,4},{4,3},{5,6},{6,5},{7,0},{0,7},{9,10},{10,9},{11,... | collective-permute-start | bytes 12296 | tf_op jit(solution)/shard_map/ppermute | solution.py:51
  41.7 1.6 %collective-permute-start.12 = (f32[8,128]{1,0:T(8,128)S(1)}, f32[8,128]{1,0:T(8,128)S(1)}, u32[]{:S(2)}, u32[]{:S(2)}) collective-permute-start(f32[8,128]{1,0:T(8,128)S(1)} %shard_map.142.sums_ref), channel_id=1, source_target_pairs={{0,3},{3,0},{1,6},{6,1},{2,5},{5,2},{4,7},{7,4},{8,11},{11,8},{9,1... | collective-permute-start | bytes 12296 | tf_op jit(solution)/shard_map/ppermute | solution.py:51
  43.3 2.7 %collective-permute-done.12.other_ref = f32[8,128]{1,0:T(8,128)S(1)} collective-permute-done((f32[8,128]{1,0:T(8,128)S(1)}, f32[8,128]{1,0:T(8,128)S(1)}, u32[]{:S(2)}, u32[]{:S(2)}) %collective-permute-start.12) | collective-permute-done | bytes 4128 | tf_op jit(solution)/shard_map/ppermute | solution.py:51
  46.0 1.7 %shard_map.143 = (bf16[4,256,128]{2,1,0:T(8,128)(2,1)S(1)}, f32[2,256,128]{2,1,0:T(8,128)S(1)}, f32[2,2,136,128]{3,2,1,0:T(8,128)S(1)}, f32[2,2,136,128]{3,2,1,0:T(8,128)S(1)}) custom-call(bf16[4,256,128]{2,1,0:T(8,128)(2,1)S(1)} %copy-done, f32[4,256,128]{2,1,0:T(8,128)S(1)} %get-tuple-element.58.mixed_ref, bf16[4,256,128]{2,1,0:T(8,128)(2,1)S(1)} %copy-done.3, ...), custom_call_target="tpu_custom_call" | custom-call | bytes 2549760 | tf_op jit(solution)/shard_map/pallas_call | solution.py:458
  47.6 4.3 %collective-permute-start.13 = (f32[2,2,136,128]{3,2,1,0:T(8,128)S(1)}, f32[2,2,136,128]{3,2,1,0:T(8,128)S(1)}, u32[]{:S(2)}, u32[]{:S(2)}) collective-permute-start(f32[2,2,136,128]{3,2,1,0:T(8,128)S(1)} %get-tuple-element.71), channel_id=1, source_target_pairs={{0,8},{8,0},{16,24},{24,16},{32,40},{40,32},{48,56},{56,48},{64,72... | collective-permute-start | bytes 835592 | tf_op jit(solution)/shard_map/ppermute | solution.py:63
  52.0 2.7 %shard_map.144 = (bf16[4,256,128]{2,1,0:T(8,128)(2,1)}, bf16[4,256,128]{2,1,0:T(8,128)(2,1)}, f32[2,2,136,128]{3,2,1,0:T(8,128)S(1)}, f32[2,2,136,128]{3,2,1,0:T(8,128)S(1)}, f32[4,128,128]{2,1,0:T(8,128)S(1)}) custom-call(bf16[4,256,128]{2,1,0:T(8,128)(2,1)S(1)} %copy-done, bf16[4,256,128]{2,1,0:T(8,128)(2,1)S(1)} %get-tuple-element.61.g_ref, ...), custom_call_target="tpu_custom_call" | custom-call | flops 1000000000 | bytes 3328000 | tf_op jit(solution)/shard_map/pallas_call | solution.py:458
  54.7 2.4 %collective-permute-start.14 = (f32[2,136,128]{2,1,0:T(8,128)S(1)}, f32[2,136,128]{2,1,0:T(8,128)S(1)}, u32[]{:S(2)}, u32[]{:S(2)}) collective-permute-start(f32[2,136,128]{2,1,0:T(8,128)S(1)} %get-tuple-element.73), channel_id=1, source_target_pairs={{0,192},{8,200},{16,208},{24,216},{32,224},{40,232},{48,240},{56,2... | collective-permute-start | bytes 417800 | tf_op jit(solution)/shard_map/ppermute | solution.py:63
  58.1 2.3 %collective-permute-done.14.one_ref = f32[2,136,128]{2,1,0:T(8,128)S(1)} collective-permute-done((f32[2,136,128]{2,1,0:T(8,128)S(1)}, f32[2,136,128]{2,1,0:T(8,128)S(1)}, u32[]{:S(2)}, u32[]{:S(2)}) %collective-permute-start.14) | collective-permute-done | bytes 139296 | tf_op jit(solution)/shard_map/ppermute | solution.py:63
  60.4 2.7 %collective-permute-done.15.two_ref = f32[2,136,128]{2,1,0:T(8,128)S(1)} collective-permute-done((f32[2,136,128]{2,1,0:T(8,128)S(1)}, f32[2,136,128]{2,1,0:T(8,128)S(1)}, u32[]{:S(2)}, u32[]{:S(2)}) %collective-permute-start.15) | collective-permute-done | bytes 139296 | tf_op jit(solution)/shard_map/ppermute | solution.py:63
  63.1 4.1 %collective-permute-done.16.three_ref = f32[2,136,128]{2,1,0:T(8,128)S(1)} collective-permute-done((f32[2,136,128]{2,1,0:T(8,128)S(1)}, f32[2,136,128]{2,1,0:T(8,128)S(1)}, u32[]{:S(2)}, u32[]{:S(2)}) %collective-permute-start.16) | collective-permute-done | bytes 139296 | tf_op jit(solution)/shard_map/ppermute | solution.py:63
  67.4 2.1 %collective-permute-start.18 = (f32[2,136,128]{2,1,0:T(8,128)S(1)}, f32[2,136,128]{2,1,0:T(8,128)S(1)}, u32[]{:S(2)}, u32[]{:S(2)}) collective-permute-start(f32[2,136,128]{2,1,0:T(8,128)S(1)} %get-tuple-element.78), channel_id=1, source_target_pairs={{0,48},{8,56},{16,0},{24,8},{32,16},{40,24},{48,32},{56,40},{64,11... | collective-permute-start | bytes 417800 | tf_op jit(solution)/shard_map/ppermute | solution.py:63
  70.3 3.2 %collective-permute-start.22 = (f32[4,128,128]{2,1,0:T(8,128)S(1)}, f32[4,128,128]{2,1,0:T(8,128)S(1)}, u32[]{:S(2)}, u32[]{:S(2)}) collective-permute-start(f32[4,128,128]{2,1,0:T(8,128)S(1)} %get-tuple-element.82), channel_id=1, source_target_pairs={{8,0},{24,16},{40,32},{56,48},{72,64},{88,80},{104,96},{120,112},{... | collective-permute-start | bytes 786440 | tf_op jit(solution)/shard_map/ppermute | solution.py:63
  73.6 1.8 %collective-permute-done.19.two_ref = f32[2,136,128]{2,1,0:T(8,128)S(1)} collective-permute-done((f32[2,136,128]{2,1,0:T(8,128)S(1)}, f32[2,136,128]{2,1,0:T(8,128)S(1)}, u32[]{:S(2)}, u32[]{:S(2)}) %collective-permute-start.19) | collective-permute-done | bytes 139296 | tf_op jit(solution)/shard_map/ppermute | solution.py:63
  75.4 4.1 %collective-permute-done.20.three_ref = f32[2,136,128]{2,1,0:T(8,128)S(1)} collective-permute-done((f32[2,136,128]{2,1,0:T(8,128)S(1)}, f32[2,136,128]{2,1,0:T(8,128)S(1)}, u32[]{:S(2)}, u32[]{:S(2)}) %collective-permute-start.20) | collective-permute-done | bytes 139296 | tf_op jit(solution)/shard_map/ppermute | solution.py:63
  80.2 4.0 %shard_map.145 = (bf16[4,256,128]{2,1,0:T(8,128)(2,1)}, f32[4,256,128]{2,1,0:T(8,128)S(1)}, f32[4,256,128]{2,1,0:T(8,128)S(1)}, f32[21,4,256]{2,1,0:T(4,128)}) custom-call(bf16[4,256,128]{2,1,0:T(8,128)(2,1)S(1)} %copy-done, bf16[4,256,128]{2,1,0:T(8,128)(2,1)S(1)} %copy-done.1, bf16[4,256,128]{2,1,0:T(8,128)(2,1)S(1)} %copy-done.2, ...), custom_call_target="tpu_custom_call" | custom-call | flops 1000000000 | bytes 6512640 | tf_op jit(solution)/shard_map/pallas_call | solution.py:458
  84.2 1.3 %shard_map.149 = (bf16[4,256,128]{2,1,0:T(8,128)(2,1)}, bf16[4,256,128]{2,1,0:T(8,128)(2,1)}, f32[4,128]{1,0:T(4,128)}) custom-call(bf16[4,256,128]{2,1,0:T(8,128)(2,1)S(1)} %copy-done.1, bf16[4,256,128]{2,1,0:T(8,128)(2,1)S(1)} %copy-done.2, f32[256,128]{1,0:T(8,128)S(1)} %get-tuple-element.51.cols_ref, f32[2,128,128]{2,1,0:T(8,128)S(1)} %get-tuple-element.81.half_ref, ...), custom_call_target="tpu_custom_call" | custom-call | bytes 2895872 | tf_op jit(solution)/shard_map/pallas_call | solution.py:458
  (43 shorter events, 7.2 us)
Async XLA Ops:
  3.0 4.3 %collective-permute-start = (f32[2,136,128]{2,1,0:T(8,128)S(1)}, f32[2,136,128]{2,1,0:T(8,128)S(1)}, u32[]{:S(2)}, u32[]{:S(2)}) collective-permute-start(f32[2,136,128]{2,1,0:T(8,128)S(1)} %get-tuple-element.53), channel_id=1, source_target_pairs={{0,8},{8,0},{16,24},{24,16},{32,40},{40,32},{48,56},{56,48},{64,72... | collective-permute-start | bytes 417800 | tf_op jit(solution)/shard_map/ppermute | solution.py:63
  7.4 6.6 %collective-permute-start.1 = (f32[2,136,128]{2,1,0:T(8,128)S(1)}, f32[2,136,128]{2,1,0:T(8,128)S(1)}, u32[]{:S(2)}, u32[]{:S(2)}) collective-permute-start(f32[2,136,128]{2,1,0:T(8,128)S(1)} %shard_map.137.own_ref), channel_id=1, source_target_pairs={{0,16},{8,24},{16,32},{24,40},{32,48},{40,56},{48,0},{56,8},{64,80... | collective-permute-start | bytes 417800 | tf_op jit(solution)/shard_map/ppermute | solution.py:63
  7.5 8.6 %collective-permute-start.2 = (f32[2,136,128]{2,1,0:T(8,128)S(1)}, f32[2,136,128]{2,1,0:T(8,128)S(1)}, u32[]{:S(2)}, u32[]{:S(2)}) collective-permute-start(f32[2,136,128]{2,1,0:T(8,128)S(1)} %shard_map.137.own_ref), channel_id=1, source_target_pairs={{0,32},{8,40},{16,48},{24,56},{32,0},{40,8},{48,16},{56,24},{64,96... | collective-permute-start | bytes 417800 | tf_op jit(solution)/shard_map/ppermute | solution.py:63
  9.7 7.2 %collective-permute-start.3 = (f32[2,136,128]{2,1,0:T(8,128)S(1)}, f32[2,136,128]{2,1,0:T(8,128)S(1)}, u32[]{:S(2)}, u32[]{:S(2)}) collective-permute-start(f32[2,136,128]{2,1,0:T(8,128)S(1)} %shard_map.137.own_ref), channel_id=1, source_target_pairs={{0,48},{8,56},{16,0},{24,8},{32,16},{40,24},{48,32},{56,40},{64,11... | collective-permute-start | bytes 417800 | tf_op jit(solution)/shard_map/ppermute | solution.py:63
  16.8 12.5 %copy-start.2 = (bf16[4,256,128]{2,1,0:T(8,128)(2,1)S(1)}, bf16[4,256,128]{2,1,0:T(8,128)(2,1)}, u32[]{:S(2)}) copy-start(bf16[4,256,128]{2,1,0:T(8,128)(2,1)} %v_ref.5) | copy-start | bytes 786436
  16.8 12.5 %copy-start.6 = (f32[4,21,256]{2,0,1:T(4,128)S(1)}, f32[4,21,256]{2,0,1:T(4,128)}, u32[]{:S(2)}) copy-start(f32[4,21,256]{2,0,1:T(4,128)} %param.12) | copy-start | bytes 258052
  16.9 6.2 %collective-permute-start.5 = (f32[2,136,128]{2,1,0:T(8,128)S(1)}, f32[2,136,128]{2,1,0:T(8,128)S(1)}, u32[]{:S(2)}, u32[]{:S(2)}) collective-permute-start(f32[2,136,128]{2,1,0:T(8,128)S(1)} %get-tuple-element.55.own_ref), channel_id=1, source_target_pairs={{0,64},{8,72},{16,80},{24,88},{32,96},{40,104},{48,112},{56,120},{... | collective-permute-start | bytes 417800 | tf_op jit(solution)/shard_map/ppermute | solution.py:63
  17.5 7.7 %collective-permute-start.6 = (f32[2,136,128]{2,1,0:T(8,128)S(1)}, f32[2,136,128]{2,1,0:T(8,128)S(1)}, u32[]{:S(2)}, u32[]{:S(2)}) collective-permute-start(f32[2,136,128]{2,1,0:T(8,128)S(1)} %get-tuple-element.55.own_ref), channel_id=1, source_target_pairs={{0,128},{8,136},{16,144},{24,152},{32,160},{40,168},{48,176},{56,1... | collective-permute-start | bytes 417800 | tf_op jit(solution)/shard_map/ppermute | solution.py:63
  19.9 5.3 %collective-permute-start.7 = (f32[2,136,128]{2,1,0:T(8,128)S(1)}, f32[2,136,128]{2,1,0:T(8,128)S(1)}, u32[]{:S(2)}, u32[]{:S(2)}) collective-permute-start(f32[2,136,128]{2,1,0:T(8,128)S(1)} %get-tuple-element.55.own_ref), channel_id=1, source_target_pairs={{0,192},{8,200},{16,208},{24,216},{32,224},{40,232},{48,240},{56,2... | collective-permute-start | bytes 417800 | tf_op jit(solution)/shard_map/ppermute | solution.py:63
  21.1 10.2 %collective-permute-start.4 = (f32[2,2,136,128]{3,2,1,0:T(8,128)S(1)}, f32[2,2,136,128]{3,2,1,0:T(8,128)S(1)}, u32[]{:S(2)}, u32[]{:S(2)}) collective-permute-start(f32[2,2,136,128]{3,2,1,0:T(8,128)S(1)} %get-tuple-element.54.near_ref), channel_id=1, source_target_pairs={{0,8},{8,0},{16,24},{24,16},{32,40},{40,32},{48,56},{56,48},{64,72... | collective-permute-start | bytes 835592 | tf_op jit(solution)/shard_map/ppermute | solution.py:63
  25.2 4.1 %copy-start = (bf16[4,256,128]{2,1,0:T(8,128)(2,1)S(1)}, bf16[4,256,128]{2,1,0:T(8,128)(2,1)}, u32[]{:S(2)}) copy-start(bf16[4,256,128]{2,1,0:T(8,128)(2,1)} %q_ref.9) | copy-start | bytes 786436
  25.2 4.1 %copy-start.1 = (bf16[4,256,128]{2,1,0:T(8,128)(2,1)S(1)}, bf16[4,256,128]{2,1,0:T(8,128)(2,1)}, u32[]{:S(2)}) copy-start(bf16[4,256,128]{2,1,0:T(8,128)(2,1)} %k_ref.5) | copy-start | bytes 786436
  25.3 6.0 %collective-permute-start.8 = (f32[2,2,136,128]{3,2,1,0:T(8,128)S(1)}, f32[2,2,136,128]{3,2,1,0:T(8,128)S(1)}, u32[]{:S(2)}, u32[]{:S(2)}) collective-permute-start(f32[2,2,136,128]{3,2,1,0:T(8,128)S(1)} %get-tuple-element.57.far_ref), channel_id=1, source_target_pairs={{0,8},{8,0},{16,24},{24,16},{32,40},{40,32},{48,56},{56,48},{64,72... | collective-permute-start | bytes 835592 | tf_op jit(solution)/shard_map/ppermute | solution.py:63
  28.0 3.2 %collective-permute-start.9 = (f32[2,136,128]{2,1,0:T(8,128)S(1)}, f32[2,136,128]{2,1,0:T(8,128)S(1)}, u32[]{:S(2)}, u32[]{:S(2)}) collective-permute-start(f32[2,136,128]{2,1,0:T(8,128)S(1)} %get-tuple-element.52.keep_ref), channel_id=1, source_target_pairs={{0,8},{16,24},{32,40},{48,56},{64,72},{80,88},{96,104},{112,120},{... | collective-permute-start | bytes 417800 | tf_op jit(solution)/shard_map/ppermute | solution.py:63
  29.4 1.9 %copy-start.3 = (bf16[4,256,128]{2,1,0:T(8,128)(2,1)S(1)}, bf16[4,256,128]{2,1,0:T(8,128)(2,1)}, u32[]{:S(2)}) copy-start(bf16[4,256,128]{2,1,0:T(8,128)(2,1)} %gate_ref.5) | copy-start | bytes 786436
  29.4 1.9 %copy-start.4 = (bf16[4,256,128]{2,1,0:T(8,128)(2,1)S(1)}, bf16[4,256,128]{2,1,0:T(8,128)(2,1)}, u32[]{:S(2)}) copy-start(bf16[4,256,128]{2,1,0:T(8,128)(2,1)} %grad_ref.5) | copy-start | bytes 786436
  30.4 0.9 %copy-start.5 = (f32[4,128]{1,0:T(4,128)S(1)}, f32[4,128]{1,0:T(4,128)}, u32[]{:S(2)}) copy-start(f32[4,128]{1,0:T(4,128)} %gain_ref.5) | copy-start | bytes 6148
  33.0 2.5 %collective-permute-start.10 = (f32[8,128]{1,0:T(8,128)S(1)}, f32[8,128]{1,0:T(8,128)S(1)}, u32[]{:S(2)}, u32[]{:S(2)}) collective-permute-start(f32[8,128]{1,0:T(8,128)S(1)} %get-tuple-element.60.a_ref), channel_id=1, source_target_pairs={{0,1},{1,0},{2,3},{3,2},{4,5},{5,4},{6,7},{7,6},{8,9},{9,8},{10,11... | collective-permute-start | bytes 12296 | tf_op jit(solution)/shard_map/ppermute | solution.py:51
  35.4 6.2 %collective-permute-start.11 = (f32[8,128]{1,0:T(8,128)S(1)}, f32[8,128]{1,0:T(8,128)S(1)}, u32[]{:S(2)}, u32[]{:S(2)}) collective-permute-start(f32[8,128]{1,0:T(8,128)S(1)} %shard_map.141.a_ref), channel_id=1, source_target_pairs={{1,2},{2,1},{3,4},{4,3},{5,6},{6,5},{7,0},{0,7},{9,10},{10,9},{11,... | collective-permute-start | bytes 12296 | tf_op jit(solution)/shard_map/ppermute | solution.py:51
  41.7 4.3 %collective-permute-start.12 = (f32[8,128]{1,0:T(8,128)S(1)}, f32[8,128]{1,0:T(8,128)S(1)}, u32[]{:S(2)}, u32[]{:S(2)}) collective-permute-start(f32[8,128]{1,0:T(8,128)S(1)} %shard_map.142.sums_ref), channel_id=1, source_target_pairs={{0,3},{3,0},{1,6},{6,1},{2,5},{5,2},{4,7},{7,4},{8,11},{11,8},{9,1... | collective-permute-start | bytes 12296 | tf_op jit(solution)/shard_map/ppermute | solution.py:51
  47.6 7.1 %collective-permute-start.13 = (f32[2,2,136,128]{3,2,1,0:T(8,128)S(1)}, f32[2,2,136,128]{3,2,1,0:T(8,128)S(1)}, u32[]{:S(2)}, u32[]{:S(2)}) collective-permute-start(f32[2,2,136,128]{3,2,1,0:T(8,128)S(1)} %get-tuple-element.71), channel_id=1, source_target_pairs={{0,8},{8,0},{16,24},{24,16},{32,40},{40,32},{48,56},{56,48},{64,72... | collective-permute-start | bytes 835592 | tf_op jit(solution)/shard_map/ppermute | solution.py:63
  54.7 3.4 %collective-permute-start.17 = (f32[2,2,136,128]{3,2,1,0:T(8,128)S(1)}, f32[2,2,136,128]{3,2,1,0:T(8,128)S(1)}, u32[]{:S(2)}, u32[]{:S(2)}) collective-permute-start(f32[2,2,136,128]{3,2,1,0:T(8,128)S(1)} %get-tuple-element.75), channel_id=1, source_target_pairs={{0,8},{8,0},{16,24},{24,16},{32,40},{40,32},{48,56},{56,48},{64,72... | collective-permute-start | bytes 835592 | tf_op jit(solution)/shard_map/ppermute | solution.py:63
  54.7 5.7 %collective-permute-start.14 = (f32[2,136,128]{2,1,0:T(8,128)S(1)}, f32[2,136,128]{2,1,0:T(8,128)S(1)}, u32[]{:S(2)}, u32[]{:S(2)}) collective-permute-start(f32[2,136,128]{2,1,0:T(8,128)S(1)} %get-tuple-element.73), channel_id=1, source_target_pairs={{0,192},{8,200},{16,208},{24,216},{32,224},{40,232},{48,240},{56,2... | collective-permute-start | bytes 417800 | tf_op jit(solution)/shard_map/ppermute | solution.py:63
  57.1 6.0 %collective-permute-start.15 = (f32[2,136,128]{2,1,0:T(8,128)S(1)}, f32[2,136,128]{2,1,0:T(8,128)S(1)}, u32[]{:S(2)}, u32[]{:S(2)}) collective-permute-start(f32[2,136,128]{2,1,0:T(8,128)S(1)} %get-tuple-element.72.own_ref), channel_id=1, source_target_pairs={{0,128},{8,136},{16,144},{24,152},{32,160},{40,168},{48,176},{56,1... | collective-permute-start | bytes 417800 | tf_op jit(solution)/shard_map/ppermute | solution.py:63
  57.7 9.6 %collective-permute-start.16 = (f32[2,136,128]{2,1,0:T(8,128)S(1)}, f32[2,136,128]{2,1,0:T(8,128)S(1)}, u32[]{:S(2)}, u32[]{:S(2)}) collective-permute-start(f32[2,136,128]{2,1,0:T(8,128)S(1)} %get-tuple-element.72.own_ref), channel_id=1, source_target_pairs={{0,64},{8,72},{16,80},{24,88},{32,96},{40,104},{48,112},{56,120},{... | collective-permute-start | bytes 417800 | tf_op jit(solution)/shard_map/ppermute | solution.py:63
  67.4 6.2 %collective-permute-start.18 = (f32[2,136,128]{2,1,0:T(8,128)S(1)}, f32[2,136,128]{2,1,0:T(8,128)S(1)}, u32[]{:S(2)}, u32[]{:S(2)}) collective-permute-start(f32[2,136,128]{2,1,0:T(8,128)S(1)} %get-tuple-element.78), channel_id=1, source_target_pairs={{0,48},{8,56},{16,0},{24,8},{32,16},{40,24},{48,32},{56,40},{64,11... | collective-permute-start | bytes 417800 | tf_op jit(solution)/shard_map/ppermute | solution.py:63
  69.4 6.0 %collective-permute-start.19 = (f32[2,136,128]{2,1,0:T(8,128)S(1)}, f32[2,136,128]{2,1,0:T(8,128)S(1)}, u32[]{:S(2)}, u32[]{:S(2)}) collective-permute-start(f32[2,136,128]{2,1,0:T(8,128)S(1)} %get-tuple-element.79), channel_id=1, source_target_pairs={{0,32},{8,40},{16,48},{24,56},{32,0},{40,8},{48,16},{56,24},{64,96... | collective-permute-start | bytes 417800 | tf_op jit(solution)/shard_map/ppermute | solution.py:63
  70.2 9.3 %collective-permute-start.20 = (f32[2,136,128]{2,1,0:T(8,128)S(1)}, f32[2,136,128]{2,1,0:T(8,128)S(1)}, u32[]{:S(2)}, u32[]{:S(2)}) collective-permute-start(f32[2,136,128]{2,1,0:T(8,128)S(1)} %get-tuple-element.80), channel_id=1, source_target_pairs={{0,16},{8,24},{16,32},{24,40},{32,48},{40,56},{48,0},{56,8},{64,80... | collective-permute-start | bytes 417800 | tf_op jit(solution)/shard_map/ppermute | solution.py:63
  70.3 13.8 %collective-permute-start.22 = (f32[4,128,128]{2,1,0:T(8,128)S(1)}, f32[4,128,128]{2,1,0:T(8,128)S(1)}, u32[]{:S(2)}, u32[]{:S(2)}) collective-permute-start(f32[4,128,128]{2,1,0:T(8,128)S(1)} %get-tuple-element.82), channel_id=1, source_target_pairs={{8,0},{24,16},{40,32},{56,48},{72,64},{88,80},{104,96},{120,112},{... | collective-permute-start | bytes 786440 | tf_op jit(solution)/shard_map/ppermute | solution.py:63
  79.5 4.6 %collective-permute-start.21 = (f32[2,128,128]{2,1,0:T(8,128)S(1)}, f32[2,128,128]{2,1,0:T(8,128)S(1)}, u32[]{:S(2)}, u32[]{:S(2)}) collective-permute-start(f32[2,128,128]{2,1,0:T(8,128)S(1)} %get-tuple-element.81.half_ref), channel_id=1, source_target_pairs={{0,8},{8,0},{16,24},{24,16},{32,40},{40,32},{48,56},{56,48},{64,72... | collective-permute-start | bytes 393224 | tf_op jit(solution)/shard_map/ppermute | solution.py:63

commit v2 on v1

--- a/solution.py
+++ b/solution.py
@@ -43,11 +43,17 @@
 DOWN = ring(lambda x, y, core: (x, y, 0) if core == 1 else None)
 
 
-Z_STEPS = (((0, 1), (2, 3), (4, 5), (6, 7)), ((1, 2), (3, 4), (5, 6), (7, 0)), ((0, 3), (1, 6), (2, 5), (4, 7)))
-
-
-def along_z(array, step):
-    pairs = [pair for a, b in Z_STEPS[step] for pair in ((a, b), (b, a))]
+Z_PAIRS = ((0, 1), (2, 3), (4, 5), (6, 7))
+Z_FAR = ((1, 4), (3, 6), (5, 0), (7, 2))
+Z_NEXT = ((1, 2), (3, 4), (5, 6), (7, 0))
+Z_TWO = [(z, (z + 6 + 4 * (z % 2)) % 8) for z in range(8)]
+
+
+def both_ways(pairs):
+    return [pair for a, b in pairs for pair in ((a, b), (b, a))]
+
+
+def along_z(array, pairs):
     return lax.ppermute(array, "head", pairs)
 
 
@@ -219,47 +225,87 @@
         wide_ref[:, 4 + j : 5 + j, :] = by_x[j]
 
 
-def mixed_kernel(
-    q_ref, inner_ref, gate_ref, grad_ref, gain_ref, cols_ref, near_ref, near_other_ref, far_ref, far_other_ref,
-    first_ref, rest_ref, mixed_ref, pay_ref, bucket_ref, finer_ref, shift_ref,
+def through(q, parts, cols_ref, head, levels):
+    bucket, finer = (jnp.concatenate([part[i] for part in parts], axis=1) for i in range(2))
+    found = dot(q, bucket, NN) + dot(q, finer, NN)
+    outer = sum(
+        cols_ref[:, 4 * level + head : 4 * level + head + 1] * found[:, HEAD_DIM * i : HEAD_DIM * (i + 1)]
+        for i, level in enumerate(levels)
+    )
+    return bucket, finer, outer
+
+
+def chosen_bucket(own_ref, other_ref, at, head, core):
+    return jnp.where(core == head // 2, own_ref[at, head % 2], other_ref[at, head % 2])
+
+
+def near_kernel(
+    q_ref, inner_ref, gate_ref, grad_ref, gain_ref, cols_ref, own_ref, other_ref, first_ref, rest_ref,
+    mixed_ref, act_ref, pulled_ref, bucket_ref, finer_ref, shift_ref, scaled_ref, turned_ref,
 ):
     core = place()[2]
     odd = flag(core == 1)
-    ones = jnp.ones((8, HEAD_DIM), BF16)
-    squares = jnp.zeros((8, WIDTH), F32)
-    crosses = jnp.zeros((8, WIDTH), F32)
-    for head in range(LOCAL):
-        slot, mine = head % 2, core == head // 2
+    for head in range(LOCAL):
+        slot = head % 2
         zeroth = rest_ref[slot, 0:HEAD_DIM, :] if head < 2 else first_ref[slot, 0:HEAD_DIM, :]
         earlier = odd * first_ref[0, HEAD_DIM + 4 + head : HEAD_DIM + 5 + head, :]
         parts = [split(odd * zeroth)]
         shift_ref[head] = jnp.ones((8, HEAD_DIM), F32)
-        for level in range(1, INTER):
-            own, other = (near_ref, near_other_ref) if level < 3 else (far_ref, far_other_ref)
-            at = (level - 1) % 2
-            chosen = jnp.where(mine, own[at, slot], other[at, slot])
+        shift_ref[head, 7:8, :] = earlier
+        for level in (1, 2):
+            chosen = chosen_bucket(own_ref, other_ref, level - 1, head, core)
             shift = jnp.exp(earlier + chosen[HEAD_DIM : HEAD_DIM + 1, :])
             shift_ref[head, level : level + 1, :] = shift
             parts.append(split(chosen[0:HEAD_DIM, :] * shift))
-        bucket, finer = (jnp.concatenate([part[i] for part in parts], axis=1) for i in range(2))
-        bucket_ref[head] = bucket
-        finer_ref[head] = finer
-        through = dot(q_ref[head], bucket, NN) + dot(q_ref[head], finer, NN)
-        mixed = inner_ref[head]
-        for level in range(INTER):
-            at = 4 * level + head
-            mixed = mixed + cols_ref[:, at : at + 1] * through[:, HEAD_DIM * level : HEAD_DIM * (level + 1)]
+        bucket_ref[head], finer_ref[head], outer = through(q_ref[head], parts, cols_ref, head, (0, 1, 2))
+        mixed_ref[head] = inner_ref[head] + outer
+        gate = gate_ref[head].astype(F32)
+        act = gate * jax.nn.sigmoid(gate)
+        act_ref[head] = act
+        pulled_ref[head] = grad_ref[head].astype(F32) * gain_ref[head : head + 1, :] * act
+        wide_q = q_ref[head].astype(F32)
+        for level in (3, 4):
+            scaled = cols_ref[:, 4 * level + head : 4 * level + head + 1] * wide_q
+            high, low = split(scaled)
+            at = 3 * HEAD_DIM * (level - 3)
+            for i, part in enumerate((high, low, high)):
+                scaled_ref[head, :, at + HEAD_DIM * i : at + HEAD_DIM * (i + 1)] = part
+            high, low = split(jnp.transpose(scaled))
+            turned_ref[head, level - 3, :, 0:WIDTH] = high
+            turned_ref[head, level - 3, :, WIDTH:] = low
+
+
+def mixed_kernel(
+    scaled_ref, near_ref, act_ref, pulled_ref, own_ref, other_ref, shifts_ref,
+    mixed_ref, pay_ref, bucket_ref, finer_ref, shift_ref,
+):
+    core = place()[2]
+    ones = jnp.ones((8, HEAD_DIM), BF16)
+    squares = jnp.zeros((8, WIDTH), F32)
+    crosses = jnp.zeros((8, WIDTH), F32)
+    for head in range(LOCAL):
+        earlier = shifts_ref[head, 7:8, :]
+        shift_ref[head] = shifts_ref[head]
+        parts = []
+        for level in (3, 4):
+            chosen = chosen_bucket(own_ref, other_ref, level - 3, head, core)
+            shift = jnp.exp(earlier + chosen[HEAD_DIM : HEAD_DIM + 1, :])
+            shift_ref[head, level : level + 1, :] = shift
+            parts.append(split(chosen[0:HEAD_DIM, :] * shift))
+        for i, (high, low) in enumerate(parts):
+            piece = slice(HEAD_DIM * i, HEAD_DIM * (i + 1))
+            bucket_ref[head, :, piece] = high
+            finer_ref[head, :, piece] = low
+        stacked = jnp.concatenate([part for high, low in parts for part in (high, high, low)], axis=0)
+        mixed = near_ref[head] + dot(scaled_ref[head], stacked, NN)
         mixed_ref[head] = mixed
-        gate = gate_ref[head].astype(F32)
-        gated = mixed * (gate * jax.nn.sigmoid(gate))
-        scaled = grad_ref[head].astype(F32) * gain_ref[head : head + 1, :]
+        gated = mixed * act_ref[head]
         squares = squares + dot(ones, (gated * gated).astype(BF16), NT)
-        crosses = crosses + dot(ones, (gated * scaled).astype(BF16), NT)
+        crosses = crosses + dot(ones, (mixed * pulled_ref[head]).astype(BF16), NT)
     for half in range(2):
         piece = slice(HEAD_DIM * half, HEAD_DIM * (half + 1))
         pay_ref[half : half + 1, :] = squares[0:1, piece]
         pay_ref[2 + half : 3 + half, :] = crosses[0:1, piece]
-    pay_ref[4:8, :] = jnp.zeros((4, HEAD_DIM), F32)
 
 
 def add_kernel(a_ref, b_ref, out_ref):
@@ -267,12 +313,13 @@
 
 
 def gate_kernel(
-    q_ref, mixed_ref, gate_ref, grad_ref, gain_ref, cols_ref, shift_ref, sums_ref, other_ref,
+    turned_ref, mixed_ref, act_ref, pulled_ref, grad_ref, shift_ref, sums_ref, three_ref, two_ref, one_ref,
     g_ref, scale_ref, keep_ref, send_ref,
 ):
     x, _, core = place()
     ones = jnp.ones((8, HEAD_DIM), F32)
-    sums = sums_ref[...] + other_ref[...]
+    sums = (sums_ref[...] + three_ref[...]) + (two_ref[...] + one_ref[...])
+    sums = jnp.concatenate([sums, jnp.zeros_like(sums)], axis=0)
     row = iotas((8, HEAD_DIM))[0]
     wide = [dot(jnp.where(row == i, sums, 0.0), ones, TN, HIGH) for i in range(4)]
     squares = jnp.concatenate(wide[0:2], axis=0)
@@ -285,15 +332,13 @@
     for ref in (keep_ref, send_ref):
         ref[:, :, HEAD_DIM:, :] = jnp.zeros((2, 2, 8, HEAD_DIM), F32)
     for head in range(LOCAL):
-        gate = gate_ref[head].astype(F32)
-        act = gate * jax.nn.sigmoid(gate)
+        act = act_ref[head]
         gated = mixed_ref[head] * act
-        grad = grad_ref[head].astype(F32)
-        gains.append(jnp.sum(grad * (gated * inverse), axis=0, keepdims=True))
-        grad_gated = inverse * (grad * gain_ref[head : head + 1, :]) - gated * pull
-        g = (grad_gated * act).astype(BF16)
+        gains.append(jnp.sum(grad_ref[head].astype(F32) * (gated * inverse), axis=0, keepdims=True))
+        g = (inverse * pulled_ref[head] - gated * act * pull).astype(BF16)
         g_ref[head] = g
-        far = reached(q_ref[head], g.astype(F32), cols_ref, shift_ref, head, (3, 4))
+        twice = jnp.concatenate([g, g], axis=0)
+        far = [dot(turned_ref[head, i], twice, NN) * shift_ref[head, 3 + i : 4 + i, :] for i in range(2)]
         near = jnp.where(lax.rem(x, 2) == 1, far[0], far[1])
 
         def put(ref):
@@ -388,7 +433,7 @@
 
 
 def backward_kernel(
-    q_ref, k_ref, v_ref, g_ref, mix_ref, weight_ref, scored_ref, bucket_ref, finer_ref, cols_ref, run_ref,
+    q_ref, k_ref, v_ref, g_ref, mix_ref, weight_ref, scored_ref, bucket_ref, finer_ref, far_ref, far_finer_ref, cols_ref, run_ref,
     grad_q_ref, grad_k_ref, grad_v_ref, levels_ref,
 ):
     early, late = iotas((WIDTH, WIDTH))
@@ -412,8 +457,9 @@
         wide_q = q.astype(F32)
         grown = jnp.exp(run_ref[head : head + 1, :])
         for level in range(INTER):
-            piece = slice(HEAD_DIM * level, HEAD_DIM * (level + 1))
-            pulled = dot(g, bucket_ref[head, :, piece], NT) + dot(g, finer_ref[head, :, piece], NT)
+            high, low = (bucket_ref, finer_ref) if level < 3 else (far_ref, far_finer_ref)
+            piece = slice(HEAD_DIM * (level % 3), HEAD_DIM * (level % 3 + 1))
+            pulled = dot(g, high[head, :, piece], NT) + dot(g, low[head, :, piece], NT)
             at = 4 * level + head
             grad_q = grad_q + cols_ref[:, at : at + 1] * pulled
             high, low = split(wide_q * pulled)
@@ -500,18 +546,28 @@
     near_other = send(near, SWAP)
     far, totals_x = call(x_kernel, [double, info], row, *from_x, totals_y)
     far_other = send(far, SWAP)
-    bucket_kind = ((LOCAL, HEAD_DIM, INTER * HEAD_DIM), BF16)
-    mixed, pay, bucket, finer, shift = call(
+    near_kind = ((LOCAL, HEAD_DIM, 3 * HEAD_DIM), BF16)
+    far_kind = ((LOCAL, HEAD_DIM, 2 * HEAD_DIM), BF16)
+    rows = ((LOCAL, 8, HEAD_DIM), F32)
+    scaled_kind = ((LOCAL, WIDTH, 6 * HEAD_DIM), BF16)
+    turned_kind = ((LOCAL, 2, HEAD_DIM, 2 * WIDTH), BF16)
+    near_mixed, act, pulled, bucket, finer, shifts, scaled_q, turned_q = call(
+        near_kernel,
+        [(tokens, F32)] * 3 + [near_kind, near_kind, rows, scaled_kind, turned_kind],
+        queries, inner, gate_input, out_grad, norm_gain, cols, near, near_other, first, rest,
+        flops=10**9,
+    )
+    mixed, pay, far_bucket, far_finer, shift = call(
         mixed_kernel,
-        [(tokens, F32), ((8, HEAD_DIM), F32), bucket_kind, bucket_kind, ((LOCAL, 8, HEAD_DIM), F32)],
-        queries, inner, gate_input, out_grad, norm_gain, cols, near, near_other, far, far_other, first, rest,
-    )
-    for step in range(2):
-        (pay,) = call(add_kernel, [((8, HEAD_DIM), F32)], pay, along_z(pay, step))
+        [(tokens, F32), ((4, HEAD_DIM), F32), far_kind, far_kind, rows],
+        scaled_q, near_mixed, act, pulled, far, far_other, shifts,
+    )
+    (pay,) = call(add_kernel, [((4, HEAD_DIM), F32)], pay, along_z(pay, both_ways(Z_PAIRS)))
+    others = [along_z(pay, pairs) for pairs in (both_ways(Z_FAR), Z_TWO, both_ways(Z_NEXT))]
     grad_mixed, scale, far_keep, far_away = call(
         gate_kernel,
         [(tokens, BF16), ((2, WIDTH, HEAD_DIM), F32), double, double],
-        queries, mixed, gate_input, out_grad, norm_gain, cols, shift, pay, along_z(pay, 2),
+        turned_q, mixed, act, pulled, out_grad, shift, pay, *others,
     )
     to_one, to_far = call(meet_kernel, [message] * 2, far_keep, send(far_away, SWAP))
     back_x = [send(to_one, along_x(-1)), send(to_far, along_x(-2)), send(to_far, along_x(-3))]
@@ -528,7 +584,7 @@
     grad_queries, grad_k, grad_v, levels = call(
         backward_kernel,
         [(tokens, BF16), (tokens, F32), (tokens, F32), ((LEVELS, LOCAL, WIDTH), F32)],
-        queries, keys, values, grad_mixed, mixing, weight, scored, bucket, finer, cols, running,
+        queries, keys, values, grad_mixed, mixing, weight, scored, bucket, finer, far_bucket, far_finer, cols, running,
         flops=10**9,
     )
     half, gain_sum = call(join_kernel, [((2, HEAD_DIM, HEAD_DIM), F32), ((LOCAL, HEAD_DIM), F32)], *back_y)

time: 85.6 us -> 84.7 us (0.989)
  waiting for transfers between devices: 29.9 us -> 27.2 us
  starting transfers between devices: 39.5 us -> 40.6 us
    ppermute x3 -> x4, waiting for transfers between devices: 4.84 us -> 2.14 us  [along_z(): return lax.ppermute(array, 'head', pairs)]
    ppermute x3 -> x4, starting transfers between devices: 8.15 us -> 10.5 us  [along_z(): return lax.ppermute(array, 'head', pairs)]
    ppermute x20, starting transfers between devices: 31.3 us -> 30.1 us  [send(): return lax.ppermute(array, 'seq', pairs)]
  transfers between devices with their start and end apart: 23 -> 24, of which waited for: 15 -> 15; matrix products, arithmetic and copies ran while one was open for 0% -> 0% of each run, Pallas kernels for 9% -> 11%
where the time goes in v2:
time: 84.7 us; the launch traced here: 84.5 us
  starting transfers between devices  40.6 us (48%)
  waiting for transfers between devices  27.2 us (32%)
  Pallas kernels  15.8 us (19%)
    ppermute x20, starting transfers between devices, send(): return lax.ppermute(array, 'seq', pairs)  30.1 us
    ppermute x20, waiting for transfers between devices, send(): return lax.ppermute(array, 'seq', pairs)  25.1 us
    pallas_call x15, Pallas kernels, call(): pl.pallas_call(kernel, out_shape=shapes, in_specs=[pl.BlockSpec(memory_sp...  15.8 us
    ppermute x4, starting transfers between devices, along_z(): return lax.ppermute(array, 'head', pairs)  10.5 us
    ppermute x4, waiting for transfers between devices, along_z(): return lax.ppermute(array, 'head', pairs)  2.14 us
  transfers between devices with their start and end apart: 24, of which 15 were waited for; matrix products, arithmetic and copies ran while one was open for 0% of the time, Pallas kernels for 11%

profile of v2, /device:TPU:1, one launch (start us, length us, event | category | flops | bytes accessed | tf_op | source)
XLA Modules:
  0.0 84.5 jit_solution(11443712749053784316)
XLA Ops:
  0.7 2.4 %shard_map.135 = (f32[2,136,128]{2,1,0:T(8,128)S(1)}, f32[2,136,128]{2,1,0:T(8,128)S(1)}, f32[4,256]{1,0:T(4,128)S(1)}) custom-call(f32[4,256]{1,0:T(4,128)} %decay_hbm.1, bf16[4,256,128]{2,1,0:T(8,128)(2,1)} %k_ref.5, bf16[4,256,128]{2,1,0:T(8,128)(2,1)} %v_ref.5), custom_call_target="tpu_custom_call" | custom-call | bytes 811008 | tf_op jit(solution)/shard_map/pallas_call | solution.py:504
  3.1 3.3 %collective-permute-start = (f32[2,136,128]{2,1,0:T(8,128)S(1)}, f32[2,136,128]{2,1,0:T(8,128)S(1)}, u32[]{:S(2)}, u32[]{:S(2)}) collective-permute-start(f32[2,136,128]{2,1,0:T(8,128)S(1)} %get-tuple-element.61), channel_id=1, source_target_pairs={{0,8},{8,0},{16,24},{24,16},{32,40},{40,32},{48,56},{56,48},{64,72... | collective-permute-start | bytes 417800 | tf_op jit(solution)/shard_map/ppermute | solution.py:69
  7.6 2.2 %collective-permute-start.2 = (f32[2,136,128]{2,1,0:T(8,128)S(1)}, f32[2,136,128]{2,1,0:T(8,128)S(1)}, u32[]{:S(2)}, u32[]{:S(2)}) collective-permute-start(f32[2,136,128]{2,1,0:T(8,128)S(1)} %shard_map.137.own_ref), channel_id=1, source_target_pairs={{0,32},{8,40},{16,48},{24,56},{32,0},{40,8},{48,16},{56,24},{64,96... | collective-permute-start | bytes 417800 | tf_op jit(solution)/shard_map/ppermute | solution.py:69
  9.8 1.1 %collective-permute-start.3 = (f32[2,136,128]{2,1,0:T(8,128)S(1)}, f32[2,136,128]{2,1,0:T(8,128)S(1)}, u32[]{:S(2)}, u32[]{:S(2)}) collective-permute-start(f32[2,136,128]{2,1,0:T(8,128)S(1)} %shard_map.137.own_ref), channel_id=1, source_target_pairs={{0,48},{8,56},{16,0},{24,8},{32,16},{40,24},{48,32},{56,40},{64,11... | collective-permute-start | bytes 417800 | tf_op jit(solution)/shard_map/ppermute | solution.py:69
  10.8 3.3 %collective-permute-done.1.one_ref = f32[2,136,128]{2,1,0:T(8,128)S(1)} collective-permute-done((f32[2,136,128]{2,1,0:T(8,128)S(1)}, f32[2,136,128]{2,1,0:T(8,128)S(1)}, u32[]{:S(2)}, u32[]{:S(2)}) %collective-permute-start.1) | collective-permute-done | bytes 139296 | tf_op jit(solution)/shard_map/ppermute | solution.py:69
  14.1 2.1 %collective-permute-done.2.two_ref = f32[2,136,128]{2,1,0:T(8,128)S(1)} collective-permute-done((f32[2,136,128]{2,1,0:T(8,128)S(1)}, f32[2,136,128]{2,1,0:T(8,128)S(1)}, u32[]{:S(2)}, u32[]{:S(2)}) %collective-permute-start.2) | collective-permute-done | bytes 139296 | tf_op jit(solution)/shard_map/ppermute | solution.py:69
  17.5 2.5 %collective-permute-start.7 = (f32[2,136,128]{2,1,0:T(8,128)S(1)}, f32[2,136,128]{2,1,0:T(8,128)S(1)}, u32[]{:S(2)}, u32[]{:S(2)}) collective-permute-start(f32[2,136,128]{2,1,0:T(8,128)S(1)} %get-tuple-element.68.own_ref), channel_id=1, source_target_pairs={{0,128},{8,136},{16,144},{24,152},{32,160},{40,168},{48,176},{56,1... | collective-permute-start | bytes 417800 | tf_op jit(solution)/shard_map/ppermute | solution.py:69
  20.0 1.1 %collective-permute-start.8 = (f32[2,136,128]{2,1,0:T(8,128)S(1)}, f32[2,136,128]{2,1,0:T(8,128)S(1)}, u32[]{:S(2)}, u32[]{:S(2)}) collective-permute-start(f32[2,136,128]{2,1,0:T(8,128)S(1)} %get-tuple-element.68.own_ref), channel_id=1, source_target_pairs={{0,192},{8,200},{16,208},{24,216},{32,224},{40,232},{48,240},{56,2... | collective-permute-start | bytes 417800 | tf_op jit(solution)/shard_map/ppermute | solution.py:69
  21.1 2.1 %collective-permute-start.4 = (f32[2,2,136,128]{3,2,1,0:T(8,128)S(1)}, f32[2,2,136,128]{3,2,1,0:T(8,128)S(1)}, u32[]{:S(2)}, u32[]{:S(2)}) collective-permute-start(f32[2,2,136,128]{3,2,1,0:T(8,128)S(1)} %get-tuple-element.62.own_ref), channel_id=1, source_target_pairs={{0,8},{8,0},{16,24},{24,16},{32,40},{40,32},{48,56},{56,48},{64,72... | collective-permute-start | bytes 835592 | tf_op jit(solution)/shard_map/ppermute | solution.py:69
  23.2 2.0 %collective-permute-done.7.two_ref = f32[2,136,128]{2,1,0:T(8,128)S(1)} collective-permute-done((f32[2,136,128]{2,1,0:T(8,128)S(1)}, f32[2,136,128]{2,1,0:T(8,128)S(1)}, u32[]{:S(2)}, u32[]{:S(2)}) %collective-permute-start.7) | collective-permute-done | bytes 139296 | tf_op jit(solution)/shard_map/ppermute | solution.py:69
  25.4 2.7 %collective-permute-start.9 = (f32[2,2,136,128]{3,2,1,0:T(8,128)S(1)}, f32[2,2,136,128]{3,2,1,0:T(8,128)S(1)}, u32[]{:S(2)}, u32[]{:S(2)}) collective-permute-start(f32[2,2,136,128]{3,2,1,0:T(8,128)S(1)} %get-tuple-element.70.own_ref), channel_id=1, source_target_pairs={{0,8},{8,0},{16,24},{24,16},{32,40},{40,32},{48,56},{56,48},{64,72... | collective-permute-start | bytes 835592 | tf_op jit(solution)/shard_map/ppermute | solution.py:69
  28.1 1.3 %collective-permute-start.5 = (f32[2,136,128]{2,1,0:T(8,128)S(1)}, f32[2,136,128]{2,1,0:T(8,128)S(1)}, u32[]{:S(2)}, u32[]{:S(2)}) collective-permute-start(f32[2,136,128]{2,1,0:T(8,128)S(1)} %get-tuple-element.60.keep_ref), channel_id=1, source_target_pairs={{0,8},{16,24},{32,40},{48,56},{64,72},{80,88},{96,104},{112,120},{... | collective-permute-start | bytes 417800 | tf_op jit(solution)/shard_map/ppermute | solution.py:69
  29.5 1.0 %shard_map.136 = (f32[4,256,128]{2,1,0:T(8,128)S(1)}, bf16[4,256,256]{2,1,0:T(8,128)(2,1)S(1)}, f32[4,256,256]{2,1,0:T(8,128)S(1)}, f32[4,256,256]{2,1,0:T(8,128)S(1)}, f32[256,128]{1,0:T(8,128)S(1)}) custom-call(bf16[4,256,128]{2,1,0:T(8,128)(2,1)S(1)} %copy-done.2, bf16[4,256,128]{2,1,0:T(8,128)(2,1)S(1)} %copy-done, bf16[4,256,128]{2,1,0:T(8,128)(2,1)S(1)} %copy-done.1, ...), custom_call_target="tpu_custom_call" | custom-call | flops 1000000000 | bytes 4153344 | tf_op jit(solution)/shard_map/pallas_call | solution.py:504
  31.4 1.3 %shard_map.139 = (f32[4,256,128]{2,1,0:T(8,128)S(1)}, f32[4,256,128]{2,1,0:T(8,128)S(1)}, f32[4,256,128]{2,1,0:T(8,128)S(1)}, bf16[4,128,384]{2,1,0:T(8,128)(2,1...) custom-call(bf16[4,256,128]{2,1,0:T(8,128)(2,1)S(1)} %copy-done.2, ...), custom_call_target="tpu_custom_call" | custom-call | flops 1000000000 | bytes 7276544 | tf_op jit(solution)/shard_map/pallas_call | solution.py:504
  32.7 1.1 %shard_map.141 = (f32[4,256,128]{2,1,0:T(8,128)S(1)}, f32[4,128]{1,0:T(4,128)S(1)}, bf16[4,128,256]{2,1,0:T(8,128)(2,1)S(1)}, bf16[4,128,256]{2,1,0:T(8,128)(2,1)S(1)}, f32[4,8,128]{2,1,0:T(8,128)S(1)}) custom-call(bf16[4,256,768]{2,1,0:T(8,128)(2,1)S(1)} %get-tuple-element.64.scaled_ref, f32[4,256,128]{2,1,0:T(8,128)S(1)} %get-tuple-element.65.near_ref, ...), custom_call_target="tpu_custom_call" | custom-call | bytes 4786176 | tf_op jit(solution)/shard_map/pallas_call | solution.py:504
  33.9 1.3 %collective-permute-start.10 = (f32[4,128]{1,0:T(4,128)S(1)}, f32[4,128]{1,0:T(4,128)S(1)}, u32[]{:S(2)}, u32[]{:S(2)}) collective-permute-start(f32[4,128]{1,0:T(4,128)S(1)} %get-tuple-element.74.a_ref), channel_id=1, source_target_pairs={{0,1},{1,0},{2,3},{3,2},{4,5},{5,4},{6,7},{7,6},{8,9},{9,8},{10,11... | collective-permute-start | bytes 6152 | tf_op jit(solution)/shard_map/ppermute | solution.py:57
  35.2 1.1 %collective-permute-done.10.b_ref = f32[4,128]{1,0:T(4,128)S(1)} collective-permute-done((f32[4,128]{1,0:T(4,128)S(1)}, f32[4,128]{1,0:T(4,128)S(1)}, u32[]{:S(2)}, u32[]{:S(2)}) %collective-permute-start.10) | collective-permute-done | bytes 2080 | tf_op jit(solution)/shard_map/ppermute | solution.py:57
  36.3 6.1 %collective-permute-start.11 = (f32[4,128]{1,0:T(4,128)S(1)}, f32[4,128]{1,0:T(4,128)S(1)}, u32[]{:S(2)}, u32[]{:S(2)}) collective-permute-start(f32[4,128]{1,0:T(4,128)S(1)} %shard_map.142.sums_ref), channel_id=1, source_target_pairs={{1,4},{4,1},{3,6},{6,3},{5,0},{0,5},{7,2},{2,7},{9,12},{12,9},{11,... | collective-permute-start | bytes 6152 | tf_op jit(solution)/shard_map/ppermute | solution.py:57
  42.7 2.9 %collective-permute-start.13 = (f32[4,128]{1,0:T(4,128)S(1)}, f32[4,128]{1,0:T(4,128)S(1)}, u32[]{:S(2)}, u32[]{:S(2)}) collective-permute-start(f32[4,128]{1,0:T(4,128)S(1)} %shard_map.142.sums_ref), channel_id=1, source_target_pairs={{1,2},{2,1},{3,4},{4,3},{5,6},{6,5},{7,0},{0,7},{9,10},{10,9},{11,... | collective-permute-start | bytes 6152 | tf_op jit(solution)/shard_map/ppermute | solution.py:57
  46.6 1.4 %shard_map.143 = (bf16[4,256,128]{2,1,0:T(8,128)(2,1)S(1)}, f32[2,256,128]{2,1,0:T(8,128)S(1)}, f32[2,2,136,128]{3,2,1,0:T(8,128)S(1)}, f32[2,2,136,128]{3,2,1,0:T(8,128)S(1)}) custom-call(bf16[4,2,128,512]{3,2,1,0:T(8,128)(2,1)S(1)} %get-tuple-element.63.turned_ref, f32[4,256,128]{2,1,0:T(8,128)S(1)} %get-tuple-element.72.mixed_ref, ...), custom_call_target="tpu_custom_call" | custom-call | bytes 3989504 | tf_op jit(solution)/shard_map/pallas_call | solution.py:504
  48.0 3.1 %collective-permute-start.14 = (f32[2,2,136,128]{3,2,1,0:T(8,128)S(1)}, f32[2,2,136,128]{3,2,1,0:T(8,128)S(1)}, u32[]{:S(2)}, u32[]{:S(2)}) collective-permute-start(f32[2,2,136,128]{3,2,1,0:T(8,128)S(1)} %get-tuple-element.87), channel_id=1, source_target_pairs={{0,8},{8,0},{16,24},{24,16},{32,40},{40,32},{48,56},{56,48},{64,72... | collective-permute-start | bytes 835592 | tf_op jit(solution)/shard_map/ppermute | solution.py:69
  51.1 2.7 %shard_map.144 = (bf16[4,256,128]{2,1,0:T(8,128)(2,1)}, bf16[4,256,128]{2,1,0:T(8,128)(2,1)}, f32[2,2,136,128]{3,2,1,0:T(8,128)S(1)}, f32[2,2,136,128]{3,2,1,0:T(8,128)S(1)}, f32[4,128,128]{2,1,0:T(8,128)S(1)}) custom-call(bf16[4,256,128]{2,1,0:T(8,128)(2,1)S(1)} %copy-done.2, bf16[4,256,128]{2,1,0:T(8,128)(2,1)S(1)} %get-tuple-element.75.g_ref, ...), custom_call_target="tpu_custom_call" | custom-call | flops 1000000000 | bytes 3328000 | tf_op jit(solution)/shard_map/pallas_call | solution.py:504
  53.8 2.4 %collective-permute-start.15 = (f32[2,136,128]{2,1,0:T(8,128)S(1)}, f32[2,136,128]{2,1,0:T(8,128)S(1)}, u32[]{:S(2)}, u32[]{:S(2)}) collective-permute-start(f32[2,136,128]{2,1,0:T(8,128)S(1)} %get-tuple-element.89), channel_id=1, source_target_pairs={{0,192},{8,200},{16,208},{24,216},{32,224},{40,232},{48,240},{56,2... | collective-permute-start | bytes 417800 | tf_op jit(solution)/shard_map/ppermute | solution.py:69
  57.2 2.3 %collective-permute-done.15.one_ref = f32[2,136,128]{2,1,0:T(8,128)S(1)} collective-permute-done((f32[2,136,128]{2,1,0:T(8,128)S(1)}, f32[2,136,128]{2,1,0:T(8,128)S(1)}, u32[]{:S(2)}, u32[]{:S(2)}) %collective-permute-start.15) | collective-permute-done | bytes 139296 | tf_op jit(solution)/shard_map/ppermute | solution.py:69
  59.5 2.7 %collective-permute-done.16.two_ref = f32[2,136,128]{2,1,0:T(8,128)S(1)} collective-permute-done((f32[2,136,128]{2,1,0:T(8,128)S(1)}, f32[2,136,128]{2,1,0:T(8,128)S(1)}, u32[]{:S(2)}, u32[]{:S(2)}) %collective-permute-start.16) | collective-permute-done | bytes 139296 | tf_op jit(solution)/shard_map/ppermute | solution.py:69
  62.2 4.1 %collective-permute-done.17.three_ref = f32[2,136,128]{2,1,0:T(8,128)S(1)} collective-permute-done((f32[2,136,128]{2,1,0:T(8,128)S(1)}, f32[2,136,128]{2,1,0:T(8,128)S(1)}, u32[]{:S(2)}, u32[]{:S(2)}) %collective-permute-start.17) | collective-permute-done | bytes 139296 | tf_op jit(solution)/shard_map/ppermute | solution.py:69
  66.5 2.1 %collective-permute-start.19 = (f32[2,136,128]{2,1,0:T(8,128)S(1)}, f32[2,136,128]{2,1,0:T(8,128)S(1)}, u32[]{:S(2)}, u32[]{:S(2)}) collective-permute-start(f32[2,136,128]{2,1,0:T(8,128)S(1)} %get-tuple-element.94), channel_id=1, source_target_pairs={{0,48},{8,56},{16,0},{24,8},{32,16},{40,24},{48,32},{56,40},{64,11... | collective-permute-start | bytes 417800 | tf_op jit(solution)/shard_map/ppermute | solution.py:69
  69.5 3.2 %collective-permute-start.23 = (f32[4,128,128]{2,1,0:T(8,128)S(1)}, f32[4,128,128]{2,1,0:T(8,128)S(1)}, u32[]{:S(2)}, u32[]{:S(2)}) collective-permute-start(f32[4,128,128]{2,1,0:T(8,128)S(1)} %get-tuple-element.98), channel_id=1, source_target_pairs={{8,0},{24,16},{40,32},{56,48},{72,64},{88,80},{104,96},{120,112},{... | collective-permute-start | bytes 786440 | tf_op jit(solution)/shard_map/ppermute | solution.py:69
  72.7 1.8 %collective-permute-done.20.two_ref = f32[2,136,128]{2,1,0:T(8,128)S(1)} collective-permute-done((f32[2,136,128]{2,1,0:T(8,128)S(1)}, f32[2,136,128]{2,1,0:T(8,128)S(1)}, u32[]{:S(2)}, u32[]{:S(2)}) %collective-permute-start.20) | collective-permute-done | bytes 139296 | tf_op jit(solution)/shard_map/ppermute | solution.py:69
  74.5 4.1 %collective-permute-done.21.three_ref = f32[2,136,128]{2,1,0:T(8,128)S(1)} collective-permute-done((f32[2,136,128]{2,1,0:T(8,128)S(1)}, f32[2,136,128]{2,1,0:T(8,128)S(1)}, u32[]{:S(2)}, u32[]{:S(2)}) %collective-permute-start.21) | collective-permute-done | bytes 139296 | tf_op jit(solution)/shard_map/ppermute | solution.py:69
  79.3 4.0 %shard_map.145 = (bf16[4,256,128]{2,1,0:T(8,128)(2,1)}, f32[4,256,128]{2,1,0:T(8,128)S(1)}, f32[4,256,128]{2,1,0:T(8,128)S(1)}, f32[21,4,256]{2,1,0:T(4,128)}) custom-call(bf16[4,256,128]{2,1,0:T(8,128)(2,1)S(1)} %copy-done.2, bf16[4,256,128]{2,1,0:T(8,128)(2,1)S(1)} %copy-done, bf16[4,256,128]{2,1,0:T(8,128)(2,1)S(1)} %copy-done.1, ...), custom_call_target="tpu_custom_call" | custom-call | flops 1000000000 | bytes 6512640 | tf_op jit(solution)/shard_map/pallas_call | solution.py:504
  83.3 1.2 %shard_map.149 = (bf16[4,256,128]{2,1,0:T(8,128)(2,1)}, bf16[4,256,128]{2,1,0:T(8,128)(2,1)}, f32[4,128]{1,0:T(4,128)}) custom-call(bf16[4,256,128]{2,1,0:T(8,128)(2,1)S(1)} %copy-done, bf16[4,256,128]{2,1,0:T(8,128)(2,1)S(1)} %copy-done.1, f32[256,128]{1,0:T(8,128)S(1)} %get-tuple-element.59.cols_ref, f32[2,128,128]{2,1,0:T(8,128)S(1)} %get-tuple-element.97.half_ref, ...), custom_call_target="tpu_custom_call" | custom-call | bytes 2895872 | tf_op jit(solution)/shard_map/pallas_call | solution.py:504
  (45 shorter events, 7.5 us)
Async XLA Ops:
  0.6 28.8 %copy-start = (bf16[4,256,128]{2,1,0:T(8,128)(2,1)S(1)}, bf16[4,256,128]{2,1,0:T(8,128)(2,1)}, u32[]{:S(2)}) copy-start(bf16[4,256,128]{2,1,0:T(8,128)(2,1)} %k_ref.5) | copy-start | bytes 786436
  0.6 28.8 %copy-start.1 = (bf16[4,256,128]{2,1,0:T(8,128)(2,1)S(1)}, bf16[4,256,128]{2,1,0:T(8,128)(2,1)}, u32[]{:S(2)}) copy-start(bf16[4,256,128]{2,1,0:T(8,128)(2,1)} %v_ref.5) | copy-start | bytes 786436
  0.7 28.8 %copy-start.2 = (bf16[4,256,128]{2,1,0:T(8,128)(2,1)S(1)}, bf16[4,256,128]{2,1,0:T(8,128)(2,1)}, u32[]{:S(2)}) copy-start(bf16[4,256,128]{2,1,0:T(8,128)(2,1)} %q_ref.7) | copy-start | bytes 786436
  0.7 28.8 %copy-start.5 = (f32[4,21,256]{2,0,1:T(4,128)S(1)}, f32[4,21,256]{2,0,1:T(4,128)}, u32[]{:S(2)}) copy-start(f32[4,21,256]{2,0,1:T(4,128)} %param.12) | copy-start | bytes 258052
  3.1 4.3 %collective-permute-start = (f32[2,136,128]{2,1,0:T(8,128)S(1)}, f32[2,136,128]{2,1,0:T(8,128)S(1)}, u32[]{:S(2)}, u32[]{:S(2)}) collective-permute-start(f32[2,136,128]{2,1,0:T(8,128)S(1)} %get-tuple-element.61), channel_id=1, source_target_pairs={{0,8},{8,0},{16,24},{24,16},{32,40},{40,32},{48,56},{56,48},{64,72... | collective-permute-start | bytes 417800 | tf_op jit(solution)/shard_map/ppermute | solution.py:69
  7.5 6.6 %collective-permute-start.1 = (f32[2,136,128]{2,1,0:T(8,128)S(1)}, f32[2,136,128]{2,1,0:T(8,128)S(1)}, u32[]{:S(2)}, u32[]{:S(2)}) collective-permute-start(f32[2,136,128]{2,1,0:T(8,128)S(1)} %shard_map.137.own_ref), channel_id=1, source_target_pairs={{0,16},{8,24},{16,32},{24,40},{32,48},{40,56},{48,0},{56,8},{64,80... | collective-permute-start | bytes 417800 | tf_op jit(solution)/shard_map/ppermute | solution.py:69
  7.6 8.6 %collective-permute-start.2 = (f32[2,136,128]{2,1,0:T(8,128)S(1)}, f32[2,136,128]{2,1,0:T(8,128)S(1)}, u32[]{:S(2)}, u32[]{:S(2)}) collective-permute-start(f32[2,136,128]{2,1,0:T(8,128)S(1)} %shard_map.137.own_ref), channel_id=1, source_target_pairs={{0,32},{8,40},{16,48},{24,56},{32,0},{40,8},{48,16},{56,24},{64,96... | collective-permute-start | bytes 417800 | tf_op jit(solution)/shard_map/ppermute | solution.py:69
  9.8 7.2 %collective-permute-start.3 = (f32[2,136,128]{2,1,0:T(8,128)S(1)}, f32[2,136,128]{2,1,0:T(8,128)S(1)}, u32[]{:S(2)}, u32[]{:S(2)}) collective-permute-start(f32[2,136,128]{2,1,0:T(8,128)S(1)} %shard_map.137.own_ref), channel_id=1, source_target_pairs={{0,48},{8,56},{16,0},{24,8},{32,16},{40,24},{48,32},{56,40},{64,11... | collective-permute-start | bytes 417800 | tf_op jit(solution)/shard_map/ppermute | solution.py:69
  17.0 6.2 %collective-permute-start.6 = (f32[2,136,128]{2,1,0:T(8,128)S(1)}, f32[2,136,128]{2,1,0:T(8,128)S(1)}, u32[]{:S(2)}, u32[]{:S(2)}) collective-permute-start(f32[2,136,128]{2,1,0:T(8,128)S(1)} %get-tuple-element.68.own_ref), channel_id=1, source_target_pairs={{0,64},{8,72},{16,80},{24,88},{32,96},{40,104},{48,112},{56,120},{... | collective-permute-start | bytes 417800 | tf_op jit(solution)/shard_map/ppermute | solution.py:69
  17.5 7.7 %collective-permute-start.7 = (f32[2,136,128]{2,1,0:T(8,128)S(1)}, f32[2,136,128]{2,1,0:T(8,128)S(1)}, u32[]{:S(2)}, u32[]{:S(2)}) collective-permute-start(f32[2,136,128]{2,1,0:T(8,128)S(1)} %get-tuple-element.68.own_ref), channel_id=1, source_target_pairs={{0,128},{8,136},{16,144},{24,152},{32,160},{40,168},{48,176},{56,1... | collective-permute-start | bytes 417800 | tf_op jit(solution)/shard_map/ppermute | solution.py:69
  20.0 5.3 %collective-permute-start.8 = (f32[2,136,128]{2,1,0:T(8,128)S(1)}, f32[2,136,128]{2,1,0:T(8,128)S(1)}, u32[]{:S(2)}, u32[]{:S(2)}) collective-permute-start(f32[2,136,128]{2,1,0:T(8,128)S(1)} %get-tuple-element.68.own_ref), channel_id=1, source_target_pairs={{0,192},{8,200},{16,208},{24,216},{32,224},{40,232},{48,240},{56,2... | collective-permute-start | bytes 417800 | tf_op jit(solution)/shard_map/ppermute | solution.py:69
  21.1 10.2 %collective-permute-start.4 = (f32[2,2,136,128]{3,2,1,0:T(8,128)S(1)}, f32[2,2,136,128]{3,2,1,0:T(8,128)S(1)}, u32[]{:S(2)}, u32[]{:S(2)}) collective-permute-start(f32[2,2,136,128]{3,2,1,0:T(8,128)S(1)} %get-tuple-element.62.own_ref), channel_id=1, source_target_pairs={{0,8},{8,0},{16,24},{24,16},{32,40},{40,32},{48,56},{56,48},{64,72... | collective-permute-start | bytes 835592 | tf_op jit(solution)/shard_map/ppermute | solution.py:69
  25.4 7.3 %collective-permute-start.9 = (f32[2,2,136,128]{3,2,1,0:T(8,128)S(1)}, f32[2,2,136,128]{3,2,1,0:T(8,128)S(1)}, u32[]{:S(2)}, u32[]{:S(2)}) collective-permute-start(f32[2,2,136,128]{3,2,1,0:T(8,128)S(1)} %get-tuple-element.70.own_ref), channel_id=1, source_target_pairs={{0,8},{8,0},{16,24},{24,16},{32,40},{40,32},{48,56},{56,48},{64,72... | collective-permute-start | bytes 835592 | tf_op jit(solution)/shard_map/ppermute | solution.py:69
  28.1 3.2 %collective-permute-start.5 = (f32[2,136,128]{2,1,0:T(8,128)S(1)}, f32[2,136,128]{2,1,0:T(8,128)S(1)}, u32[]{:S(2)}, u32[]{:S(2)}) collective-permute-start(f32[2,136,128]{2,1,0:T(8,128)S(1)} %get-tuple-element.60.keep_ref), channel_id=1, source_target_pairs={{0,8},{16,24},{32,40},{48,56},{64,72},{80,88},{96,104},{112,120},{... | collective-permute-start | bytes 417800 | tf_op jit(solution)/shard_map/ppermute | solution.py:69
  29.5 1.9 %copy-start.3 = (bf16[4,256,128]{2,1,0:T(8,128)(2,1)S(1)}, bf16[4,256,128]{2,1,0:T(8,128)(2,1)}, u32[]{:S(2)}) copy-start(bf16[4,256,128]{2,1,0:T(8,128)(2,1)} %grad_ref.5) | copy-start | bytes 786436
  29.5 1.9 %copy-start.4 = (bf16[4,256,128]{2,1,0:T(8,128)(2,1)S(1)}, bf16[4,256,128]{2,1,0:T(8,128)(2,1)}, u32[]{:S(2)}) copy-start(bf16[4,256,128]{2,1,0:T(8,128)(2,1)} %gate_ref.3) | copy-start | bytes 786436
  29.5 1.9 %copy-start.6 = (f32[4,128]{1,0:T(4,128)S(1)}, f32[4,128]{1,0:T(4,128)}, u32[]{:S(2)}) copy-start(f32[4,128]{1,0:T(4,128)} %gain_ref.3) | copy-start | bytes 6148
  33.9 2.4 %collective-permute-start.10 = (f32[4,128]{1,0:T(4,128)S(1)}, f32[4,128]{1,0:T(4,128)S(1)}, u32[]{:S(2)}, u32[]{:S(2)}) collective-permute-start(f32[4,128]{1,0:T(4,128)S(1)} %get-tuple-element.74.a_ref), channel_id=1, source_target_pairs={{0,1},{1,0},{2,3},{3,2},{4,5},{5,4},{6,7},{7,6},{8,9},{9,8},{10,11... | collective-permute-start | bytes 6152 | tf_op jit(solution)/shard_map/ppermute | solution.py:57
  36.3 9.2 %collective-permute-start.11 = (f32[4,128]{1,0:T(4,128)S(1)}, f32[4,128]{1,0:T(4,128)S(1)}, u32[]{:S(2)}, u32[]{:S(2)}) collective-permute-start(f32[4,128]{1,0:T(4,128)S(1)} %shard_map.142.sums_ref), channel_id=1, source_target_pairs={{1,4},{4,1},{3,6},{6,3},{5,0},{0,5},{7,2},{2,7},{9,12},{12,9},{11,... | collective-permute-start | bytes 6152 | tf_op jit(solution)/shard_map/ppermute | solution.py:57
  42.4 3.3 %collective-permute-start.12 = (f32[4,128]{1,0:T(4,128)S(1)}, f32[4,128]{1,0:T(4,128)S(1)}, u32[]{:S(2)}, u32[]{:S(2)}) collective-permute-start(f32[4,128]{1,0:T(4,128)S(1)} %shard_map.142.sums_ref), channel_id=1, source_target_pairs={{0,6},{1,3},{2,0},{3,5},{4,2},{5,7},{6,4},{7,1},{8,14},{9,11},{10,... | collective-permute-start | bytes 6152 | tf_op jit(solution)/shard_map/ppermute | solution.py:57
  42.7 3.9 %collective-permute-start.13 = (f32[4,128]{1,0:T(4,128)S(1)}, f32[4,128]{1,0:T(4,128)S(1)}, u32[]{:S(2)}, u32[]{:S(2)}) collective-permute-start(f32[4,128]{1,0:T(4,128)S(1)} %shard_map.142.sums_ref), channel_id=1, source_target_pairs={{1,2},{2,1},{3,4},{4,3},{5,6},{6,5},{7,0},{0,7},{9,10},{10,9},{11,... | collective-permute-start | bytes 6152 | tf_op jit(solution)/shard_map/ppermute | solution.py:57
  48.0 5.8 %collective-permute-start.14 = (f32[2,2,136,128]{3,2,1,0:T(8,128)S(1)}, f32[2,2,136,128]{3,2,1,0:T(8,128)S(1)}, u32[]{:S(2)}, u32[]{:S(2)}) collective-permute-start(f32[2,2,136,128]{3,2,1,0:T(8,128)S(1)} %get-tuple-element.87), channel_id=1, source_target_pairs={{0,8},{8,0},{16,24},{24,16},{32,40},{40,32},{48,56},{56,48},{64,72... | collective-permute-start | bytes 835592 | tf_op jit(solution)/shard_map/ppermute | solution.py:69
  53.8 3.4 %collective-permute-start.18 = (f32[2,2,136,128]{3,2,1,0:T(8,128)S(1)}, f32[2,2,136,128]{3,2,1,0:T(8,128)S(1)}, u32[]{:S(2)}, u32[]{:S(2)}) collective-permute-start(f32[2,2,136,128]{3,2,1,0:T(8,128)S(1)} %get-tuple-element.91), channel_id=1, source_target_pairs={{0,8},{8,0},{16,24},{24,16},{32,40},{40,32},{48,56},{56,48},{64,72... | collective-permute-start | bytes 835592 | tf_op jit(solution)/shard_map/ppermute | solution.py:69
  53.8 5.6 %collective-permute-start.15 = (f32[2,136,128]{2,1,0:T(8,128)S(1)}, f32[2,136,128]{2,1,0:T(8,128)S(1)}, u32[]{:S(2)}, u32[]{:S(2)}) collective-permute-start(f32[2,136,128]{2,1,0:T(8,128)S(1)} %get-tuple-element.89), channel_id=1, source_target_pairs={{0,192},{8,200},{16,208},{24,216},{32,224},{40,232},{48,240},{56,2... | collective-permute-start | bytes 417800 | tf_op jit(solution)/shard_map/ppermute | solution.py:69
  56.2 6.0 %collective-permute-start.16 = (f32[2,136,128]{2,1,0:T(8,128)S(1)}, f32[2,136,128]{2,1,0:T(8,128)S(1)}, u32[]{:S(2)}, u32[]{:S(2)}) collective-permute-start(f32[2,136,128]{2,1,0:T(8,128)S(1)} %get-tuple-element.88.own_ref), channel_id=1, source_target_pairs={{0,128},{8,136},{16,144},{24,152},{32,160},{40,168},{48,176},{56,1... | collective-permute-start | bytes 417800 | tf_op jit(solution)/shard_map/ppermute | solution.py:69
  56.7 9.6 %collective-permute-start.17 = (f32[2,136,128]{2,1,0:T(8,128)S(1)}, f32[2,136,128]{2,1,0:T(8,128)S(1)}, u32[]{:S(2)}, u32[]{:S(2)}) collective-permute-start(f32[2,136,128]{2,1,0:T(8,128)S(1)} %get-tuple-element.88.own_ref), channel_id=1, source_target_pairs={{0,64},{8,72},{16,80},{24,88},{32,96},{40,104},{48,112},{56,120},{... | collective-permute-start | bytes 417800 | tf_op jit(solution)/shard_map/ppermute | solution.py:69
  66.5 6.2 %collective-permute-start.19 = (f32[2,136,128]{2,1,0:T(8,128)S(1)}, f32[2,136,128]{2,1,0:T(8,128)S(1)}, u32[]{:S(2)}, u32[]{:S(2)}) collective-permute-start(f32[2,136,128]{2,1,0:T(8,128)S(1)} %get-tuple-element.94), channel_id=1, source_target_pairs={{0,48},{8,56},{16,0},{24,8},{32,16},{40,24},{48,32},{56,40},{64,11... | collective-permute-start | bytes 417800 | tf_op jit(solution)/shard_map/ppermute | solution.py:69
  68.5 6.0 %collective-permute-start.20 = (f32[2,136,128]{2,1,0:T(8,128)S(1)}, f32[2,136,128]{2,1,0:T(8,128)S(1)}, u32[]{:S(2)}, u32[]{:S(2)}) collective-permute-start(f32[2,136,128]{2,1,0:T(8,128)S(1)} %get-tuple-element.95), channel_id=1, source_target_pairs={{0,32},{8,40},{16,48},{24,56},{32,0},{40,8},{48,16},{56,24},{64,96... | collective-permute-start | bytes 417800 | tf_op jit(solution)/shard_map/ppermute | solution.py:69
  69.3 9.3 %collective-permute-start.21 = (f32[2,136,128]{2,1,0:T(8,128)S(1)}, f32[2,136,128]{2,1,0:T(8,128)S(1)}, u32[]{:S(2)}, u32[]{:S(2)}) collective-permute-start(f32[2,136,128]{2,1,0:T(8,128)S(1)} %get-tuple-element.96), channel_id=1, source_target_pairs={{0,16},{8,24},{16,32},{24,40},{32,48},{40,56},{48,0},{56,8},{64,80... | collective-permute-start | bytes 417800 | tf_op jit(solution)/shard_map/ppermute | solution.py:69
  69.5 13.8 %collective-permute-start.23 = (f32[4,128,128]{2,1,0:T(8,128)S(1)}, f32[4,128,128]{2,1,0:T(8,128)S(1)}, u32[]{:S(2)}, u32[]{:S(2)}) collective-permute-start(f32[4,128,128]{2,1,0:T(8,128)S(1)} %get-tuple-element.98), channel_id=1, source_target_pairs={{8,0},{24,16},{40,32},{56,48},{72,64},{88,80},{104,96},{120,112},{... | collective-permute-start | bytes 786440 | tf_op jit(solution)/shard_map/ppermute | solution.py:69
  78.6 4.6 %collective-permute-start.22 = (f32[2,128,128]{2,1,0:T(8,128)S(1)}, f32[2,128,128]{2,1,0:T(8,128)S(1)}, u32[]{:S(2)}, u32[]{:S(2)}) collective-permute-start(f32[2,128,128]{2,1,0:T(8,128)S(1)} %get-tuple-element.97.half_ref), channel_id=1, source_target_pairs={{0,8},{8,0},{16,24},{24,16},{32,40},{40,32},{48,56},{56,48},{64,72... | collective-permute-start | bytes 393224 | tf_op jit(solution)/shard_map/ppermute | solution.py:69

commit v3 on v2

--- a/solution.py
+++ b/solution.py
@@ -10,7 +10,6 @@
 HEAD_DIM = 128
 TOTAL = HEADS * HEAD_DIM
 EPSILON = 1e-05
-HIGH = lax.Precision.HIGHEST
 F32 = jnp.float32
 BF16 = jnp.bfloat16
 
@@ -317,13 +316,15 @@
     g_ref, scale_ref, keep_ref, send_ref,
 ):
     x, _, core = place()
-    ones = jnp.ones((8, HEAD_DIM), F32)
     sums = (sums_ref[...] + three_ref[...]) + (two_ref[...] + one_ref[...])
-    sums = jnp.concatenate([sums, jnp.zeros_like(sums)], axis=0)
-    row = iotas((8, HEAD_DIM))[0]
-    wide = [dot(jnp.where(row == i, sums, 0.0), ones, TN, HIGH) for i in range(4)]
-    squares = jnp.concatenate(wide[0:2], axis=0)
-    crosses = jnp.concatenate(wide[2:4], axis=0)
+    first = sums.astype(BF16).astype(F32)
+    second = (sums - first).astype(BF16).astype(F32)
+    parts = jnp.concatenate([first, second, sums - first - second, jnp.zeros_like(sums)], axis=0).astype(BF16)
+    row, column = iotas((16, 4 * HEAD_DIM))
+    chosen = ((row < 12) & (lax.rem(row, 4) == column // HEAD_DIM)).astype(F32).astype(BF16)
+    wide = dot(parts, chosen, TN)
+    squares = jnp.concatenate([wide[:, 0:HEAD_DIM], wide[:, HEAD_DIM : 2 * HEAD_DIM]], axis=0)
+    crosses = jnp.concatenate([wide[:, 2 * HEAD_DIM : 3 * HEAD_DIM], wide[:, 3 * HEAD_DIM :]], axis=0)
     inverse = lax.rsqrt(squares * (1.0 / TOTAL) + EPSILON)
     pull = inverse * inverse * inverse * crosses * (1.0 / TOTAL)
     scale_ref[0] = inverse
@@ -489,11 +490,11 @@
         slot = head % 2
         half = jnp.where(core == head // 2, half_ref[slot], other_ref[slot])
         carry = jnp.exp(first_ref[0, HEAD_DIM + 4 + head : HEAD_DIM + 5 + head, :])
-        high, low = split(jnp.where(even, carry * half + zeroth_ref[head], half))
+        state = jnp.where(even, carry * half + zeroth_ref[head], half).astype(BF16)
         tail = cols_ref[:, 24 + head : 25 + head]
         k, v = k_ref[head], v_ref[head]
-        out_k_ref[head] = (grad_k_ref[head] + tail * (dot(v, high, NT) + dot(v, low, NT))).astype(BF16)
-        out_v_ref[head] = (grad_v_ref[head] + tail * (dot(k, high, NN) + dot(k, low, NN))).astype(BF16)
+        out_k_ref[head] = (grad_k_ref[head] + tail * dot(v, state, NT)).astype(BF16)
+        out_v_ref[head] = (grad_v_ref[head] + tail * dot(k, state, NN)).astype(BF16)
 
 
 def call(kernel, outs, *args, scratch=(), flops=0, hbm=(), limit=12):

time: 84.7 us -> 84.3 us (level)
  no operation moved by 1% of the time
where the time goes in v3:
time: 84.3 us; the launch traced here: 84.2 us
  starting transfers between devices  40.6 us (48%)
  waiting for transfers between devices  27.2 us (32%)
  Pallas kernels  15.5 us (18%)
    ppermute x20, starting transfers between devices, send(): return lax.ppermute(array, 'seq', pairs)  30.1 us
    ppermute x20, waiting for transfers between devices, send(): return lax.ppermute(array, 'seq', pairs)  25.1 us
    pallas_call x15, Pallas kernels, call(): pl.pallas_call(kernel, out_shape=shapes, in_specs=[pl.BlockSpec(memory_sp...  15.5 us
    ppermute x4, starting transfers between devices, along_z(): return lax.ppermute(array, 'head', pairs)  10.5 us
    ppermute x4, waiting for transfers between devices, along_z(): return lax.ppermute(array, 'head', pairs)  2.14 us
  transfers between devices with their start and end apart: 24, of which 15 were waited for; matrix products, arithmetic and copies ran while one was open for 0% of the time, Pallas kernels for 11%

profile of v3, /device:TPU:1, one launch (start us, length us, event | category | flops | bytes accessed | tf_op | source)
XLA Modules:
  0.0 84.2 jit_solution(8679354881351769423)
XLA Ops:
  0.7 2.4 %shard_map.135 = (f32[2,136,128]{2,1,0:T(8,128)S(1)}, f32[2,136,128]{2,1,0:T(8,128)S(1)}, f32[4,256]{1,0:T(4,128)S(1)}) custom-call(f32[4,256]{1,0:T(4,128)} %decay_hbm.1, bf16[4,256,128]{2,1,0:T(8,128)(2,1)} %k_ref.5, bf16[4,256,128]{2,1,0:T(8,128)(2,1)} %v_ref.5), custom_call_target="tpu_custom_call" | custom-call | bytes 811008 | tf_op jit(solution)/shard_map/pallas_call | solution.py:505
  3.1 3.3 %collective-permute-start = (f32[2,136,128]{2,1,0:T(8,128)S(1)}, f32[2,136,128]{2,1,0:T(8,128)S(1)}, u32[]{:S(2)}, u32[]{:S(2)}) collective-permute-start(f32[2,136,128]{2,1,0:T(8,128)S(1)} %get-tuple-element.61), channel_id=1, source_target_pairs={{0,8},{8,0},{16,24},{24,16},{32,40},{40,32},{48,56},{56,48},{64,72... | collective-permute-start | bytes 417800 | tf_op jit(solution)/shard_map/ppermute | solution.py:68
  7.6 2.2 %collective-permute-start.2 = (f32[2,136,128]{2,1,0:T(8,128)S(1)}, f32[2,136,128]{2,1,0:T(8,128)S(1)}, u32[]{:S(2)}, u32[]{:S(2)}) collective-permute-start(f32[2,136,128]{2,1,0:T(8,128)S(1)} %shard_map.137.own_ref), channel_id=1, source_target_pairs={{0,32},{8,40},{16,48},{24,56},{32,0},{40,8},{48,16},{56,24},{64,96... | collective-permute-start | bytes 417800 | tf_op jit(solution)/shard_map/ppermute | solution.py:68
  9.8 1.1 %collective-permute-start.3 = (f32[2,136,128]{2,1,0:T(8,128)S(1)}, f32[2,136,128]{2,1,0:T(8,128)S(1)}, u32[]{:S(2)}, u32[]{:S(2)}) collective-permute-start(f32[2,136,128]{2,1,0:T(8,128)S(1)} %shard_map.137.own_ref), channel_id=1, source_target_pairs={{0,48},{8,56},{16,0},{24,8},{32,16},{40,24},{48,32},{56,40},{64,11... | collective-permute-start | bytes 417800 | tf_op jit(solution)/shard_map/ppermute | solution.py:68
  10.8 3.3 %collective-permute-done.1.one_ref = f32[2,136,128]{2,1,0:T(8,128)S(1)} collective-permute-done((f32[2,136,128]{2,1,0:T(8,128)S(1)}, f32[2,136,128]{2,1,0:T(8,128)S(1)}, u32[]{:S(2)}, u32[]{:S(2)}) %collective-permute-start.1) | collective-permute-done | bytes 139296 | tf_op jit(solution)/shard_map/ppermute | solution.py:68
  14.1 2.1 %collective-permute-done.2.two_ref = f32[2,136,128]{2,1,0:T(8,128)S(1)} collective-permute-done((f32[2,136,128]{2,1,0:T(8,128)S(1)}, f32[2,136,128]{2,1,0:T(8,128)S(1)}, u32[]{:S(2)}, u32[]{:S(2)}) %collective-permute-start.2) | collective-permute-done | bytes 139296 | tf_op jit(solution)/shard_map/ppermute | solution.py:68
  17.5 2.5 %collective-permute-start.7 = (f32[2,136,128]{2,1,0:T(8,128)S(1)}, f32[2,136,128]{2,1,0:T(8,128)S(1)}, u32[]{:S(2)}, u32[]{:S(2)}) collective-permute-start(f32[2,136,128]{2,1,0:T(8,128)S(1)} %get-tuple-element.68.own_ref), channel_id=1, source_target_pairs={{0,128},{8,136},{16,144},{24,152},{32,160},{40,168},{48,176},{56,1... | collective-permute-start | bytes 417800 | tf_op jit(solution)/shard_map/ppermute | solution.py:68
  20.0 1.1 %collective-permute-start.8 = (f32[2,136,128]{2,1,0:T(8,128)S(1)}, f32[2,136,128]{2,1,0:T(8,128)S(1)}, u32[]{:S(2)}, u32[]{:S(2)}) collective-permute-start(f32[2,136,128]{2,1,0:T(8,128)S(1)} %get-tuple-element.68.own_ref), channel_id=1, source_target_pairs={{0,192},{8,200},{16,208},{24,216},{32,224},{40,232},{48,240},{56,2... | collective-permute-start | bytes 417800 | tf_op jit(solution)/shard_map/ppermute | solution.py:68
  21.1 2.1 %collective-permute-start.4 = (f32[2,2,136,128]{3,2,1,0:T(8,128)S(1)}, f32[2,2,136,128]{3,2,1,0:T(8,128)S(1)}, u32[]{:S(2)}, u32[]{:S(2)}) collective-permute-start(f32[2,2,136,128]{3,2,1,0:T(8,128)S(1)} %get-tuple-element.62.own_ref), channel_id=1, source_target_pairs={{0,8},{8,0},{16,24},{24,16},{32,40},{40,32},{48,56},{56,48},{64,72... | collective-permute-start | bytes 835592 | tf_op jit(solution)/shard_map/ppermute | solution.py:68
  23.2 2.0 %collective-permute-done.7.two_ref = f32[2,136,128]{2,1,0:T(8,128)S(1)} collective-permute-done((f32[2,136,128]{2,1,0:T(8,128)S(1)}, f32[2,136,128]{2,1,0:T(8,128)S(1)}, u32[]{:S(2)}, u32[]{:S(2)}) %collective-permute-start.7) | collective-permute-done | bytes 139296 | tf_op jit(solution)/shard_map/ppermute | solution.py:68
  25.4 2.7 %collective-permute-start.9 = (f32[2,2,136,128]{3,2,1,0:T(8,128)S(1)}, f32[2,2,136,128]{3,2,1,0:T(8,128)S(1)}, u32[]{:S(2)}, u32[]{:S(2)}) collective-permute-start(f32[2,2,136,128]{3,2,1,0:T(8,128)S(1)} %get-tuple-element.70.own_ref), channel_id=1, source_target_pairs={{0,8},{8,0},{16,24},{24,16},{32,40},{40,32},{48,56},{56,48},{64,72... | collective-permute-start | bytes 835592 | tf_op jit(solution)/shard_map/ppermute | solution.py:68
  28.1 1.3 %collective-permute-start.5 = (f32[2,136,128]{2,1,0:T(8,128)S(1)}, f32[2,136,128]{2,1,0:T(8,128)S(1)}, u32[]{:S(2)}, u32[]{:S(2)}) collective-permute-start(f32[2,136,128]{2,1,0:T(8,128)S(1)} %get-tuple-element.60.keep_ref), channel_id=1, source_target_pairs={{0,8},{16,24},{32,40},{48,56},{64,72},{80,88},{96,104},{112,120},{... | collective-permute-start | bytes 417800 | tf_op jit(solution)/shard_map/ppermute | solution.py:68
  29.5 1.0 %shard_map.136 = (f32[4,256,128]{2,1,0:T(8,128)S(1)}, bf16[4,256,256]{2,1,0:T(8,128)(2,1)S(1)}, f32[4,256,256]{2,1,0:T(8,128)S(1)}, f32[4,256,256]{2,1,0:T(8,128)S(1)}, f32[256,128]{1,0:T(8,128)S(1)}) custom-call(bf16[4,256,128]{2,1,0:T(8,128)(2,1)S(1)} %copy-done.2, bf16[4,256,128]{2,1,0:T(8,128)(2,1)S(1)} %copy-done, bf16[4,256,128]{2,1,0:T(8,128)(2,1)S(1)} %copy-done.1, ...), custom_call_target="tpu_custom_call" | custom-call | flops 1000000000 | bytes 4153344 | tf_op jit(solution)/shard_map/pallas_call | solution.py:505
  31.4 1.3 %shard_map.139 = (f32[4,256,128]{2,1,0:T(8,128)S(1)}, f32[4,256,128]{2,1,0:T(8,128)S(1)}, f32[4,256,128]{2,1,0:T(8,128)S(1)}, bf16[4,128,384]{2,1,0:T(8,128)(2,1...) custom-call(bf16[4,256,128]{2,1,0:T(8,128)(2,1)S(1)} %copy-done.2, ...), custom_call_target="tpu_custom_call" | custom-call | flops 1000000000 | bytes 7276544 | tf_op jit(solution)/shard_map/pallas_call | solution.py:505
  32.7 1.1 %shard_map.141 = (f32[4,256,128]{2,1,0:T(8,128)S(1)}, f32[4,128]{1,0:T(4,128)S(1)}, bf16[4,128,256]{2,1,0:T(8,128)(2,1)S(1)}, bf16[4,128,256]{2,1,0:T(8,128)(2,1)S(1)}, f32[4,8,128]{2,1,0:T(8,128)S(1)}) custom-call(bf16[4,256,768]{2,1,0:T(8,128)(2,1)S(1)} %get-tuple-element.64.scaled_ref, f32[4,256,128]{2,1,0:T(8,128)S(1)} %get-tuple-element.65.near_ref, ...), custom_call_target="tpu_custom_call" | custom-call | bytes 4786176 | tf_op jit(solution)/shard_map/pallas_call | solution.py:505
  33.9 1.3 %collective-permute-start.10 = (f32[4,128]{1,0:T(4,128)S(1)}, f32[4,128]{1,0:T(4,128)S(1)}, u32[]{:S(2)}, u32[]{:S(2)}) collective-permute-start(f32[4,128]{1,0:T(4,128)S(1)} %get-tuple-element.74.a_ref), channel_id=1, source_target_pairs={{0,1},{1,0},{2,3},{3,2},{4,5},{5,4},{6,7},{7,6},{8,9},{9,8},{10,11... | collective-permute-start | bytes 6152 | tf_op jit(solution)/shard_map/ppermute | solution.py:56
  35.2 1.1 %collective-permute-done.10.b_ref = f32[4,128]{1,0:T(4,128)S(1)} collective-permute-done((f32[4,128]{1,0:T(4,128)S(1)}, f32[4,128]{1,0:T(4,128)S(1)}, u32[]{:S(2)}, u32[]{:S(2)}) %collective-permute-start.10) | collective-permute-done | bytes 2080 | tf_op jit(solution)/shard_map/ppermute | solution.py:56
  36.3 6.1 %collective-permute-start.11 = (f32[4,128]{1,0:T(4,128)S(1)}, f32[4,128]{1,0:T(4,128)S(1)}, u32[]{:S(2)}, u32[]{:S(2)}) collective-permute-start(f32[4,128]{1,0:T(4,128)S(1)} %shard_map.142.sums_ref), channel_id=1, source_target_pairs={{1,4},{4,1},{3,6},{6,3},{5,0},{0,5},{7,2},{2,7},{9,12},{12,9},{11,... | collective-permute-start | bytes 6152 | tf_op jit(solution)/shard_map/ppermute | solution.py:56
  42.7 2.9 %collective-permute-start.13 = (f32[4,128]{1,0:T(4,128)S(1)}, f32[4,128]{1,0:T(4,128)S(1)}, u32[]{:S(2)}, u32[]{:S(2)}) collective-permute-start(f32[4,128]{1,0:T(4,128)S(1)} %shard_map.142.sums_ref), channel_id=1, source_target_pairs={{1,2},{2,1},{3,4},{4,3},{5,6},{6,5},{7,0},{0,7},{9,10},{10,9},{11,... | collective-permute-start | bytes 6152 | tf_op jit(solution)/shard_map/ppermute | solution.py:56
  46.6 1.2 %shard_map.143 = (bf16[4,256,128]{2,1,0:T(8,128)(2,1)S(1)}, f32[2,256,128]{2,1,0:T(8,128)S(1)}, f32[2,2,136,128]{3,2,1,0:T(8,128)S(1)}, f32[2,2,136,128]{3,2,1,0:T(8,128)S(1)}) custom-call(bf16[4,2,128,512]{3,2,1,0:T(8,128)(2,1)S(1)} %get-tuple-element.63.turned_ref, f32[4,256,128]{2,1,0:T(8,128)S(1)} %get-tuple-element.72.mixed_ref, ...), custom_call_target="tpu_custom_call" | custom-call | bytes 3989504 | tf_op jit(solution)/shard_map/pallas_call | solution.py:505
  47.8 3.1 %collective-permute-start.14 = (f32[2,2,136,128]{3,2,1,0:T(8,128)S(1)}, f32[2,2,136,128]{3,2,1,0:T(8,128)S(1)}, u32[]{:S(2)}, u32[]{:S(2)}) collective-permute-start(f32[2,2,136,128]{3,2,1,0:T(8,128)S(1)} %get-tuple-element.87), channel_id=1, source_target_pairs={{0,8},{8,0},{16,24},{24,16},{32,40},{40,32},{48,56},{56,48},{64,72... | collective-permute-start | bytes 835592 | tf_op jit(solution)/shard_map/ppermute | solution.py:68
  50.9 2.7 %shard_map.144 = (bf16[4,256,128]{2,1,0:T(8,128)(2,1)}, bf16[4,256,128]{2,1,0:T(8,128)(2,1)}, f32[2,2,136,128]{3,2,1,0:T(8,128)S(1)}, f32[2,2,136,128]{3,2,1,0:T(8,128)S(1)}, f32[4,128,128]{2,1,0:T(8,128)S(1)}) custom-call(bf16[4,256,128]{2,1,0:T(8,128)(2,1)S(1)} %copy-done.2, bf16[4,256,128]{2,1,0:T(8,128)(2,1)S(1)} %get-tuple-element.75.g_ref, ...), custom_call_target="tpu_custom_call" | custom-call | flops 1000000000 | bytes 3328000 | tf_op jit(solution)/shard_map/pallas_call | solution.py:505
  53.7 2.4 %collective-permute-start.15 = (f32[2,136,128]{2,1,0:T(8,128)S(1)}, f32[2,136,128]{2,1,0:T(8,128)S(1)}, u32[]{:S(2)}, u32[]{:S(2)}) collective-permute-start(f32[2,136,128]{2,1,0:T(8,128)S(1)} %get-tuple-element.89), channel_id=1, source_target_pairs={{0,192},{8,200},{16,208},{24,216},{32,224},{40,232},{48,240},{56,2... | collective-permute-start | bytes 417800 | tf_op jit(solution)/shard_map/ppermute | solution.py:68
  57.0 2.3 %collective-permute-done.15.one_ref = f32[2,136,128]{2,1,0:T(8,128)S(1)} collective-permute-done((f32[2,136,128]{2,1,0:T(8,128)S(1)}, f32[2,136,128]{2,1,0:T(8,128)S(1)}, u32[]{:S(2)}, u32[]{:S(2)}) %collective-permute-start.15) | collective-permute-done | bytes 139296 | tf_op jit(solution)/shard_map/ppermute | solution.py:68
  59.3 2.7 %collective-permute-done.16.two_ref = f32[2,136,128]{2,1,0:T(8,128)S(1)} collective-permute-done((f32[2,136,128]{2,1,0:T(8,128)S(1)}, f32[2,136,128]{2,1,0:T(8,128)S(1)}, u32[]{:S(2)}, u32[]{:S(2)}) %collective-permute-start.16) | collective-permute-done | bytes 139296 | tf_op jit(solution)/shard_map/ppermute | solution.py:68
  62.0 4.1 %collective-permute-done.17.three_ref = f32[2,136,128]{2,1,0:T(8,128)S(1)} collective-permute-done((f32[2,136,128]{2,1,0:T(8,128)S(1)}, f32[2,136,128]{2,1,0:T(8,128)S(1)}, u32[]{:S(2)}, u32[]{:S(2)}) %collective-permute-start.17) | collective-permute-done | bytes 139296 | tf_op jit(solution)/shard_map/ppermute | solution.py:68
  66.3 2.1 %collective-permute-start.19 = (f32[2,136,128]{2,1,0:T(8,128)S(1)}, f32[2,136,128]{2,1,0:T(8,128)S(1)}, u32[]{:S(2)}, u32[]{:S(2)}) collective-permute-start(f32[2,136,128]{2,1,0:T(8,128)S(1)} %get-tuple-element.94), channel_id=1, source_target_pairs={{0,48},{8,56},{16,0},{24,8},{32,16},{40,24},{48,32},{56,40},{64,11... | collective-permute-start | bytes 417800 | tf_op jit(solution)/shard_map/ppermute | solution.py:68
  69.3 3.2 %collective-permute-start.23 = (f32[4,128,128]{2,1,0:T(8,128)S(1)}, f32[4,128,128]{2,1,0:T(8,128)S(1)}, u32[]{:S(2)}, u32[]{:S(2)}) collective-permute-start(f32[4,128,128]{2,1,0:T(8,128)S(1)} %get-tuple-element.98), channel_id=1, source_target_pairs={{8,0},{24,16},{40,32},{56,48},{72,64},{88,80},{104,96},{120,112},{... | collective-permute-start | bytes 786440 | tf_op jit(solution)/shard_map/ppermute | solution.py:68
  72.5 1.8 %collective-permute-done.20.two_ref = f32[2,136,128]{2,1,0:T(8,128)S(1)} collective-permute-done((f32[2,136,128]{2,1,0:T(8,128)S(1)}, f32[2,136,128]{2,1,0:T(8,128)S(1)}, u32[]{:S(2)}, u32[]{:S(2)}) %collective-permute-start.20) | collective-permute-done | bytes 139296 | tf_op jit(solution)/shard_map/ppermute | solution.py:68
  74.3 4.1 %collective-permute-done.21.three_ref = f32[2,136,128]{2,1,0:T(8,128)S(1)} collective-permute-done((f32[2,136,128]{2,1,0:T(8,128)S(1)}, f32[2,136,128]{2,1,0:T(8,128)S(1)}, u32[]{:S(2)}, u32[]{:S(2)}) %collective-permute-start.21) | collective-permute-done | bytes 139296 | tf_op jit(solution)/shard_map/ppermute | solution.py:68
  79.1 4.0 %shard_map.145 = (bf16[4,256,128]{2,1,0:T(8,128)(2,1)}, f32[4,256,128]{2,1,0:T(8,128)S(1)}, f32[4,256,128]{2,1,0:T(8,128)S(1)}, f32[21,4,256]{2,1,0:T(4,128)}) custom-call(bf16[4,256,128]{2,1,0:T(8,128)(2,1)S(1)} %copy-done.2, bf16[4,256,128]{2,1,0:T(8,128)(2,1)S(1)} %copy-done, bf16[4,256,128]{2,1,0:T(8,128)(2,1)S(1)} %copy-done.1, ...), custom_call_target="tpu_custom_call" | custom-call | flops 1000000000 | bytes 6512640 | tf_op jit(solution)/shard_map/pallas_call | solution.py:505
  83.1 1.1 %shard_map.149 = (bf16[4,256,128]{2,1,0:T(8,128)(2,1)}, bf16[4,256,128]{2,1,0:T(8,128)(2,1)}, f32[4,128]{1,0:T(4,128)}) custom-call(bf16[4,256,128]{2,1,0:T(8,128)(2,1)S(1)} %copy-done, bf16[4,256,128]{2,1,0:T(8,128)(2,1)S(1)} %copy-done.1, f32[256,128]{1,0:T(8,128)S(1)} %get-tuple-element.59.cols_ref, f32[2,128,128]{2,1,0:T(8,128)S(1)} %get-tuple-element.97.half_ref, ...), custom_call_target="tpu_custom_call" | custom-call | bytes 2895872 | tf_op jit(solution)/shard_map/pallas_call | solution.py:505
  (45 shorter events, 7.5 us)
Async XLA Ops:
  0.6 28.8 %copy-start = (bf16[4,256,128]{2,1,0:T(8,128)(2,1)S(1)}, bf16[4,256,128]{2,1,0:T(8,128)(2,1)}, u32[]{:S(2)}) copy-start(bf16[4,256,128]{2,1,0:T(8,128)(2,1)} %k_ref.5) | copy-start | bytes 786436
  0.6 28.8 %copy-start.1 = (bf16[4,256,128]{2,1,0:T(8,128)(2,1)S(1)}, bf16[4,256,128]{2,1,0:T(8,128)(2,1)}, u32[]{:S(2)}) copy-start(bf16[4,256,128]{2,1,0:T(8,128)(2,1)} %v_ref.5) | copy-start | bytes 786436
  0.7 28.8 %copy-start.2 = (bf16[4,256,128]{2,1,0:T(8,128)(2,1)S(1)}, bf16[4,256,128]{2,1,0:T(8,128)(2,1)}, u32[]{:S(2)}) copy-start(bf16[4,256,128]{2,1,0:T(8,128)(2,1)} %q_ref.7) | copy-start | bytes 786436
  0.7 28.8 %copy-start.5 = (f32[4,21,256]{2,0,1:T(4,128)S(1)}, f32[4,21,256]{2,0,1:T(4,128)}, u32[]{:S(2)}) copy-start(f32[4,21,256]{2,0,1:T(4,128)} %param.12) | copy-start | bytes 258052
  3.1 4.3 %collective-permute-start = (f32[2,136,128]{2,1,0:T(8,128)S(1)}, f32[2,136,128]{2,1,0:T(8,128)S(1)}, u32[]{:S(2)}, u32[]{:S(2)}) collective-permute-start(f32[2,136,128]{2,1,0:T(8,128)S(1)} %get-tuple-element.61), channel_id=1, source_target_pairs={{0,8},{8,0},{16,24},{24,16},{32,40},{40,32},{48,56},{56,48},{64,72... | collective-permute-start | bytes 417800 | tf_op jit(solution)/shard_map/ppermute | solution.py:68
  7.5 6.6 %collective-permute-start.1 = (f32[2,136,128]{2,1,0:T(8,128)S(1)}, f32[2,136,128]{2,1,0:T(8,128)S(1)}, u32[]{:S(2)}, u32[]{:S(2)}) collective-permute-start(f32[2,136,128]{2,1,0:T(8,128)S(1)} %shard_map.137.own_ref), channel_id=1, source_target_pairs={{0,16},{8,24},{16,32},{24,40},{32,48},{40,56},{48,0},{56,8},{64,80... | collective-permute-start | bytes 417800 | tf_op jit(solution)/shard_map/ppermute | solution.py:68
  7.6 8.6 %collective-permute-start.2 = (f32[2,136,128]{2,1,0:T(8,128)S(1)}, f32[2,136,128]{2,1,0:T(8,128)S(1)}, u32[]{:S(2)}, u32[]{:S(2)}) collective-permute-start(f32[2,136,128]{2,1,0:T(8,128)S(1)} %shard_map.137.own_ref), channel_id=1, source_target_pairs={{0,32},{8,40},{16,48},{24,56},{32,0},{40,8},{48,16},{56,24},{64,96... | collective-permute-start | bytes 417800 | tf_op jit(solution)/shard_map/ppermute | solution.py:68
  9.8 7.2 %collective-permute-start.3 = (f32[2,136,128]{2,1,0:T(8,128)S(1)}, f32[2,136,128]{2,1,0:T(8,128)S(1)}, u32[]{:S(2)}, u32[]{:S(2)}) collective-permute-start(f32[2,136,128]{2,1,0:T(8,128)S(1)} %shard_map.137.own_ref), channel_id=1, source_target_pairs={{0,48},{8,56},{16,0},{24,8},{32,16},{40,24},{48,32},{56,40},{64,11... | collective-permute-start | bytes 417800 | tf_op jit(solution)/shard_map/ppermute | solution.py:68
  17.0 6.2 %collective-permute-start.6 = (f32[2,136,128]{2,1,0:T(8,128)S(1)}, f32[2,136,128]{2,1,0:T(8,128)S(1)}, u32[]{:S(2)}, u32[]{:S(2)}) collective-permute-start(f32[2,136,128]{2,1,0:T(8,128)S(1)} %get-tuple-element.68.own_ref), channel_id=1, source_target_pairs={{0,64},{8,72},{16,80},{24,88},{32,96},{40,104},{48,112},{56,120},{... | collective-permute-start | bytes 417800 | tf_op jit(solution)/shard_map/ppermute | solution.py:68
  17.5 7.7 %collective-permute-start.7 = (f32[2,136,128]{2,1,0:T(8,128)S(1)}, f32[2,136,128]{2,1,0:T(8,128)S(1)}, u32[]{:S(2)}, u32[]{:S(2)}) collective-permute-start(f32[2,136,128]{2,1,0:T(8,128)S(1)} %get-tuple-element.68.own_ref), channel_id=1, source_target_pairs={{0,128},{8,136},{16,144},{24,152},{32,160},{40,168},{48,176},{56,1... | collective-permute-start | bytes 417800 | tf_op jit(solution)/shard_map/ppermute | solution.py:68
  20.0 5.3 %collective-permute-start.8 = (f32[2,136,128]{2,1,0:T(8,128)S(1)}, f32[2,136,128]{2,1,0:T(8,128)S(1)}, u32[]{:S(2)}, u32[]{:S(2)}) collective-permute-start(f32[2,136,128]{2,1,0:T(8,128)S(1)} %get-tuple-element.68.own_ref), channel_id=1, source_target_pairs={{0,192},{8,200},{16,208},{24,216},{32,224},{40,232},{48,240},{56,2... | collective-permute-start | bytes 417800 | tf_op jit(solution)/shard_map/ppermute | solution.py:68
  21.1 10.2 %collective-permute-start.4 = (f32[2,2,136,128]{3,2,1,0:T(8,128)S(1)}, f32[2,2,136,128]{3,2,1,0:T(8,128)S(1)}, u32[]{:S(2)}, u32[]{:S(2)}) collective-permute-start(f32[2,2,136,128]{3,2,1,0:T(8,128)S(1)} %get-tuple-element.62.own_ref), channel_id=1, source_target_pairs={{0,8},{8,0},{16,24},{24,16},{32,40},{40,32},{48,56},{56,48},{64,72... | collective-permute-start | bytes 835592 | tf_op jit(solution)/shard_map/ppermute | solution.py:68
  25.4 7.3 %collective-permute-start.9 = (f32[2,2,136,128]{3,2,1,0:T(8,128)S(1)}, f32[2,2,136,128]{3,2,1,0:T(8,128)S(1)}, u32[]{:S(2)}, u32[]{:S(2)}) collective-permute-start(f32[2,2,136,128]{3,2,1,0:T(8,128)S(1)} %get-tuple-element.70.own_ref), channel_id=1, source_target_pairs={{0,8},{8,0},{16,24},{24,16},{32,40},{40,32},{48,56},{56,48},{64,72... | collective-permute-start | bytes 835592 | tf_op jit(solution)/shard_map/ppermute | solution.py:68
  28.1 3.2 %collective-permute-start.5 = (f32[2,136,128]{2,1,0:T(8,128)S(1)}, f32[2,136,128]{2,1,0:T(8,128)S(1)}, u32[]{:S(2)}, u32[]{:S(2)}) collective-permute-start(f32[2,136,128]{2,1,0:T(8,128)S(1)} %get-tuple-element.60.keep_ref), channel_id=1, source_target_pairs={{0,8},{16,24},{32,40},{48,56},{64,72},{80,88},{96,104},{112,120},{... | collective-permute-start | bytes 417800 | tf_op jit(solution)/shard_map/ppermute | solution.py:68
  29.5 1.9 %copy-start.3 = (bf16[4,256,128]{2,1,0:T(8,128)(2,1)S(1)}, bf16[4,256,128]{2,1,0:T(8,128)(2,1)}, u32[]{:S(2)}) copy-start(bf16[4,256,128]{2,1,0:T(8,128)(2,1)} %grad_ref.5) | copy-start | bytes 786436
  29.5 1.9 %copy-start.4 = (bf16[4,256,128]{2,1,0:T(8,128)(2,1)S(1)}, bf16[4,256,128]{2,1,0:T(8,128)(2,1)}, u32[]{:S(2)}) copy-start(bf16[4,256,128]{2,1,0:T(8,128)(2,1)} %gate_ref.3) | copy-start | bytes 786436
  29.5 1.9 %copy-start.6 = (f32[4,128]{1,0:T(4,128)S(1)}, f32[4,128]{1,0:T(4,128)}, u32[]{:S(2)}) copy-start(f32[4,128]{1,0:T(4,128)} %gain_ref.3) | copy-start | bytes 6148
  33.9 2.4 %collective-permute-start.10 = (f32[4,128]{1,0:T(4,128)S(1)}, f32[4,128]{1,0:T(4,128)S(1)}, u32[]{:S(2)}, u32[]{:S(2)}) collective-permute-start(f32[4,128]{1,0:T(4,128)S(1)} %get-tuple-element.74.a_ref), channel_id=1, source_target_pairs={{0,1},{1,0},{2,3},{3,2},{4,5},{5,4},{6,7},{7,6},{8,9},{9,8},{10,11... | collective-permute-start | bytes 6152 | tf_op jit(solution)/shard_map/ppermute | solution.py:56
  36.3 9.2 %collective-permute-start.11 = (f32[4,128]{1,0:T(4,128)S(1)}, f32[4,128]{1,0:T(4,128)S(1)}, u32[]{:S(2)}, u32[]{:S(2)}) collective-permute-start(f32[4,128]{1,0:T(4,128)S(1)} %shard_map.142.sums_ref), channel_id=1, source_target_pairs={{1,4},{4,1},{3,6},{6,3},{5,0},{0,5},{7,2},{2,7},{9,12},{12,9},{11,... | collective-permute-start | bytes 6152 | tf_op jit(solution)/shard_map/ppermute | solution.py:56
  42.4 3.3 %collective-permute-start.12 = (f32[4,128]{1,0:T(4,128)S(1)}, f32[4,128]{1,0:T(4,128)S(1)}, u32[]{:S(2)}, u32[]{:S(2)}) collective-permute-start(f32[4,128]{1,0:T(4,128)S(1)} %shard_map.142.sums_ref), channel_id=1, source_target_pairs={{0,6},{1,3},{2,0},{3,5},{4,2},{5,7},{6,4},{7,1},{8,14},{9,11},{10,... | collective-permute-start | bytes 6152 | tf_op jit(solution)/shard_map/ppermute | solution.py:56
  42.7 3.9 %collective-permute-start.13 = (f32[4,128]{1,0:T(4,128)S(1)}, f32[4,128]{1,0:T(4,128)S(1)}, u32[]{:S(2)}, u32[]{:S(2)}) collective-permute-start(f32[4,128]{1,0:T(4,128)S(1)} %shard_map.142.sums_ref), channel_id=1, source_target_pairs={{1,2},{2,1},{3,4},{4,3},{5,6},{6,5},{7,0},{0,7},{9,10},{10,9},{11,... | collective-permute-start | bytes 6152 | tf_op jit(solution)/shard_map/ppermute | solution.py:56
  47.8 5.8 %collective-permute-start.14 = (f32[2,2,136,128]{3,2,1,0:T(8,128)S(1)}, f32[2,2,136,128]{3,2,1,0:T(8,128)S(1)}, u32[]{:S(2)}, u32[]{:S(2)}) collective-permute-start(f32[2,2,136,128]{3,2,1,0:T(8,128)S(1)} %get-tuple-element.87), channel_id=1, source_target_pairs={{0,8},{8,0},{16,24},{24,16},{32,40},{40,32},{48,56},{56,48},{64,72... | collective-permute-start | bytes 835592 | tf_op jit(solution)/shard_map/ppermute | solution.py:68
  53.6 3.4 %collective-permute-start.18 = (f32[2,2,136,128]{3,2,1,0:T(8,128)S(1)}, f32[2,2,136,128]{3,2,1,0:T(8,128)S(1)}, u32[]{:S(2)}, u32[]{:S(2)}) collective-permute-start(f32[2,2,136,128]{3,2,1,0:T(8,128)S(1)} %get-tuple-element.91), channel_id=1, source_target_pairs={{0,8},{8,0},{16,24},{24,16},{32,40},{40,32},{48,56},{56,48},{64,72... | collective-permute-start | bytes 835592 | tf_op jit(solution)/shard_map/ppermute | solution.py:68
  53.7 5.6 %collective-permute-start.15 = (f32[2,136,128]{2,1,0:T(8,128)S(1)}, f32[2,136,128]{2,1,0:T(8,128)S(1)}, u32[]{:S(2)}, u32[]{:S(2)}) collective-permute-start(f32[2,136,128]{2,1,0:T(8,128)S(1)} %get-tuple-element.89), channel_id=1, source_target_pairs={{0,192},{8,200},{16,208},{24,216},{32,224},{40,232},{48,240},{56,2... | collective-permute-start | bytes 417800 | tf_op jit(solution)/shard_map/ppermute | solution.py:68
  56.1 6.0 %collective-permute-start.16 = (f32[2,136,128]{2,1,0:T(8,128)S(1)}, f32[2,136,128]{2,1,0:T(8,128)S(1)}, u32[]{:S(2)}, u32[]{:S(2)}) collective-permute-start(f32[2,136,128]{2,1,0:T(8,128)S(1)} %get-tuple-element.88.own_ref), channel_id=1, source_target_pairs={{0,128},{8,136},{16,144},{24,152},{32,160},{40,168},{48,176},{56,1... | collective-permute-start | bytes 417800 | tf_op jit(solution)/shard_map/ppermute | solution.py:68
  56.6 9.6 %collective-permute-start.17 = (f32[2,136,128]{2,1,0:T(8,128)S(1)}, f32[2,136,128]{2,1,0:T(8,128)S(1)}, u32[]{:S(2)}, u32[]{:S(2)}) collective-permute-start(f32[2,136,128]{2,1,0:T(8,128)S(1)} %get-tuple-element.88.own_ref), channel_id=1, source_target_pairs={{0,64},{8,72},{16,80},{24,88},{32,96},{40,104},{48,112},{56,120},{... | collective-permute-start | bytes 417800 | tf_op jit(solution)/shard_map/ppermute | solution.py:68
  66.3 6.2 %collective-permute-start.19 = (f32[2,136,128]{2,1,0:T(8,128)S(1)}, f32[2,136,128]{2,1,0:T(8,128)S(1)}, u32[]{:S(2)}, u32[]{:S(2)}) collective-permute-start(f32[2,136,128]{2,1,0:T(8,128)S(1)} %get-tuple-element.94), channel_id=1, source_target_pairs={{0,48},{8,56},{16,0},{24,8},{32,16},{40,24},{48,32},{56,40},{64,11... | collective-permute-start | bytes 417800 | tf_op jit(solution)/shard_map/ppermute | solution.py:68
  68.4 6.0 %collective-permute-start.20 = (f32[2,136,128]{2,1,0:T(8,128)S(1)}, f32[2,136,128]{2,1,0:T(8,128)S(1)}, u32[]{:S(2)}, u32[]{:S(2)}) collective-permute-start(f32[2,136,128]{2,1,0:T(8,128)S(1)} %get-tuple-element.95), channel_id=1, source_target_pairs={{0,32},{8,40},{16,48},{24,56},{32,0},{40,8},{48,16},{56,24},{64,96... | collective-permute-start | bytes 417800 | tf_op jit(solution)/shard_map/ppermute | solution.py:68
  69.2 9.3 %collective-permute-start.21 = (f32[2,136,128]{2,1,0:T(8,128)S(1)}, f32[2,136,128]{2,1,0:T(8,128)S(1)}, u32[]{:S(2)}, u32[]{:S(2)}) collective-permute-start(f32[2,136,128]{2,1,0:T(8,128)S(1)} %get-tuple-element.96), channel_id=1, source_target_pairs={{0,16},{8,24},{16,32},{24,40},{32,48},{40,56},{48,0},{56,8},{64,80... | collective-permute-start | bytes 417800 | tf_op jit(solution)/shard_map/ppermute | solution.py:68
  69.3 13.8 %collective-permute-start.23 = (f32[4,128,128]{2,1,0:T(8,128)S(1)}, f32[4,128,128]{2,1,0:T(8,128)S(1)}, u32[]{:S(2)}, u32[]{:S(2)}) collective-permute-start(f32[4,128,128]{2,1,0:T(8,128)S(1)} %get-tuple-element.98), channel_id=1, source_target_pairs={{8,0},{24,16},{40,32},{56,48},{72,64},{88,80},{104,96},{120,112},{... | collective-permute-start | bytes 786440 | tf_op jit(solution)/shard_map/ppermute | solution.py:68
  78.5 4.6 %collective-permute-start.22 = (f32[2,128,128]{2,1,0:T(8,128)S(1)}, f32[2,128,128]{2,1,0:T(8,128)S(1)}, u32[]{:S(2)}, u32[]{:S(2)}) collective-permute-start(f32[2,128,128]{2,1,0:T(8,128)S(1)} %get-tuple-element.97.half_ref), channel_id=1, source_target_pairs={{0,8},{8,0},{16,24},{24,16},{32,40},{40,32},{48,56},{56,48},{64,72... | collective-permute-start | bytes 393224 | tf_op jit(solution)/shard_map/ppermute | solution.py:68

commit v4 on v3

--- a/solution.py
+++ b/solution.py
@@ -93,10 +93,10 @@
 def state_kernel(
     decay_hbm, k_hbm, v_hbm, keep_ref, send_ref, run_ref, decay_ref, k_ref, v_ref, rows_ref, sems
 ):
-    copies = [
-        pltpu.make_async_copy(source, to, sems.at[i])
-        for i, (source, to) in enumerate(((decay_hbm, decay_ref), (v_hbm, v_ref), (k_hbm, k_ref)))
-    ]
+    copies = [pltpu.make_async_copy(decay_hbm, decay_ref, sems.at[0])]
+    for head in range(LOCAL):
+        copies.append(pltpu.make_async_copy(v_hbm.at[head], v_ref.at[head], sems.at[1 + 2 * head]))
+        copies.append(pltpu.make_async_copy(k_hbm.at[head], k_ref.at[head], sems.at[2 + 2 * head]))
     for copy in copies:
         copy.start()
     core = place()[2]
@@ -115,9 +115,9 @@
     run_ref[...] = running
     rows_ref[0:4, :] = jnp.exp(running[:, WIDTH - 1 :] - running)
     tails = jnp.transpose(rows_ref[...])
-    for copy in copies[1:]:
-        copy.wait()
-    for head in range(LOCAL):
+    for head in range(LOCAL):
+        for copy in copies[1 + 2 * head : 3 + 2 * head]:
+            copy.wait()
         weighted = v_ref[head].astype(F32) * tails[:, head : head + 1]
         both = dot(k_ref[head], jnp.concatenate(split(weighted), axis=1), TN)
         state = both[:, 0:HEAD_DIM] + both[:, HEAD_DIM:]
@@ -527,7 +527,7 @@
         *(pltpu.with_memory_space_constraint(a, pltpu.HBM) for a in (log_decay, keys, values)),
         scratch=[
             pltpu.VMEM((LOCAL, WIDTH), F32), pltpu.VMEM(tokens, BF16), pltpu.VMEM(tokens, BF16),
-            pltpu.VMEM((16, WIDTH), F32), pltpu.SemaphoreType.DMA((3,)),
+            pltpu.VMEM((16, WIDTH), F32), pltpu.SemaphoreType.DMA((1 + 2 * LOCAL,)),
         ],
         hbm=(0, 1, 2),
     )

time: 84.3 us -> 84.4 us (level)
  no operation moved by 1% of the time
where the time goes in v4:
time: 84.4 us; the launch traced here: 84.2 us
  starting transfers between devices  40.6 us (48%)
  waiting for transfers between devices  27.2 us (32%)
  Pallas kernels  15.5 us (18%)
    ppermute x20, starting transfers between devices, send(): return lax.ppermute(array, 'seq', pairs)  30.1 us
    ppermute x20, waiting for transfers between devices, send(): return lax.ppermute(array, 'seq', pairs)  25.1 us
    pallas_call x15, Pallas kernels, call(): pl.pallas_call(kernel, out_shape=shapes, in_specs=[pl.BlockSpec(memory_sp...  15.5 us
    ppermute x4, starting transfers between devices, along_z(): return lax.ppermute(array, 'head', pairs)  10.5 us
    ppermute x4, waiting for transfers between devices, along_z(): return lax.ppermute(array, 'head', pairs)  2.14 us
  transfers between devices with their start and end apart: 24, of which 15 were waited for; matrix products, arithmetic and copies ran while one was open for 0% of the time, Pallas kernels for 11%

profile of v4, /device:TPU:1, one launch (start us, length us, event | category | flops | bytes accessed | tf_op | source)
XLA Modules:
  0.0 84.2 jit_solution(16691633938629054775)
XLA Ops:
  0.7 2.5 %shard_map.135 = (f32[2,136,128]{2,1,0:T(8,128)S(1)}, f32[2,136,128]{2,1,0:T(8,128)S(1)}, f32[4,256]{1,0:T(4,128)S(1)}) custom-call(f32[4,256]{1,0:T(4,128)} %decay_hbm.1, bf16[4,256,128]{2,1,0:T(8,128)(2,1)} %k_ref.5, bf16[4,256,128]{2,1,0:T(8,128)(2,1)} %v_ref.5), custom_call_target="tpu_custom_call" | custom-call | bytes 811008 | tf_op jit(solution)/shard_map/pallas_call | solution.py:505
  3.2 3.3 %collective-permute-start = (f32[2,136,128]{2,1,0:T(8,128)S(1)}, f32[2,136,128]{2,1,0:T(8,128)S(1)}, u32[]{:S(2)}, u32[]{:S(2)}) collective-permute-start(f32[2,136,128]{2,1,0:T(8,128)S(1)} %get-tuple-element.61), channel_id=1, source_target_pairs={{0,8},{8,0},{16,24},{24,16},{32,40},{40,32},{48,56},{56,48},{64,72... | collective-permute-start | bytes 417800 | tf_op jit(solution)/shard_map/ppermute | solution.py:68
  7.6 2.2 %collective-permute-start.2 = (f32[2,136,128]{2,1,0:T(8,128)S(1)}, f32[2,136,128]{2,1,0:T(8,128)S(1)}, u32[]{:S(2)}, u32[]{:S(2)}) collective-permute-start(f32[2,136,128]{2,1,0:T(8,128)S(1)} %shard_map.137.own_ref), channel_id=1, source_target_pairs={{0,32},{8,40},{16,48},{24,56},{32,0},{40,8},{48,16},{56,24},{64,96... | collective-permute-start | bytes 417800 | tf_op jit(solution)/shard_map/ppermute | solution.py:68
  9.8 1.1 %collective-permute-start.3 = (f32[2,136,128]{2,1,0:T(8,128)S(1)}, f32[2,136,128]{2,1,0:T(8,128)S(1)}, u32[]{:S(2)}, u32[]{:S(2)}) collective-permute-start(f32[2,136,128]{2,1,0:T(8,128)S(1)} %shard_map.137.own_ref), channel_id=1, source_target_pairs={{0,48},{8,56},{16,0},{24,8},{32,16},{40,24},{48,32},{56,40},{64,11... | collective-permute-start | bytes 417800 | tf_op jit(solution)/shard_map/ppermute | solution.py:68
  10.9 3.3 %collective-permute-done.1.one_ref = f32[2,136,128]{2,1,0:T(8,128)S(1)} collective-permute-done((f32[2,136,128]{2,1,0:T(8,128)S(1)}, f32[2,136,128]{2,1,0:T(8,128)S(1)}, u32[]{:S(2)}, u32[]{:S(2)}) %collective-permute-start.1) | collective-permute-done | bytes 139296 | tf_op jit(solution)/shard_map/ppermute | solution.py:68
  14.1 2.1 %collective-permute-done.2.two_ref = f32[2,136,128]{2,1,0:T(8,128)S(1)} collective-permute-done((f32[2,136,128]{2,1,0:T(8,128)S(1)}, f32[2,136,128]{2,1,0:T(8,128)S(1)}, u32[]{:S(2)}, u32[]{:S(2)}) %collective-permute-start.2) | collective-permute-done | bytes 139296 | tf_op jit(solution)/shard_map/ppermute | solution.py:68
  17.6 2.5 %collective-permute-start.7 = (f32[2,136,128]{2,1,0:T(8,128)S(1)}, f32[2,136,128]{2,1,0:T(8,128)S(1)}, u32[]{:S(2)}, u32[]{:S(2)}) collective-permute-start(f32[2,136,128]{2,1,0:T(8,128)S(1)} %get-tuple-element.68.own_ref), channel_id=1, source_target_pairs={{0,128},{8,136},{16,144},{24,152},{32,160},{40,168},{48,176},{56,1... | collective-permute-start | bytes 417800 | tf_op jit(solution)/shard_map/ppermute | solution.py:68
  20.0 1.1 %collective-permute-start.8 = (f32[2,136,128]{2,1,0:T(8,128)S(1)}, f32[2,136,128]{2,1,0:T(8,128)S(1)}, u32[]{:S(2)}, u32[]{:S(2)}) collective-permute-start(f32[2,136,128]{2,1,0:T(8,128)S(1)} %get-tuple-element.68.own_ref), channel_id=1, source_target_pairs={{0,192},{8,200},{16,208},{24,216},{32,224},{40,232},{48,240},{56,2... | collective-permute-start | bytes 417800 | tf_op jit(solution)/shard_map/ppermute | solution.py:68
  21.2 2.1 %collective-permute-start.4 = (f32[2,2,136,128]{3,2,1,0:T(8,128)S(1)}, f32[2,2,136,128]{3,2,1,0:T(8,128)S(1)}, u32[]{:S(2)}, u32[]{:S(2)}) collective-permute-start(f32[2,2,136,128]{3,2,1,0:T(8,128)S(1)} %get-tuple-element.62.own_ref), channel_id=1, source_target_pairs={{0,8},{8,0},{16,24},{24,16},{32,40},{40,32},{48,56},{56,48},{64,72... | collective-permute-start | bytes 835592 | tf_op jit(solution)/shard_map/ppermute | solution.py:68
  23.3 2.0 %collective-permute-done.7.two_ref = f32[2,136,128]{2,1,0:T(8,128)S(1)} collective-permute-done((f32[2,136,128]{2,1,0:T(8,128)S(1)}, f32[2,136,128]{2,1,0:T(8,128)S(1)}, u32[]{:S(2)}, u32[]{:S(2)}) %collective-permute-start.7) | collective-permute-done | bytes 139296 | tf_op jit(solution)/shard_map/ppermute | solution.py:68
  25.4 2.7 %collective-permute-start.9 = (f32[2,2,136,128]{3,2,1,0:T(8,128)S(1)}, f32[2,2,136,128]{3,2,1,0:T(8,128)S(1)}, u32[]{:S(2)}, u32[]{:S(2)}) collective-permute-start(f32[2,2,136,128]{3,2,1,0:T(8,128)S(1)} %get-tuple-element.70.own_ref), channel_id=1, source_target_pairs={{0,8},{8,0},{16,24},{24,16},{32,40},{40,32},{48,56},{56,48},{64,72... | collective-permute-start | bytes 835592 | tf_op jit(solution)/shard_map/ppermute | solution.py:68
  28.2 1.3 %collective-permute-start.5 = (f32[2,136,128]{2,1,0:T(8,128)S(1)}, f32[2,136,128]{2,1,0:T(8,128)S(1)}, u32[]{:S(2)}, u32[]{:S(2)}) collective-permute-start(f32[2,136,128]{2,1,0:T(8,128)S(1)} %get-tuple-element.60.keep_ref), channel_id=1, source_target_pairs={{0,8},{16,24},{32,40},{48,56},{64,72},{80,88},{96,104},{112,120},{... | collective-permute-start | bytes 417800 | tf_op jit(solution)/shard_map/ppermute | solution.py:68
  29.5 1.0 %shard_map.136 = (f32[4,256,128]{2,1,0:T(8,128)S(1)}, bf16[4,256,256]{2,1,0:T(8,128)(2,1)S(1)}, f32[4,256,256]{2,1,0:T(8,128)S(1)}, f32[4,256,256]{2,1,0:T(8,128)S(1)}, f32[256,128]{1,0:T(8,128)S(1)}) custom-call(bf16[4,256,128]{2,1,0:T(8,128)(2,1)S(1)} %copy-done.2, bf16[4,256,128]{2,1,0:T(8,128)(2,1)S(1)} %copy-done, bf16[4,256,128]{2,1,0:T(8,128)(2,1)S(1)} %copy-done.1, ...), custom_call_target="tpu_custom_call" | custom-call | flops 1000000000 | bytes 4153344 | tf_op jit(solution)/shard_map/pallas_call | solution.py:505
  31.4 1.3 %shard_map.139 = (f32[4,256,128]{2,1,0:T(8,128)S(1)}, f32[4,256,128]{2,1,0:T(8,128)S(1)}, f32[4,256,128]{2,1,0:T(8,128)S(1)}, bf16[4,128,384]{2,1,0:T(8,128)(2,1...) custom-call(bf16[4,256,128]{2,1,0:T(8,128)(2,1)S(1)} %copy-done.2, ...), custom_call_target="tpu_custom_call" | custom-call | flops 1000000000 | bytes 7276544 | tf_op jit(solution)/shard_map/pallas_call | solution.py:505
  32.8 1.1 %shard_map.141 = (f32[4,256,128]{2,1,0:T(8,128)S(1)}, f32[4,128]{1,0:T(4,128)S(1)}, bf16[4,128,256]{2,1,0:T(8,128)(2,1)S(1)}, bf16[4,128,256]{2,1,0:T(8,128)(2,1)S(1)}, f32[4,8,128]{2,1,0:T(8,128)S(1)}) custom-call(bf16[4,256,768]{2,1,0:T(8,128)(2,1)S(1)} %get-tuple-element.64.scaled_ref, f32[4,256,128]{2,1,0:T(8,128)S(1)} %get-tuple-element.65.near_ref, ...), custom_call_target="tpu_custom_call" | custom-call | bytes 4786176 | tf_op jit(solution)/shard_map/pallas_call | solution.py:505
  33.9 1.3 %collective-permute-start.10 = (f32[4,128]{1,0:T(4,128)S(1)}, f32[4,128]{1,0:T(4,128)S(1)}, u32[]{:S(2)}, u32[]{:S(2)}) collective-permute-start(f32[4,128]{1,0:T(4,128)S(1)} %get-tuple-element.74.a_ref), channel_id=1, source_target_pairs={{0,1},{1,0},{2,3},{3,2},{4,5},{5,4},{6,7},{7,6},{8,9},{9,8},{10,11... | collective-permute-start | bytes 6152 | tf_op jit(solution)/shard_map/ppermute | solution.py:56
  35.2 1.1 %collective-permute-done.10.b_ref = f32[4,128]{1,0:T(4,128)S(1)} collective-permute-done((f32[4,128]{1,0:T(4,128)S(1)}, f32[4,128]{1,0:T(4,128)S(1)}, u32[]{:S(2)}, u32[]{:S(2)}) %collective-permute-start.10) | collective-permute-done | bytes 2080 | tf_op jit(solution)/shard_map/ppermute | solution.py:56
  36.4 6.1 %collective-permute-start.11 = (f32[4,128]{1,0:T(4,128)S(1)}, f32[4,128]{1,0:T(4,128)S(1)}, u32[]{:S(2)}, u32[]{:S(2)}) collective-permute-start(f32[4,128]{1,0:T(4,128)S(1)} %shard_map.142.sums_ref), channel_id=1, source_target_pairs={{1,4},{4,1},{3,6},{6,3},{5,0},{0,5},{7,2},{2,7},{9,12},{12,9},{11,... | collective-permute-start | bytes 6152 | tf_op jit(solution)/shard_map/ppermute | solution.py:56
  42.7 2.8 %collective-permute-start.13 = (f32[4,128]{1,0:T(4,128)S(1)}, f32[4,128]{1,0:T(4,128)S(1)}, u32[]{:S(2)}, u32[]{:S(2)}) collective-permute-start(f32[4,128]{1,0:T(4,128)S(1)} %shard_map.142.sums_ref), channel_id=1, source_target_pairs={{1,2},{2,1},{3,4},{4,3},{5,6},{6,5},{7,0},{0,7},{9,10},{10,9},{11,... | collective-permute-start | bytes 6152 | tf_op jit(solution)/shard_map/ppermute | solution.py:56
  46.6 1.2 %shard_map.143 = (bf16[4,256,128]{2,1,0:T(8,128)(2,1)S(1)}, f32[2,256,128]{2,1,0:T(8,128)S(1)}, f32[2,2,136,128]{3,2,1,0:T(8,128)S(1)}, f32[2,2,136,128]{3,2,1,0:T(8,128)S(1)}) custom-call(bf16[4,2,128,512]{3,2,1,0:T(8,128)(2,1)S(1)} %get-tuple-element.63.turned_ref, f32[4,256,128]{2,1,0:T(8,128)S(1)} %get-tuple-element.72.mixed_ref, ...), custom_call_target="tpu_custom_call" | custom-call | bytes 3989504 | tf_op jit(solution)/shard_map/pallas_call | solution.py:505
  47.8 3.1 %collective-permute-start.14 = (f32[2,2,136,128]{3,2,1,0:T(8,128)S(1)}, f32[2,2,136,128]{3,2,1,0:T(8,128)S(1)}, u32[]{:S(2)}, u32[]{:S(2)}) collective-permute-start(f32[2,2,136,128]{3,2,1,0:T(8,128)S(1)} %get-tuple-element.87), channel_id=1, source_target_pairs={{0,8},{8,0},{16,24},{24,16},{32,40},{40,32},{48,56},{56,48},{64,72... | collective-permute-start | bytes 835592 | tf_op jit(solution)/shard_map/ppermute | solution.py:68
  50.9 2.7 %shard_map.144 = (bf16[4,256,128]{2,1,0:T(8,128)(2,1)}, bf16[4,256,128]{2,1,0:T(8,128)(2,1)}, f32[2,2,136,128]{3,2,1,0:T(8,128)S(1)}, f32[2,2,136,128]{3,2,1,0:T(8,128)S(1)}, f32[4,128,128]{2,1,0:T(8,128)S(1)}) custom-call(bf16[4,256,128]{2,1,0:T(8,128)(2,1)S(1)} %copy-done.2, bf16[4,256,128]{2,1,0:T(8,128)(2,1)S(1)} %get-tuple-element.75.g_ref, ...), custom_call_target="tpu_custom_call" | custom-call | flops 1000000000 | bytes 3328000 | tf_op jit(solution)/shard_map/pallas_call | solution.py:505
  53.7 2.4 %collective-permute-start.15 = (f32[2,136,128]{2,1,0:T(8,128)S(1)}, f32[2,136,128]{2,1,0:T(8,128)S(1)}, u32[]{:S(2)}, u32[]{:S(2)}) collective-permute-start(f32[2,136,128]{2,1,0:T(8,128)S(1)} %get-tuple-element.89), channel_id=1, source_target_pairs={{0,192},{8,200},{16,208},{24,216},{32,224},{40,232},{48,240},{56,2... | collective-permute-start | bytes 417800 | tf_op jit(solution)/shard_map/ppermute | solution.py:68
  57.0 2.3 %collective-permute-done.15.one_ref = f32[2,136,128]{2,1,0:T(8,128)S(1)} collective-permute-done((f32[2,136,128]{2,1,0:T(8,128)S(1)}, f32[2,136,128]{2,1,0:T(8,128)S(1)}, u32[]{:S(2)}, u32[]{:S(2)}) %collective-permute-start.15) | collective-permute-done | bytes 139296 | tf_op jit(solution)/shard_map/ppermute | solution.py:68
  59.3 2.7 %collective-permute-done.16.two_ref = f32[2,136,128]{2,1,0:T(8,128)S(1)} collective-permute-done((f32[2,136,128]{2,1,0:T(8,128)S(1)}, f32[2,136,128]{2,1,0:T(8,128)S(1)}, u32[]{:S(2)}, u32[]{:S(2)}) %collective-permute-start.16) | collective-permute-done | bytes 139296 | tf_op jit(solution)/shard_map/ppermute | solution.py:68
  62.1 4.1 %collective-permute-done.17.three_ref = f32[2,136,128]{2,1,0:T(8,128)S(1)} collective-permute-done((f32[2,136,128]{2,1,0:T(8,128)S(1)}, f32[2,136,128]{2,1,0:T(8,128)S(1)}, u32[]{:S(2)}, u32[]{:S(2)}) %collective-permute-start.17) | collective-permute-done | bytes 139296 | tf_op jit(solution)/shard_map/ppermute | solution.py:68
  66.3 2.1 %collective-permute-start.19 = (f32[2,136,128]{2,1,0:T(8,128)S(1)}, f32[2,136,128]{2,1,0:T(8,128)S(1)}, u32[]{:S(2)}, u32[]{:S(2)}) collective-permute-start(f32[2,136,128]{2,1,0:T(8,128)S(1)} %get-tuple-element.94), channel_id=1, source_target_pairs={{0,48},{8,56},{16,0},{24,8},{32,16},{40,24},{48,32},{56,40},{64,11... | collective-permute-start | bytes 417800 | tf_op jit(solution)/shard_map/ppermute | solution.py:68
  69.3 3.2 %collective-permute-start.23 = (f32[4,128,128]{2,1,0:T(8,128)S(1)}, f32[4,128,128]{2,1,0:T(8,128)S(1)}, u32[]{:S(2)}, u32[]{:S(2)}) collective-permute-start(f32[4,128,128]{2,1,0:T(8,128)S(1)} %get-tuple-element.98), channel_id=1, source_target_pairs={{8,0},{24,16},{40,32},{56,48},{72,64},{88,80},{104,96},{120,112},{... | collective-permute-start | bytes 786440 | tf_op jit(solution)/shard_map/ppermute | solution.py:68
  72.6 1.8 %collective-permute-done.20.two_ref = f32[2,136,128]{2,1,0:T(8,128)S(1)} collective-permute-done((f32[2,136,128]{2,1,0:T(8,128)S(1)}, f32[2,136,128]{2,1,0:T(8,128)S(1)}, u32[]{:S(2)}, u32[]{:S(2)}) %collective-permute-start.20) | collective-permute-done | bytes 139296 | tf_op jit(solution)/shard_map/ppermute | solution.py:68
  74.4 4.1 %collective-permute-done.21.three_ref = f32[2,136,128]{2,1,0:T(8,128)S(1)} collective-permute-done((f32[2,136,128]{2,1,0:T(8,128)S(1)}, f32[2,136,128]{2,1,0:T(8,128)S(1)}, u32[]{:S(2)}, u32[]{:S(2)}) %collective-permute-start.21) | collective-permute-done | bytes 139296 | tf_op jit(solution)/shard_map/ppermute | solution.py:68
  79.1 4.0 %shard_map.145 = (bf16[4,256,128]{2,1,0:T(8,128)(2,1)}, f32[4,256,128]{2,1,0:T(8,128)S(1)}, f32[4,256,128]{2,1,0:T(8,128)S(1)}, f32[21,4,256]{2,1,0:T(4,128)}) custom-call(bf16[4,256,128]{2,1,0:T(8,128)(2,1)S(1)} %copy-done.2, bf16[4,256,128]{2,1,0:T(8,128)(2,1)S(1)} %copy-done, bf16[4,256,128]{2,1,0:T(8,128)(2,1)S(1)} %copy-done.1, ...), custom_call_target="tpu_custom_call" | custom-call | flops 1000000000 | bytes 6512640 | tf_op jit(solution)/shard_map/pallas_call | solution.py:505
  83.1 1.1 %shard_map.149 = (bf16[4,256,128]{2,1,0:T(8,128)(2,1)}, bf16[4,256,128]{2,1,0:T(8,128)(2,1)}, f32[4,128]{1,0:T(4,128)}) custom-call(bf16[4,256,128]{2,1,0:T(8,128)(2,1)S(1)} %copy-done, bf16[4,256,128]{2,1,0:T(8,128)(2,1)S(1)} %copy-done.1, f32[256,128]{1,0:T(8,128)S(1)} %get-tuple-element.59.cols_ref, f32[2,128,128]{2,1,0:T(8,128)S(1)} %get-tuple-element.97.half_ref, ...), custom_call_target="tpu_custom_call" | custom-call | bytes 2895872 | tf_op jit(solution)/shard_map/pallas_call | solution.py:505
  (45 shorter events, 7.5 us)
Async XLA Ops:
  0.6 28.8 %copy-start = (bf16[4,256,128]{2,1,0:T(8,128)(2,1)S(1)}, bf16[4,256,128]{2,1,0:T(8,128)(2,1)}, u32[]{:S(2)}) copy-start(bf16[4,256,128]{2,1,0:T(8,128)(2,1)} %k_ref.5) | copy-start | bytes 786436
  0.6 28.8 %copy-start.1 = (bf16[4,256,128]{2,1,0:T(8,128)(2,1)S(1)}, bf16[4,256,128]{2,1,0:T(8,128)(2,1)}, u32[]{:S(2)}) copy-start(bf16[4,256,128]{2,1,0:T(8,128)(2,1)} %v_ref.5) | copy-start | bytes 786436
  0.7 28.8 %copy-start.2 = (bf16[4,256,128]{2,1,0:T(8,128)(2,1)S(1)}, bf16[4,256,128]{2,1,0:T(8,128)(2,1)}, u32[]{:S(2)}) copy-start(bf16[4,256,128]{2,1,0:T(8,128)(2,1)} %q_ref.7) | copy-start | bytes 786436
  0.7 28.8 %copy-start.5 = (f32[4,21,256]{2,0,1:T(4,128)S(1)}, f32[4,21,256]{2,0,1:T(4,128)}, u32[]{:S(2)}) copy-start(f32[4,21,256]{2,0,1:T(4,128)} %param.12) | copy-start | bytes 258052
  3.2 4.3 %collective-permute-start = (f32[2,136,128]{2,1,0:T(8,128)S(1)}, f32[2,136,128]{2,1,0:T(8,128)S(1)}, u32[]{:S(2)}, u32[]{:S(2)}) collective-permute-start(f32[2,136,128]{2,1,0:T(8,128)S(1)} %get-tuple-element.61), channel_id=1, source_target_pairs={{0,8},{8,0},{16,24},{24,16},{32,40},{40,32},{48,56},{56,48},{64,72... | collective-permute-start | bytes 417800 | tf_op jit(solution)/shard_map/ppermute | solution.py:68
  7.5 6.6 %collective-permute-start.1 = (f32[2,136,128]{2,1,0:T(8,128)S(1)}, f32[2,136,128]{2,1,0:T(8,128)S(1)}, u32[]{:S(2)}, u32[]{:S(2)}) collective-permute-start(f32[2,136,128]{2,1,0:T(8,128)S(1)} %shard_map.137.own_ref), channel_id=1, source_target_pairs={{0,16},{8,24},{16,32},{24,40},{32,48},{40,56},{48,0},{56,8},{64,80... | collective-permute-start | bytes 417800 | tf_op jit(solution)/shard_map/ppermute | solution.py:68
  7.6 8.6 %collective-permute-start.2 = (f32[2,136,128]{2,1,0:T(8,128)S(1)}, f32[2,136,128]{2,1,0:T(8,128)S(1)}, u32[]{:S(2)}, u32[]{:S(2)}) collective-permute-start(f32[2,136,128]{2,1,0:T(8,128)S(1)} %shard_map.137.own_ref), channel_id=1, source_target_pairs={{0,32},{8,40},{16,48},{24,56},{32,0},{40,8},{48,16},{56,24},{64,96... | collective-permute-start | bytes 417800 | tf_op jit(solution)/shard_map/ppermute | solution.py:68
  9.8 7.2 %collective-permute-start.3 = (f32[2,136,128]{2,1,0:T(8,128)S(1)}, f32[2,136,128]{2,1,0:T(8,128)S(1)}, u32[]{:S(2)}, u32[]{:S(2)}) collective-permute-start(f32[2,136,128]{2,1,0:T(8,128)S(1)} %shard_map.137.own_ref), channel_id=1, source_target_pairs={{0,48},{8,56},{16,0},{24,8},{32,16},{40,24},{48,32},{56,40},{64,11... | collective-permute-start | bytes 417800 | tf_op jit(solution)/shard_map/ppermute | solution.py:68
  17.1 6.2 %collective-permute-start.6 = (f32[2,136,128]{2,1,0:T(8,128)S(1)}, f32[2,136,128]{2,1,0:T(8,128)S(1)}, u32[]{:S(2)}, u32[]{:S(2)}) collective-permute-start(f32[2,136,128]{2,1,0:T(8,128)S(1)} %get-tuple-element.68.own_ref), channel_id=1, source_target_pairs={{0,64},{8,72},{16,80},{24,88},{32,96},{40,104},{48,112},{56,120},{... | collective-permute-start | bytes 417800 | tf_op jit(solution)/shard_map/ppermute | solution.py:68
  17.6 7.7 %collective-permute-start.7 = (f32[2,136,128]{2,1,0:T(8,128)S(1)}, f32[2,136,128]{2,1,0:T(8,128)S(1)}, u32[]{:S(2)}, u32[]{:S(2)}) collective-permute-start(f32[2,136,128]{2,1,0:T(8,128)S(1)} %get-tuple-element.68.own_ref), channel_id=1, source_target_pairs={{0,128},{8,136},{16,144},{24,152},{32,160},{40,168},{48,176},{56,1... | collective-permute-start | bytes 417800 | tf_op jit(solution)/shard_map/ppermute | solution.py:68
  20.0 5.3 %collective-permute-start.8 = (f32[2,136,128]{2,1,0:T(8,128)S(1)}, f32[2,136,128]{2,1,0:T(8,128)S(1)}, u32[]{:S(2)}, u32[]{:S(2)}) collective-permute-start(f32[2,136,128]{2,1,0:T(8,128)S(1)} %get-tuple-element.68.own_ref), channel_id=1, source_target_pairs={{0,192},{8,200},{16,208},{24,216},{32,224},{40,232},{48,240},{56,2... | collective-permute-start | bytes 417800 | tf_op jit(solution)/shard_map/ppermute | solution.py:68
  21.2 10.2 %collective-permute-start.4 = (f32[2,2,136,128]{3,2,1,0:T(8,128)S(1)}, f32[2,2,136,128]{3,2,1,0:T(8,128)S(1)}, u32[]{:S(2)}, u32[]{:S(2)}) collective-permute-start(f32[2,2,136,128]{3,2,1,0:T(8,128)S(1)} %get-tuple-element.62.own_ref), channel_id=1, source_target_pairs={{0,8},{8,0},{16,24},{24,16},{32,40},{40,32},{48,56},{56,48},{64,72... | collective-permute-start | bytes 835592 | tf_op jit(solution)/shard_map/ppermute | solution.py:68
  25.4 7.3 %collective-permute-start.9 = (f32[2,2,136,128]{3,2,1,0:T(8,128)S(1)}, f32[2,2,136,128]{3,2,1,0:T(8,128)S(1)}, u32[]{:S(2)}, u32[]{:S(2)}) collective-permute-start(f32[2,2,136,128]{3,2,1,0:T(8,128)S(1)} %get-tuple-element.70.own_ref), channel_id=1, source_target_pairs={{0,8},{8,0},{16,24},{24,16},{32,40},{40,32},{48,56},{56,48},{64,72... | collective-permute-start | bytes 835592 | tf_op jit(solution)/shard_map/ppermute | solution.py:68
  28.2 3.2 %collective-permute-start.5 = (f32[2,136,128]{2,1,0:T(8,128)S(1)}, f32[2,136,128]{2,1,0:T(8,128)S(1)}, u32[]{:S(2)}, u32[]{:S(2)}) collective-permute-start(f32[2,136,128]{2,1,0:T(8,128)S(1)} %get-tuple-element.60.keep_ref), channel_id=1, source_target_pairs={{0,8},{16,24},{32,40},{48,56},{64,72},{80,88},{96,104},{112,120},{... | collective-permute-start | bytes 417800 | tf_op jit(solution)/shard_map/ppermute | solution.py:68
  29.5 1.9 %copy-start.3 = (bf16[4,256,128]{2,1,0:T(8,128)(2,1)S(1)}, bf16[4,256,128]{2,1,0:T(8,128)(2,1)}, u32[]{:S(2)}) copy-start(bf16[4,256,128]{2,1,0:T(8,128)(2,1)} %grad_ref.5) | copy-start | bytes 786436
  29.5 1.9 %copy-start.4 = (bf16[4,256,128]{2,1,0:T(8,128)(2,1)S(1)}, bf16[4,256,128]{2,1,0:T(8,128)(2,1)}, u32[]{:S(2)}) copy-start(bf16[4,256,128]{2,1,0:T(8,128)(2,1)} %gate_ref.3) | copy-start | bytes 786436
  29.5 1.9 %copy-start.6 = (f32[4,128]{1,0:T(4,128)S(1)}, f32[4,128]{1,0:T(4,128)}, u32[]{:S(2)}) copy-start(f32[4,128]{1,0:T(4,128)} %gain_ref.3) | copy-start | bytes 6148
  33.9 2.4 %collective-permute-start.10 = (f32[4,128]{1,0:T(4,128)S(1)}, f32[4,128]{1,0:T(4,128)S(1)}, u32[]{:S(2)}, u32[]{:S(2)}) collective-permute-start(f32[4,128]{1,0:T(4,128)S(1)} %get-tuple-element.74.a_ref), channel_id=1, source_target_pairs={{0,1},{1,0},{2,3},{3,2},{4,5},{5,4},{6,7},{7,6},{8,9},{9,8},{10,11... | collective-permute-start | bytes 6152 | tf_op jit(solution)/shard_map/ppermute | solution.py:56
  36.4 9.2 %collective-permute-start.11 = (f32[4,128]{1,0:T(4,128)S(1)}, f32[4,128]{1,0:T(4,128)S(1)}, u32[]{:S(2)}, u32[]{:S(2)}) collective-permute-start(f32[4,128]{1,0:T(4,128)S(1)} %shard_map.142.sums_ref), channel_id=1, source_target_pairs={{1,4},{4,1},{3,6},{6,3},{5,0},{0,5},{7,2},{2,7},{9,12},{12,9},{11,... | collective-permute-start | bytes 6152 | tf_op jit(solution)/shard_map/ppermute | solution.py:56
  42.5 3.3 %collective-permute-start.12 = (f32[4,128]{1,0:T(4,128)S(1)}, f32[4,128]{1,0:T(4,128)S(1)}, u32[]{:S(2)}, u32[]{:S(2)}) collective-permute-start(f32[4,128]{1,0:T(4,128)S(1)} %shard_map.142.sums_ref), channel_id=1, source_target_pairs={{0,6},{1,3},{2,0},{3,5},{4,2},{5,7},{6,4},{7,1},{8,14},{9,11},{10,... | collective-permute-start | bytes 6152 | tf_op jit(solution)/shard_map/ppermute | solution.py:56
  42.7 3.8 %collective-permute-start.13 = (f32[4,128]{1,0:T(4,128)S(1)}, f32[4,128]{1,0:T(4,128)S(1)}, u32[]{:S(2)}, u32[]{:S(2)}) collective-permute-start(f32[4,128]{1,0:T(4,128)S(1)} %shard_map.142.sums_ref), channel_id=1, source_target_pairs={{1,2},{2,1},{3,4},{4,3},{5,6},{6,5},{7,0},{0,7},{9,10},{10,9},{11,... | collective-permute-start | bytes 6152 | tf_op jit(solution)/shard_map/ppermute | solution.py:56
  47.8 5.8 %collective-permute-start.14 = (f32[2,2,136,128]{3,2,1,0:T(8,128)S(1)}, f32[2,2,136,128]{3,2,1,0:T(8,128)S(1)}, u32[]{:S(2)}, u32[]{:S(2)}) collective-permute-start(f32[2,2,136,128]{3,2,1,0:T(8,128)S(1)} %get-tuple-element.87), channel_id=1, source_target_pairs={{0,8},{8,0},{16,24},{24,16},{32,40},{40,32},{48,56},{56,48},{64,72... | collective-permute-start | bytes 835592 | tf_op jit(solution)/shard_map/ppermute | solution.py:68
  53.6 3.4 %collective-permute-start.18 = (f32[2,2,136,128]{3,2,1,0:T(8,128)S(1)}, f32[2,2,136,128]{3,2,1,0:T(8,128)S(1)}, u32[]{:S(2)}, u32[]{:S(2)}) collective-permute-start(f32[2,2,136,128]{3,2,1,0:T(8,128)S(1)} %get-tuple-element.91), channel_id=1, source_target_pairs={{0,8},{8,0},{16,24},{24,16},{32,40},{40,32},{48,56},{56,48},{64,72... | collective-permute-start | bytes 835592 | tf_op jit(solution)/shard_map/ppermute | solution.py:68
  53.7 5.7 %collective-permute-start.15 = (f32[2,136,128]{2,1,0:T(8,128)S(1)}, f32[2,136,128]{2,1,0:T(8,128)S(1)}, u32[]{:S(2)}, u32[]{:S(2)}) collective-permute-start(f32[2,136,128]{2,1,0:T(8,128)S(1)} %get-tuple-element.89), channel_id=1, source_target_pairs={{0,192},{8,200},{16,208},{24,216},{32,224},{40,232},{48,240},{56,2... | collective-permute-start | bytes 417800 | tf_op jit(solution)/shard_map/ppermute | solution.py:68
  56.1 6.0 %collective-permute-start.16 = (f32[2,136,128]{2,1,0:T(8,128)S(1)}, f32[2,136,128]{2,1,0:T(8,128)S(1)}, u32[]{:S(2)}, u32[]{:S(2)}) collective-permute-start(f32[2,136,128]{2,1,0:T(8,128)S(1)} %get-tuple-element.88.own_ref), channel_id=1, source_target_pairs={{0,128},{8,136},{16,144},{24,152},{32,160},{40,168},{48,176},{56,1... | collective-permute-start | bytes 417800 | tf_op jit(solution)/shard_map/ppermute | solution.py:68
  56.6 9.6 %collective-permute-start.17 = (f32[2,136,128]{2,1,0:T(8,128)S(1)}, f32[2,136,128]{2,1,0:T(8,128)S(1)}, u32[]{:S(2)}, u32[]{:S(2)}) collective-permute-start(f32[2,136,128]{2,1,0:T(8,128)S(1)} %get-tuple-element.88.own_ref), channel_id=1, source_target_pairs={{0,64},{8,72},{16,80},{24,88},{32,96},{40,104},{48,112},{56,120},{... | collective-permute-start | bytes 417800 | tf_op jit(solution)/shard_map/ppermute | solution.py:68
  66.3 6.2 %collective-permute-start.19 = (f32[2,136,128]{2,1,0:T(8,128)S(1)}, f32[2,136,128]{2,1,0:T(8,128)S(1)}, u32[]{:S(2)}, u32[]{:S(2)}) collective-permute-start(f32[2,136,128]{2,1,0:T(8,128)S(1)} %get-tuple-element.94), channel_id=1, source_target_pairs={{0,48},{8,56},{16,0},{24,8},{32,16},{40,24},{48,32},{56,40},{64,11... | collective-permute-start | bytes 417800 | tf_op jit(solution)/shard_map/ppermute | solution.py:68
  68.4 6.0 %collective-permute-start.20 = (f32[2,136,128]{2,1,0:T(8,128)S(1)}, f32[2,136,128]{2,1,0:T(8,128)S(1)}, u32[]{:S(2)}, u32[]{:S(2)}) collective-permute-start(f32[2,136,128]{2,1,0:T(8,128)S(1)} %get-tuple-element.95), channel_id=1, source_target_pairs={{0,32},{8,40},{16,48},{24,56},{32,0},{40,8},{48,16},{56,24},{64,96... | collective-permute-start | bytes 417800 | tf_op jit(solution)/shard_map/ppermute | solution.py:68
  69.2 9.3 %collective-permute-start.21 = (f32[2,136,128]{2,1,0:T(8,128)S(1)}, f32[2,136,128]{2,1,0:T(8,128)S(1)}, u32[]{:S(2)}, u32[]{:S(2)}) collective-permute-start(f32[2,136,128]{2,1,0:T(8,128)S(1)} %get-tuple-element.96), channel_id=1, source_target_pairs={{0,16},{8,24},{16,32},{24,40},{32,48},{40,56},{48,0},{56,8},{64,80... | collective-permute-start | bytes 417800 | tf_op jit(solution)/shard_map/ppermute | solution.py:68
  69.3 13.8 %collective-permute-start.23 = (f32[4,128,128]{2,1,0:T(8,128)S(1)}, f32[4,128,128]{2,1,0:T(8,128)S(1)}, u32[]{:S(2)}, u32[]{:S(2)}) collective-permute-start(f32[4,128,128]{2,1,0:T(8,128)S(1)} %get-tuple-element.98), channel_id=1, source_target_pairs={{8,0},{24,16},{40,32},{56,48},{72,64},{88,80},{104,96},{120,112},{... | collective-permute-start | bytes 786440 | tf_op jit(solution)/shard_map/ppermute | solution.py:68
  78.5 4.6 %collective-permute-start.22 = (f32[2,128,128]{2,1,0:T(8,128)S(1)}, f32[2,128,128]{2,1,0:T(8,128)S(1)}, u32[]{:S(2)}, u32[]{:S(2)}) collective-permute-start(f32[2,128,128]{2,1,0:T(8,128)S(1)} %get-tuple-element.97.half_ref), channel_id=1, source_target_pairs={{0,8},{8,0},{16,24},{24,16},{32,40},{40,32},{48,56},{56,48},{64,72... | collective-permute-start | bytes 393224 | tf_op jit(solution)/shard_map/ppermute | solution.py:68
